TPU v7x, 32 devices: a whole 2x2x4 slice. The times are simulated.
32 devices in a mesh: fsdp: 8 (over z, y), rep: 4 (over x, core).
Axes of the slice: x: 2, y: 2, z: 4, core: 2. Of those that a mesh axis runs over, the one named last changes fastest.
Arguments:
- tokens: bfloat16 [4, 8192, 1024], P('rep', 'fsdp'), may hold values from -6 to 6
- segment_ids: int32 [4, 8192], P('rep', 'fsdp'), may hold values from 0 to 255, as said below
- cotangent: bfloat16 [4, 8192, 1024], P('rep', 'fsdp'), may hold values from -6 to 6
- w_query: float32 [1024, 1024], P(('fsdp', 'rep')), may hold values from -0.1875 to 0.1875
- b_query: float32 [1024], P(('fsdp', 'rep')), may hold values from -1.75 to 1.75
- w_key: float32 [1024, 1024], P(('fsdp', 'rep')), may hold values from -0.1875 to 0.1875
- w_value: float32 [1024, 1024], P(('fsdp', 'rep')), may hold values from -0.1875 to 0.1875
- b_value: float32 [1024], P(('fsdp', 'rep')), may hold values from -3 to 3
- w_out: float32 [1024, 1024], P(('fsdp', 'rep')), may hold values from -0.75 to 0.75
- b_out: float32 [1024], P(('fsdp', 'rep')), may hold values from -3 to 3
- gain_attn: float32 [1024], P(('fsdp', 'rep')), may hold values from 0.5 to 1.5
- shift_attn: float32 [1024], P(('fsdp', 'rep')), may hold values from -3 to 3
- w_up: float32 [1024, 4096], P(('fsdp', 'rep')), may hold values from -0.1875 to 0.1875
- b_up: float32 [4096], P(('fsdp', 'rep')), may hold values from -3 to 3
- w_down: float32 [4096, 1024], P(('fsdp', 'rep')), may hold values from -0.09375 to 0.09375
- b_down: float32 [1024], P(('fsdp', 'rep')), may hold values from -3 to 3
- gain_ffn: float32 [1024], P(('fsdp', 'rep')), may hold values from 0.5 to 1.5
- shift_ffn: float32 [1024], P(('fsdp', 'rep')), may hold values from -3 to 3
Outputs:
- encoder_output: bfloat16 [4, 8192, 1024], P('rep', 'fsdp')
- layer_input_gradient: bfloat16 [4, 8192, 1024], P('rep', 'fsdp')
- grad_w_query: float32 [1024, 1024], P(('fsdp', 'rep'))
- grad_b_query: float32 [1024], P(('fsdp', 'rep'))
- grad_w_key: float32 [1024, 1024], P(('fsdp', 'rep'))
- grad_w_value: float32 [1024, 1024], P(('fsdp', 'rep'))
- grad_b_value: float32 [1024], P(('fsdp', 'rep'))
- grad_w_out: float32 [1024, 1024], P(('fsdp', 'rep'))
- grad_b_out: float32 [1024], P(('fsdp', 'rep'))
- grad_gain_attn: float32 [1024], P(('fsdp', 'rep'))
- grad_shift_attn: float32 [1024], P(('fsdp', 'rep'))
- grad_w_up: float32 [1024, 4096], P(('fsdp', 'rep'))
- grad_b_up: float32 [4096], P(('fsdp', 'rep'))
- grad_w_down: float32 [4096, 1024], P(('fsdp', 'rep'))
- grad_b_down: float32 [1024], P(('fsdp', 'rep'))
- grad_gain_ffn: float32 [1024], P(('fsdp', 'rep'))
- grad_shift_ffn: float32 [1024], P(('fsdp', 'rep'))
Inputs may be any that keep to these rules, and one draw needn't show every extreme that they name: `segment_ids`: within each sequence of 1024 tokens the ids start at 0 and never fall; they stay below 256.
All inputs are finite; a program needn't handle non-finite values.
Results may differ from a plain program's by a relative error of at most 0.013.
The roundings to bfloat16 on the way count: a program that leaves them out, or rounds other values in their place, can miss the bound.
Values may be sent and summed in bfloat16 or wider, within the bound.
No kernel may reach another device: no remote copies, remote signals or barrier semaphores. Data moves between devices by JAX's collectives and lax.ppermute only.
A program may use at most 256 MiB of HBM per device.

v0:
```python
from functools import partial

import jax
import jax.numpy as jnp
from jax import lax
from jax.experimental import pallas as pl
from jax.experimental.pallas import tpu as pltpu
from jax.sharding import PartitionSpec as P


HEAD_DIM = 64
PAIR = 128
TILE = 256
CHUNKS = 4
SCALE = 0.125
EPS = 1e-05
NEG = -1e30
AXES = ("fsdp", "rep")
BF = jnp.bfloat16
F32 = jnp.float32


def matmul(left, right):
    return jnp.dot(left, right, preferred_element_type=F32)


def contract_rows(left, right):
    return lax.dot_general(left, right, (((0,), (0,)), ((), ())), preferred_element_type=F32)


def contract_cols(left, right):
    return lax.dot_general(left, right, (((1,), (1,)), ((), ())), preferred_element_type=F32)


def normalize(hidden, gain, shift):
    mean = jnp.mean(hidden, axis=-1, keepdims=True)
    centered = hidden - mean
    inverse = lax.rsqrt(jnp.mean(centered * centered, axis=-1, keepdims=True) + EPS)
    normed = centered * inverse
    return (normed * gain + shift, normed, inverse)


def normalize_back(grad, normed, inverse, gain):
    scaled = grad * gain
    inner = scaled - jnp.mean(scaled, axis=-1, keepdims=True)
    inner = inner - normed * jnp.mean(scaled * normed, axis=-1, keepdims=True)
    return (inverse * inner, jnp.sum(grad * normed, axis=0), jnp.sum(grad, axis=0))


def fill_bias(seg_col, seg_row, bias):
    @pl.when(pl.program_id(0) == 0)
    def _():
        bias[...] = jnp.where(seg_col[...] == seg_row[...], 0.0, NEG)


def head_lanes(head):
    lane = lax.broadcasted_iota(jnp.int32, (TILE, PAIR), 1)
    return lane < HEAD_DIM if head == 0 else lane >= HEAD_DIM


def forward_kernel(seg_col, seg_row, q_ref, k_ref, v_ref, o_ref, lse_ref, bias, out_t):
    fill_bias(seg_col, seg_row, bias)
    keys = k_ref[...]
    values_t = v_ref[...].T
    for tile in range(q_ref.shape[0] // TILE):
        at = slice(tile * TILE, (tile + 1) * TILE)
        query = q_ref[at, :] * jnp.asarray(SCALE, BF)
        for head in range(2):
            mine = jnp.where(head_lanes(head), query, jnp.zeros_like(query))
            scores = contract_cols(keys, mine) + bias[:, at]
            top = jnp.max(scores, axis=0, keepdims=True)
            weights = jnp.exp(scores - top)
            total = jnp.sum(weights, axis=0, keepdims=True)
            probs = (weights * (1.0 / total)).astype(BF)
            rows = slice(head * HEAD_DIM, (head + 1) * HEAD_DIM)
            out_t[rows, at] = matmul(values_t[rows, :], probs)
            lse_ref[0, head : head + 1, at] = top + jnp.log(total)
    o_ref[...] = out_t[...].T.astype(BF)


def backward_kernel(
    seg_col, seg_row, q_ref, k_ref, v_ref, do_ref, lse_ref,
    dq_ref, dk_ref, dv_ref, bq_ref, bv_ref, bias, dq_t, dk_sum, dv_sum,
):
    fill_bias(seg_col, seg_row, bias)
    keys = k_ref[...]
    values = v_ref[...]
    keys_t = keys.T
    for tile in range(q_ref.shape[0] // TILE):
        at = slice(tile * TILE, (tile + 1) * TILE)
        query = q_ref[at, :]
        grad = do_ref[at, :]
        for head in range(2):
            lanes = head_lanes(head)
            query_h = jnp.where(lanes, query, jnp.zeros_like(query))
            grad_h = jnp.where(lanes, grad, jnp.zeros_like(grad))
            scores = contract_cols(keys, query_h * jnp.asarray(SCALE, BF)) + bias[:, at]
            probs = jnp.exp(scores - lse_ref[0, head : head + 1, at])
            grad_probs = contract_cols(values, grad_h)
            inner = jnp.sum(grad_probs * probs, axis=0, keepdims=True)
            grad_scores = (probs * (grad_probs - inner)).astype(BF)
            rows = slice(head * HEAD_DIM, (head + 1) * HEAD_DIM)
            dq_t[rows, at] = matmul(keys_t[rows, :], grad_scores)
            dk_part = matmul(grad_scores, query_h)
            dv_part = matmul(probs.astype(BF), grad_h)
            if tile == 0 and head == 0:
                dk_sum[...] = dk_part
                dv_sum[...] = dv_part
            else:
                dk_sum[...] += dk_part
                dv_sum[...] += dv_part
    dq = (dq_t[...].T * SCALE).astype(BF)
    dv = dv_sum[...].astype(BF)
    dq_ref[...] = dq
    dk_ref[...] = (dk_sum[...] * SCALE).astype(BF)
    dv_ref[...] = dv
    bq_ref[...] = jnp.sum(dq.astype(F32), axis=0, keepdims=True)
    bv_ref[...] = jnp.sum(dv.astype(F32), axis=0, keepdims=True)


def columns(tokens, first):
    return pl.BlockSpec((tokens, PAIR), lambda i: (0, first + i))


def segment_specs(tokens):
    return [pl.BlockSpec((tokens, 1), lambda i: (0, 0)), pl.BlockSpec((1, tokens), lambda i: (0, 0))]


PARAMS = pltpu.CompilerParams(dimension_semantics=("arbitrary",), vmem_limit_bytes=56 * 2**20)


def attend(segments, packed):
    tokens = packed.shape[0]
    width = packed.shape[1] // 3
    pairs = width // PAIR
    return pl.pallas_call(
        forward_kernel,
        grid=(pairs,),
        name="attend",
        in_specs=segment_specs(tokens) + [columns(tokens, part * pairs) for part in range(3)],
        out_specs=[columns(tokens, 0), pl.BlockSpec((1, 2, tokens), lambda i: (i, 0, 0))],
        out_shape=[
            jax.ShapeDtypeStruct((tokens, width), BF),
            jax.ShapeDtypeStruct((pairs, 2, tokens), F32),
        ],
        scratch_shapes=[pltpu.VMEM((tokens, tokens), F32), pltpu.VMEM((PAIR, tokens), F32)],
        compiler_params=PARAMS,
    )(segments.reshape(tokens, 1), segments.reshape(1, tokens), packed, packed, packed)


def attend_back(segments, packed, grad, logsum, chunk):
    tokens = packed.shape[0]
    width = packed.shape[1] // 3
    pairs = width // PAIR
    count = pairs // CHUNKS
    first = chunk * count
    row = pl.BlockSpec((1, PAIR), lambda i: (0, i))
    return pl.pallas_call(
        backward_kernel,
        grid=(count,),
        name="attend_back",
        in_specs=segment_specs(tokens)
        + [columns(tokens, part * pairs + first) for part in range(3)]
        + [columns(tokens, first), pl.BlockSpec((1, 2, tokens), lambda i: (first + i, 0, 0))],
        out_specs=[columns(tokens, 0)] * 3 + [row] * 2,
        out_shape=[jax.ShapeDtypeStruct((tokens, count * PAIR), BF)] * 3
        + [jax.ShapeDtypeStruct((1, count * PAIR), F32)] * 2,
        scratch_shapes=[
            pltpu.VMEM((tokens, tokens), F32),
            pltpu.VMEM((PAIR, tokens), F32),
            pltpu.VMEM((tokens, PAIR), F32),
            pltpu.VMEM((tokens, PAIR), F32),
        ],
        compiler_params=PARAMS,
    )(segments.reshape(tokens, 1), segments.reshape(1, tokens), packed, packed, packed, grad, logsum)


def swap(value, bit, devices):
    return lax.ppermute(value, AXES, [(i, i ^ (1 << bit)) for i in range(devices)])


def bit_orders(bits):
    rest = list(range(1, bits))
    starts = (0, (bits - 1) // 4, (bits - 1) // 2)
    return [[0] + rest[s:] + rest[:s] for s in starts]


def spans(width, parts):
    step = width // PAIR // parts * PAIR
    edges = [step * p for p in range(parts)] + [width]
    return list(zip(edges[:-1], edges[1:]))


class Chain:
    def __init__(self, value, order, devices, kind=BF):
        self.devices, self.kind, self.order = devices, kind, list(order)
        self.left = list(range(devices.bit_length() - 1))
        self.halve(value.reshape((2,) * len(self.left) + (value.shape[0] // devices, value.shape[1])))
        self.got = None

    def halve(self, work):
        bit = self.order[0]
        axis = self.left.index(len(range(self.devices.bit_length() - 1)) - 1 - bit)
        own = (lax.axis_index(AXES) >> bit) & 1
        self.keep = lax.dynamic_index_in_dim(work, own, axis, keepdims=False)
        self.send = lax.dynamic_index_in_dim(work, 1 - own, axis, keepdims=False).astype(self.kind)
        self.left.pop(axis)

    def begin(self):
        self.got = swap(self.send, self.order.pop(0), self.devices)

    def finish(self):
        total = self.keep.astype(F32) + self.got.astype(F32)
        self.got = None
        if self.order:
            self.halve(total)
        else:
            self.keep, self.send = total, None

    @property
    def over(self):
        return self.send is None


def tick(chains, value):
    active = [c for c in chains if not c.over]
    for c in active:
        if c.got is not None:
            c.finish()
    held = lax.optimization_barrier((value, [(c.keep, c.send) for c in active]))
    for c, (keep, send) in zip(active, held[1]):
        c.keep, c.send = keep, send
        if not c.over:
            c.begin()
    return held[0]


def chains_of(value, devices, parts=3, turn=0, kind=BF):
    orders = bit_orders(devices.bit_length() - 1)
    return [
        Chain(value[:, a:b], orders[(p + turn) % 3], devices, kind)
        for p, (a, b) in enumerate(spans(value.shape[1], parts))
    ]


def result(chains):
    return jnp.concatenate([c.keep for c in chains], axis=1)


def gather_pairs(value, devices, later, parts=3):
    bits = devices.bit_length() - 1
    here = lax.axis_index(AXES)
    orders = [order[::-1] for order in bit_orders(bits)]
    work = [value[:, a:b] for a, b in spans(value.shape[1], parts)]
    held = [[] for _ in range(parts)]
    for step in range(bits):
        for p in range(parts):
            bit = orders[p][step]
            name = bits - 1 - bit
            axis = sum(1 for h in held[p] if h < name)
            own = (here >> bit) & 1
            mine, got = work[p], swap(work[p], bit, devices)
            work[p] = jnp.where(own == 0, jnp.stack([mine, got], axis), jnp.stack([got, mine], axis))
            held[p] = sorted(held[p] + [name])
        if step == bits - 3:
            work, later = lax.optimization_barrier((work, later))
    return [w.reshape(devices * value.shape[0], w.shape[-1]) for w in work], later


def widen(vector):
    return vector.astype(F32)


def local(
    tokens, segment_ids, cotangent, w_query, b_query, w_key, w_value, b_value, w_out, b_out,
    gain_attn, shift_attn, w_up, b_up, w_down, b_down, gain_ffn, shift_ffn, devices,
):
    blocks, length, width = tokens.shape
    rows = tokens.reshape(blocks * length, width)
    own = w_query.shape[0]
    ratio = b_up.shape[0] // own
    vectors = [b_query, b_value, b_out, gain_attn, shift_attn, b_down, gain_ffn, shift_ffn]
    names = len(vectors)
    side = jnp.stack(vectors, axis=1)
    side = jnp.concatenate([side, b_up.reshape(own, ratio)], axis=1)
    side = jnp.pad(side, ((0, 0), (0, PAIR - names - ratio)))
    head = jnp.concatenate([side, w_query, w_key, w_value], axis=1).astype(BF)
    later = (jnp.concatenate([w_out, w_up], axis=1).astype(BF), w_down.astype(BF))
    head, later = gather_pairs(head, devices, later)
    head = jnp.concatenate(head, axis=1)
    packed_full = head[:, PAIR:]
    query_bias, value_bias, out_bias, attn_gain, attn_shift, down_bias, ffn_gain, ffn_shift = [
        widen(head[:, i]) for i in range(names)
    ]
    up_bias = widen(head[:, names : names + ratio].reshape(-1))
    out_up = lax.all_gather(later[0], AXES, axis=0, tiled=True)
    down_full = lax.all_gather(later[1], AXES, axis=0, tiled=True)
    out_full, up_full = out_up[:, :width], out_up[:, width:]

    packed_bias = jnp.concatenate([query_bias, jnp.zeros_like(query_bias), value_bias])
    packed = (matmul(rows, packed_full) + packed_bias).astype(BF)
    segments = segment_ids.reshape(-1)
    context, logsums = attend(segments, packed)
    attended = matmul(context, out_full) + out_bias
    first, normed_one, inverse_one = normalize(rows.astype(F32) + attended, attn_gain, attn_shift)
    first_low = first.astype(BF)
    pre = matmul(first_low, up_full) + up_bias
    hidden = jax.nn.gelu(pre, approximate=False).astype(BF)
    branch = matmul(hidden, down_full) + down_bias
    output, normed_two, inverse_two = normalize(first + branch, ffn_gain, ffn_shift)
    encoder_output = output.astype(BF).reshape(tokens.shape)

    incoming = cotangent.reshape(blocks * length, width).astype(F32)
    grad_two, ffn_gain_grad, ffn_shift_grad = normalize_back(incoming, normed_two, inverse_two, ffn_gain)
    grad_branch = grad_two.astype(BF)
    down = chains_of(contract_rows(hidden, grad_branch).astype(BF), devices)
    down_bias_grad = jnp.sum(grad_branch.astype(F32), axis=0)
    running = list(down)
    grad_branch = tick(running, grad_branch)
    grad_hidden = contract_cols(grad_branch, down_full)
    _, gelu_pull = jax.vjp(partial(jax.nn.gelu, approximate=False), pre)
    grad_pre = gelu_pull(grad_hidden)[0].astype(BF)
    up_bias_grad = jnp.sum(grad_pre.astype(F32), axis=0)
    grad_pre = tick(running, grad_pre)
    up_product = contract_rows(first_low, grad_pre).astype(BF)
    up = chains_of(up_product, devices, turn=1)
    running += up
    grad_pre = tick(running, grad_pre)
    grad_first = grad_two + contract_cols(grad_pre, up_full)
    grad_one, attn_gain_grad, attn_shift_grad = normalize_back(grad_first, normed_one, inverse_one, attn_gain)
    grad_attended = grad_one.astype(BF)
    out_bias_grad = jnp.sum(grad_attended.astype(F32), axis=0)
    grad_attended = tick(running, grad_attended)
    out_product = contract_rows(context, grad_attended).astype(BF)
    out = chains_of(out_product, devices, parts=1, turn=2)
    grad_context = contract_cols(grad_attended, out_full).astype(BF)
    running += out

    pieces, shares = [], []
    for chunk in range(CHUNKS):
        grad_context = tick(running, grad_context)
        piece = attend_back(segments, packed, grad_context, logsums, chunk)
        if chunk + 1 < CHUNKS:
            grad_context, piece = lax.optimization_barrier((grad_context, piece))
        pieces.append(piece)
        grads = jnp.concatenate([contract_rows(rows, part).astype(BF) for part in piece[:3]], axis=1)
        shares.append(chains_of(grads, devices, parts=1, turn=chunk))
        running += shares[-1]
    joined = [jnp.concatenate([piece[part] for piece in pieces], axis=1) for part in range(5)]
    vector_grads = [
        joined[3][0], joined[4][0], out_bias_grad, attn_gain_grad, attn_shift_grad,
        down_bias_grad, ffn_gain_grad, ffn_shift_grad,
    ]
    side_grad = jnp.concatenate(
        [v.reshape(devices, own) for v in vector_grads] + [up_bias_grad.reshape(devices, own * ratio)],
        axis=1,
    )
    side = chains_of(side_grad, devices, parts=1, kind=F32)
    running += side
    total = tick(running, jnp.concatenate(joined[:3], axis=1))
    total_input = grad_one + contract_cols(total, packed_full)
    layer_input_gradient = total_input.astype(BF).reshape(tokens.shape)
    while not all(c.over for c in running):
        tick(running, ())

    down_grad, up_grad, out_grad = result(down), result(up), result(out)
    shares = [result(share) for share in shares]
    step = width // CHUNKS
    query_grad, key_grad, value_grad = [
        jnp.concatenate([share[:, part * step : (part + 1) * step] for share in shares], axis=1)
        for part in range(3)
    ]
    side_grad = result(side)[0]
    parts = [side_grad[i * own : (i + 1) * own] for i in range(names)]
    up_bias_share = side_grad[names * own :]
    return (
        encoder_output, layer_input_gradient, query_grad, parts[0], key_grad, value_grad, parts[1],
        out_grad, parts[2], parts[3], parts[4], up_grad, up_bias_share, down_grad, parts[5],
        parts[6], parts[7],
    )


def solution(mesh):
    devices = mesh.shape["fsdp"] * mesh.shape["rep"]
    act, ids = P("rep", "fsdp", None), P("rep", "fsdp")
    mat, vec = P(AXES, None), P(AXES)
    return jax.shard_map(
        partial(local, devices=devices),
        mesh=mesh,
        in_specs=(
            act, ids, act, mat, vec, mat, mat, vec, mat, vec, vec, vec, mat, vec, mat, vec, vec, vec,
        ),
        out_specs=(act, act, mat, vec, mat, mat, vec, mat, vec, vec, vec, mat, vec, mat, vec, vec, vec),
        check_vma=False,
    )
```

profile of v0, /device:TPU:0, one launch (start us, length us, event | category | flops | bytes accessed | tf_op | source)
XLA Modules:
  0.0 768.1 jit_solution(5551074854447009160)
XLA Ops:
  16.1 4.1 collective-permute-start
  42.0 7.2 collective-permute-done.5
  49.3 4.7 collective-permute-done.8
  75.8 7.9 %collective-permute-done.13 = bf16[2,2,2,32,1152]{4,3,1,2,0:T(8,128)(2,1)} collective-permute-done((bf16[2,2,2,32,1152]{4,3,1,2,0:T(8,128)(2,1)S(1)}, bf16[2,2,2,32,1152]{4,3,1,2,0:T(8,128)(2,1)}, u32[]{:S(2)}, u32[]{:S(2)}) %collective-permute-start.13) | collective-permute-done | bytes 589856 | tf_op jit(solution)/shard_map/ppermute | solution.py:179
  94.4 4.0 convert_reduce_fusion.5
  102.4 8.9 %fusion.10.q_ref.k_ref.v_ref = bf16[1024,3072]{1,0:T(8,128)(2,1)} fusion(f32[3072]{0:T(1024)S(1)} %pad_maximum_fusion.22, bf16[1024,1152]{1,0:T(8,128)(2,1)S(1)} %bitcast.545, bf16[1024,1024]{1,0:T(8,128)(2,1)S(1)} %bitcast.548, bf16[1024,1024]{1,0:T(8,128)(2,1)S(1)} %bitcast.524, bf16[1,1024,1024]{2,1,0:T(8,128)(2,1)S(1)} %copy-done), kind=kOutput, calls=%fused_computation.25 | convolution fusion | flops 6467616768 | bytes 14954496 | tf_op jit(solution)/shard_map/dot_general | solution.py:24
  111.3 59.7 %attend.1 = (bf16[1024,1024]{1,0:T(8,128)(2,1)}, f32[8,2,1024]{2,1,0:T(2,128)}) custom-call(s32[1024,1]{1,0:T(8,128)} %copy.146.seg_col, s32[1,1024]{1,0:T(1,128)} %seg_row.9, bf16[1024,3072]{1,0:T(8,128)(2,1)} %fusion.10.q_ref.k_ref.v_ref, bf16[1024,3072]{1,0:T(8,128)(2,1)} %fusion.10.q_ref.k_ref.v_ref, bf16[1024,3072]{1,0:T(8,128)(2,1)} %fusion.10.q_ref.k_ref.v_ref), custom_call_target="tpu_custom_call" | custom-call | tf_op jit(solution)/shard_map/attend/pallas_call | solution.py:136
  171.0 5.0 fusion.197
  181.7 46.6 %multiply_convert_fusion = (bf16[1024,4096]{1,0:T(8,128)(2,1)}, f32[1024,4096]{1,0:T(8,128)}, f32[1024,4096]{1,0:T(8,128)}) fusion(f32[4096]{0:T(1024)S(1)} %reshape.996, bf16[1024,5120]{1,0:T(8,128)(2,1)S(1)} %copy-done.102, bf16[1024,1024]{0,1:T(8,128)(2,1)S(1)} %fusion.187.clone.5), kind=kOutput, calls=%fused_computation.4 | convolution fusion | flops 8866758656 | bytes 52445184 | tf_op jit(solution)/shard_map/dot_general | solution.py:24
  228.3 14.9 %fusion.198 = (f32[1024]{0:T(1024)S(1)}, f32[1024,1024]{0,1:T(8,128)S(1)}) fusion(f32[1024]{0:T(1024)S(1)} %copy-done.95, bf16[1024,4096]{1,0:T(8,128)(2,1)} %get-tuple-element.461, bf16[4096,1024]{1,0:T(8,128)(2,1)} %all-gather.5.cloned.1.call-done, f32[1024]{0:T(1024)S(1)} %get-tuple-element.450, f32[1024]{0:T(1024)S(1)} %get-tuple-element.451, ...), kind=kOutput, calls=%fused_computation.458 | convolution fusion | flops 8597273600 | bytes 25190400 | tf_op jit(solution)/shard_map/dot_general | solution.py:24
  251.2 10.5 %convolution_convert_fusion.1 = bf16[4096,1024]{1,0:T(8,128)(2,1)S(1)} fusion(bf16[1024,4096]{1,0:T(8,128)(2,1)S(1)} %bitcast.585, bf16[1024,1024]{0,1:T(8,128)(2,1)S(1)} %get-tuple-element.209), kind=kOutput, calls=%fused_computation.20 | convolution fusion | flops 8594128896 | bytes 18874368 | tf_op jit(solution)/shard_map/dot_general | solution.py:28
  269.3 24.1 %convert_reduce_fusion = (f32[4096]{0:T(1024)}, bf16[1024,4096]{1,0:T(8,128)(2,1)}) fusion(f32[1024,4096]{1,0:T(8,128)} %get-tuple-element.462, f32[1024,4096]{1,0:T(8,128)} %get-tuple-element.528, f32[4096]{0:T(1024)S(1)} %reshape.996, bf16[1024,1024]{0,1:T(8,128)(2,1)S(1)} %get-tuple-element.209, bf16[4096,1024]{1,0:T(8,128)(2,1)} %all-gather.5.cloned.1.call-done), kind=kOutput, calls=%fused_computation.2 | convolution fusion | flops 8661233664 | bytes 52461568 | tf_op jit(solution)/shard_map/dot_general | solution.py:32
  310.4 11.7 %convolution_convert_fusion = bf16[1024,4096]{1,0:T(8,128)(2,1)S(1)} fusion(bf16[1024,4096]{1,0:T(8,128)(2,1)} %get-tuple-element.223, f32[1024,1024]{0,1:T(8,128)S(1)} %copy-done.3, f32[1024]{0:T(1024)S(1)} %get-tuple-element.450, f32[1024]{0:T(1024)S(1)} %get-tuple-element.451, f32[1024]{0:T(1024)S(1)} %add_rsqrt_fusion.1, ...), kind=kOutput, calls=%fused_computation.19 | convolution fusion | flops 8599371776 | bytes 20987904 | tf_op jit(solution)/shard_map/dot_general | solution.py:28
  343.4 17.5 %collective-permute-done.20 = bf16[2,2,2,128,512]{4,3,1,2,0:T(8,128)(2,1)S(1)} collective-permute-done((bf16[2,2,2,128,512]{4,3,1,2,0:T(8,128)(2,1)S(1)}, bf16[2,2,2,128,512]{4,3,1,2,0:T(8,128)(2,1)S(1)}, u32[]{:S(2)}, u32[]{:S(2)}) %collective-permute-start.20) | collective-permute-done | bytes 1048608 | tf_op jit(solution)/shard_map/ppermute | solution.py:179
  362.9 17.4 %multiply_reduce_fusion = (f32[1024]{0:T(1024)S(1)}, f32[1024]{0:T(1024)S(1)}, f32[1024]{0:T(1024)S(1)}, f32[1024]{0:T(1024)S(1)}, f32[1024,1024]{0,1:T(8,128)}) fusion(f32[1024,1024]{0,1:T(8,128)S(1)} %copy-done.3, f32[1024]{0:T(1024)S(1)} %add_rsqrt_fusion.1, f32[1024]{0:T(1024)S(1)} %broadcast_multiply_fusion.5, f32[1024]{0:T(1024)S(1)} %get-tuple-element.451, ...), kind=kOutput, calls=%fused_computation.41 | convolution fusion | flops 8608804864 | bytes 31506432 | tf_op jit(solution)/shard_map/dot_general | solution.py:32
  380.3 4.9 convert_reduce_fusion.3
  389.7 22.8 %collective-permute-done.23 = bf16[2,2,128,512]{3,2,0,1:T(8,128)(2,1)S(1)} collective-permute-done((bf16[2,2,128,512]{3,2,0,1:T(8,128)(2,1)S(1)}, bf16[2,2,128,512]{3,2,0,1:T(8,128)(2,1)S(1)}, u32[]{:S(2)}, u32[]{:S(2)}) %collective-permute-start.23) | collective-permute-done | bytes 524320 | tf_op jit(solution)/shard_map/ppermute | solution.py:179
  422.6 5.3 convolution_convert_fusion.3.do_ref
  436.2 15.0 %collective-permute-done.27 = bf16[2,128,256]{2,1,0:T(8,128)(2,1)S(1)} collective-permute-done((bf16[2,128,256]{2,1,0:T(8,128)(2,1)S(1)}, bf16[2,128,256]{2,1,0:T(8,128)(2,1)S(1)}, u32[]{:S(2)}, u32[]{:S(2)}) %collective-permute-start.27) | collective-permute-done | bytes 131104 | tf_op jit(solution)/shard_map/ppermute | solution.py:179
  459.9 19.5 %attend_back.4 = (bf16[1024,256]{1,0:T(8,128)(2,1)}, bf16[1024,256]{1,0:T(8,128)(2,1)}, bf16[1024,256]{1,0:T(8,128)(2,1)}, f32[1,256]{1,0:T(1,128)}, f32[1,256]{1,0:T(1,128)}) custom-call(s32[1024,1]{1,0:T(8,128)} %copy.146.seg_col, s32[1,1024]{1,0:T(1,128)} %seg_row.9, bf16[1024,3072]{1,0:T(8,128)(2,1)} %fusion.10.q_ref.k_ref.v_ref, ...), custom_call_target="tpu_custom_call" | custom-call | tf_op jit(solution)/shard_map/attend_back/pallas_call | solution.py:158
  503.3 8.1 %collective-permute-done.33 = bf16[128,256]{1,0:T(8,128)(2,1)S(1)} collective-permute-done((bf16[128,256]{1,0:T(8,128)(2,1)S(1)}, bf16[128,256]{1,0:T(8,128)(2,1)S(1)}, u32[]{:S(2)}, u32[]{:S(2)}) %collective-permute-start.33) | collective-permute-done | bytes 65568 | tf_op jit(solution)/shard_map/ppermute | solution.py:179
  511.9 4.4 collective-permute-done.35
  521.6 19.0 %attend_back.5 = (bf16[1024,256]{1,0:T(8,128)(2,1)}, bf16[1024,256]{1,0:T(8,128)(2,1)}, bf16[1024,256]{1,0:T(8,128)(2,1)}, f32[1,256]{1,0:T(1,128)}, f32[1,256]{1,0:T(1,128)}) custom-call(s32[1024,1]{1,0:T(8,128)} %copy.146.seg_col, s32[1,1024]{1,0:T(1,128)} %seg_row.9, bf16[1024,3072]{1,0:T(8,128)(2,1)} %fusion.10.q_ref.k_ref.v_ref, ...), custom_call_target="tpu_custom_call" | custom-call | tf_op jit(solution)/shard_map/attend_back/pallas_call | solution.py:158
  545.1 4.0 collective-permute-start.43
  562.6 6.3 collective-permute-done.40
  577.1 19.1 %attend_back.6 = (bf16[1024,256]{1,0:T(8,128)(2,1)}, bf16[1024,256]{1,0:T(8,128)(2,1)}, bf16[1024,256]{1,0:T(8,128)(2,1)}, f32[1,256]{1,0:T(1,128)}, f32[1,256]{1,0:T(1,128)}) custom-call(s32[1024,1]{1,0:T(8,128)} %copy.146.seg_col, s32[1,1024]{1,0:T(1,128)} %seg_row.9, bf16[1024,3072]{1,0:T(8,128)(2,1)} %fusion.10.q_ref.k_ref.v_ref, ...), custom_call_target="tpu_custom_call" | custom-call | tf_op jit(solution)/shard_map/attend_back/pallas_call | solution.py:158
  622.5 6.5 collective-permute-done.47
  634.1 19.3 %attend_back.7 = (bf16[1024,256]{1,0:T(8,128)(2,1)}, bf16[1024,256]{1,0:T(8,128)(2,1)}, bf16[1024,256]{1,0:T(8,128)(2,1)}, f32[1,256]{1,0:T(1,128)}, f32[1,256]{1,0:T(1,128)}) custom-call(s32[1024,1]{1,0:T(8,128)} %copy.146.seg_col, s32[1,1024]{1,0:T(1,128)} %seg_row.9, bf16[1024,3072]{1,0:T(8,128)(2,1)} %fusion.10.q_ref.k_ref.v_ref, ...), custom_call_target="tpu_custom_call" | custom-call | tf_op jit(solution)/shard_map/attend_back/pallas_call | solution.py:158
  688.1 10.7 %collective-permute-done.56 = bf16[2,32,768]{2,1,0:T(8,128)(2,1)S(1)} collective-permute-done((bf16[2,32,768]{2,1,0:T(8,128)(2,1)S(1)}, bf16[2,32,768]{2,1,0:T(8,128)(2,1)S(1)}, u32[]{:S(2)}, u32[]{:S(2)}) %collective-permute-start.56) | collective-permute-done | bytes 98336 | tf_op jit(solution)/shard_map/ppermute | solution.py:179
  703.8 11.5 %fusion.26 = bf16[1,1024,1024]{1,2,0:T(8,128)(2,1)} fusion(bf16[1024,3072]{1,0:T(8,128)(2,1)} %constant_dynamic-update-slice_fusion, bf16[1024,1152]{1,0:T(8,128)(2,1)S(1)} %bitcast.546, bf16[1024,1024]{1,0:T(8,128)(2,1)S(1)} %bitcast.549, bf16[1024,1024]{1,0:T(8,128)(2,1)S(1)} %bitcast.525, f32[1024]{0:T(1024)S(1)} %copy-done.91, ...), kind=kOutput, calls=%fused_computation.63 | convolution fusion | flops 6470762496 | bytes 23351296 | tf_op jit(solution)/shard_map/dot_general | solution.py:32
  715.3 4.0 copy.182
  724.7 13.2 %collective-permute-done.61 = bf16[32,768]{1,0:T(8,128)(2,1)S(1)} collective-permute-done((bf16[32,768]{1,0:T(8,128)(2,1)S(1)}, bf16[32,768]{1,0:T(8,128)(2,1)S(1)}, u32[]{:S(2)}, u32[]{:S(2)}) %collective-permute-start.61) | collective-permute-done | bytes 49184 | tf_op jit(solution)/shard_map/ppermute | solution.py:179
  (676 shorter events, 313.6 us)
Async XLA Ops:
  7.2 163.8 %all-gather.3.cloned.1.call-start = ((), (), s32[]{:S(2)}) async-start(), calls=%async_computation | async-start | bytes 10813440 | tf_op jit(solution)/shard_map/all_gather | solution.py:296
  54.1 174.2 %all-gather.5.cloned.1.call-start = ((), (), s32[]{:S(2)}) async-start(), calls=%async_computation.1 | async-start | bytes 8650752 | tf_op jit(solution)/shard_map/all_gather | solution.py:297
  268.2 37.4 %collective-permute-start.17 = (bf16[2,2,2,2,128,512]{5,4,2,3,0,1:T(8,128)(2,1)}, bf16[2,2,2,2,128,512]{5,4,2,3,0,1:T(8,128)(2,1)}, u32[]{:S(2)}, u32[]{:S(2)}) collective-permute-start(bf16[2,2,2,2,128,512]{5,4,2,3,0,1:T(8,128)(2,1)} %bitcast.504), channel_id=1, source_target_pairs={{0,1},{1,0},{2,3},{3,2},{4,5},{5,4},{6,7},{7,6},{8,9},{9,8},{10,11... | collective-permute-start | bytes 6291464 | tf_op jit(solution)/shard_map/ppermute | solution.py:179
  268.8 29.9 %collective-permute-start.16 = (bf16[2,2,2,2,128,256]{5,4,3,0,1,2:T(8,128)(2,1)}, bf16[2,2,2,2,128,256]{5,4,3,0,1,2:T(8,128)(2,1)}, u32[]{:S(2)}, u32[]{:S(2)}) collective-permute-start(bf16[2,2,2,2,128,256]{5,4,3,0,1,2:T(8,128)(2,1)} %bitcast.514), channel_id=1, source_target_pairs={{0,1},{1,0},{2,3},{3,2},{4,5},{5,4},{6,7},{7,6},{8,9},{9,8},{10,11... | collective-permute-start | bytes 3145736 | tf_op jit(solution)/shard_map/ppermute | solution.py:179
  268.8 32.3 %collective-permute-start.15 = (bf16[2,2,2,2,128,256]{5,4,0,1,2,3:T(8,128)(2,1)}, bf16[2,2,2,2,128,256]{5,4,0,1,2,3:T(8,128)(2,1)}, u32[]{:S(2)}, u32[]{:S(2)}) collective-permute-start(bf16[2,2,2,2,128,256]{5,4,0,1,2,3:T(8,128)(2,1)} %bitcast.516), channel_id=1, source_target_pairs={{0,1},{1,0},{2,3},{3,2},{4,5},{5,4},{6,7},{7,6},{8,9},{9,8},{10,11... | collective-permute-start | bytes 3145736 | tf_op jit(solution)/shard_map/ppermute | solution.py:179
  336.4 24.5 %collective-permute-start.20 = (bf16[2,2,2,128,512]{4,3,1,2,0:T(8,128)(2,1)S(1)}, bf16[2,2,2,128,512]{4,3,1,2,0:T(8,128)(2,1)S(1)}, u32[]{:S(2)}, u32[]{:S(2)}) collective-permute-start(bf16[2,2,2,128,512]{4,3,1,2,0:T(8,128)(2,1)S(1)} %copy-done.52), channel_id=1, source_target_pairs={{0,8},{1,9},{2,10},{3,11},{4,12},{5,13},{6,14},{7,15},{8,0},{9,1},... | collective-permute-start | bytes 3145736 | tf_op jit(solution)/shard_map/ppermute | solution.py:179
  361.4 55.2 %collective-permute-start.26 = (bf16[2,2,2,2,32,1536]{5,4,0,1,2,3:T(8,128)(2,1)}, bf16[2,2,2,2,32,1536]{5,4,0,1,2,3:T(8,128)(2,1)}, u32[]{:S(2)}, u32[]{:S(2)}) collective-permute-start(bf16[2,2,2,2,32,1536]{5,4,0,1,2,3:T(8,128)(2,1)} %bitcast.506), channel_id=1, source_target_pairs={{0,1},{1,0},{2,3},{3,2},{4,5},{5,4},{6,7},{7,6},{8,9},{9,8},{10,11... | collective-permute-start | bytes 4718600 | tf_op jit(solution)/shard_map/ppermute | solution.py:179
  361.4 51.3 %collective-permute-start.25 = (bf16[2,2,2,2,32,1280]{5,4,2,3,0,1:T(8,128)(2,1)}, bf16[2,2,2,2,32,1280]{5,4,2,3,0,1:T(8,128)(2,1)}, u32[]{:S(2)}, u32[]{:S(2)}) collective-permute-start(bf16[2,2,2,2,32,1280]{5,4,2,3,0,1:T(8,128)(2,1)} %bitcast.508), channel_id=1, source_target_pairs={{0,1},{1,0},{2,3},{3,2},{4,5},{5,4},{6,7},{7,6},{8,9},{9,8},{10,11... | collective-permute-start | bytes 3932168 | tf_op jit(solution)/shard_map/ppermute | solution.py:179
  361.9 52.7 %collective-permute-start.24 = (bf16[2,2,2,2,32,1280]{5,4,3,0,1,2:T(8,128)(2,1)}, bf16[2,2,2,2,32,1280]{5,4,3,0,1,2:T(8,128)(2,1)}, u32[]{:S(2)}, u32[]{:S(2)}) collective-permute-start(bf16[2,2,2,2,32,1280]{5,4,3,0,1,2:T(8,128)(2,1)} %bitcast.510), channel_id=1, source_target_pairs={{0,1},{1,0},{2,3},{3,2},{4,5},{5,4},{6,7},{7,6},{8,9},{9,8},{10,11... | collective-permute-start | bytes 3932168 | tf_op jit(solution)/shard_map/ppermute | solution.py:179
  362.0 24.7 %collective-permute-start.22 = (bf16[2,2,128,256]{3,2,1,0:T(8,128)(2,1)}, bf16[2,2,128,256]{3,2,1,0:T(8,128)(2,1)}, u32[]{:S(2)}, u32[]{:S(2)}) collective-permute-start(bf16[2,2,128,256]{3,2,1,0:T(8,128)(2,1)} %fusion.143), channel_id=1, source_target_pairs={{0,8},{1,9},{2,10},{3,11},{4,12},{5,13},{6,14},{7,15},{8,0},{9,1},... | collective-permute-start | bytes 786440 | tf_op jit(solution)/shard_map/ppermute | solution.py:179
  362.3 27.2 %collective-permute-start.21 = (bf16[2,2,128,256]{3,2,0,1:T(8,128)(2,1)}, bf16[2,2,128,256]{3,2,0,1:T(8,128)(2,1)S(1)}, u32[]{:S(2)}, u32[]{:S(2)}) collective-permute-start(bf16[2,2,128,256]{3,2,0,1:T(8,128)(2,1)} %fusion.142), channel_id=1, source_target_pairs={{0,4},{1,5},{2,6},{3,7},{4,0},{5,1},{6,2},{7,3},{8,12},{9,13},{10,... | collective-permute-start | bytes 786440 | tf_op jit(solution)/shard_map/ppermute | solution.py:179
  386.7 25.8 %collective-permute-start.23 = (bf16[2,2,128,512]{3,2,0,1:T(8,128)(2,1)S(1)}, bf16[2,2,128,512]{3,2,0,1:T(8,128)(2,1)S(1)}, u32[]{:S(2)}, u32[]{:S(2)}) collective-permute-start(bf16[2,2,128,512]{3,2,0,1:T(8,128)(2,1)S(1)} %fusion.132), channel_id=1, source_target_pairs={{0,16},{1,17},{2,18},{3,19},{4,20},{5,21},{6,22},{7,23},{8,24},{9,... | collective-permute-start | bytes 1572872 | tf_op jit(solution)/shard_map/ppermute | solution.py:179
  429.3 28.5 %collective-permute-start.32 = (bf16[2,2,2,32,1536]{4,3,0,1,2:T(8,128)(2,1)S(1)}, bf16[2,2,2,32,1536]{4,3,0,1,2:T(8,128)(2,1)S(1)}, u32[]{:S(2)}, u32[]{:S(2)}) collective-permute-start(bf16[2,2,2,32,1536]{4,3,0,1,2:T(8,128)(2,1)S(1)} %fusion.127), channel_id=1, source_target_pairs={{0,2},{1,3},{2,0},{3,1},{4,6},{5,7},{6,4},{7,5},{8,10},{9,11},{10,... | collective-permute-start | bytes 2359304 | tf_op jit(solution)/shard_map/ppermute | solution.py:179
  430.8 23.4 %collective-permute-start.31 = (bf16[2,2,2,32,1280]{4,3,1,2,0:T(8,128)(2,1)S(1)}, bf16[2,2,2,32,1280]{4,3,1,2,0:T(8,128)(2,1)S(1)}, u32[]{:S(2)}, u32[]{:S(2)}) collective-permute-start(bf16[2,2,2,32,1280]{4,3,1,2,0:T(8,128)(2,1)S(1)} %fusion.129), channel_id=1, source_target_pairs={{0,8},{1,9},{2,10},{3,11},{4,12},{5,13},{6,14},{7,15},{8,0},{9,1},... | collective-permute-start | bytes 1966088 | tf_op jit(solution)/shard_map/ppermute | solution.py:179
  434.1 20.3 %collective-permute-start.30 = (bf16[2,2,2,32,1280]{4,3,2,0,1:T(8,128)(2,1)S(1)}, bf16[2,2,2,32,1280]{4,3,2,0,1:T(8,128)(2,1)S(1)}, u32[]{:S(2)}, u32[]{:S(2)}) collective-permute-start(bf16[2,2,2,32,1280]{4,3,2,0,1:T(8,128)(2,1)S(1)} %fusion.128), channel_id=1, source_target_pairs={{0,4},{1,5},{2,6},{3,7},{4,0},{5,1},{6,2},{7,3},{8,12},{9,13},{10,... | collective-permute-start | bytes 1966088 | tf_op jit(solution)/shard_map/ppermute | solution.py:179
  434.7 18.8 %collective-permute-start.29 = (bf16[2,128,512]{2,1,0:T(8,128)(2,1)S(1)}, bf16[2,128,512]{2,1,0:T(8,128)(2,1)S(1)}, u32[]{:S(2)}, u32[]{:S(2)}) collective-permute-start(bf16[2,128,512]{2,1,0:T(8,128)(2,1)S(1)} %fusion.144), channel_id=1, source_target_pairs={{0,2},{1,3},{2,0},{3,1},{4,6},{5,7},{6,4},{7,5},{8,10},{9,11},{10,... | collective-permute-start | bytes 786440 | tf_op jit(solution)/shard_map/ppermute | solution.py:179
  490.4 29.8 %collective-permute-start.39 = (bf16[2,2,2,2,32,1024]{5,4,2,3,0,1:T(8,128)(2,1)}, bf16[2,2,2,2,32,1024]{5,4,2,3,0,1:T(8,128)(2,1)S(1)}, u32[]{:S(2)}, u32[]{:S(2)}) collective-permute-start(bf16[2,2,2,2,32,1024]{5,4,2,3,0,1:T(8,128)(2,1)} %bitcast.555), channel_id=1, source_target_pairs={{0,1},{1,0},{2,3},{3,2},{4,5},{5,4},{6,7},{7,6},{8,9},{9,8},{10,11... | collective-permute-start | bytes 3145736 | tf_op jit(solution)/shard_map/ppermute | solution.py:179
  490.4 29.0 %collective-permute-start.38 = (bf16[2,2,32,1536]{3,2,0,1:T(8,128)(2,1)}, bf16[2,2,32,1536]{3,2,0,1:T(8,128)(2,1)S(1)}, u32[]{:S(2)}, u32[]{:S(2)}) collective-permute-start(bf16[2,2,32,1536]{3,2,0,1:T(8,128)(2,1)} %fusion.135), channel_id=1, source_target_pairs={{0,4},{1,5},{2,6},{3,7},{4,0},{5,1},{6,2},{7,3},{8,12},{9,13},{10,... | collective-permute-start | bytes 1179656 | tf_op jit(solution)/shard_map/ppermute | solution.py:179
  491.9 24.4 %collective-permute-start.37 = (bf16[2,2,32,1280]{3,2,0,1:T(8,128)(2,1)}, bf16[2,2,32,1280]{3,2,0,1:T(8,128)(2,1)S(1)}, u32[]{:S(2)}, u32[]{:S(2)}) collective-permute-start(bf16[2,2,32,1280]{3,2,0,1:T(8,128)(2,1)} %fusion.141), channel_id=1, source_target_pairs={{0,16},{1,17},{2,18},{3,19},{4,20},{5,21},{6,22},{7,23},{8,24},{9,... | collective-permute-start | bytes 983048 | tf_op jit(solution)/shard_map/ppermute | solution.py:179
  494.6 22.7 %collective-permute-start.36 = (bf16[2,2,32,1280]{3,2,1,0:T(8,128)(2,1)}, bf16[2,2,32,1280]{3,2,1,0:T(8,128)(2,1)S(1)}, u32[]{:S(2)}, u32[]{:S(2)}) collective-permute-start(bf16[2,2,32,1280]{3,2,1,0:T(8,128)(2,1)} %fusion.140), channel_id=1, source_target_pairs={{0,8},{1,9},{2,10},{3,11},{4,12},{5,13},{6,14},{7,15},{8,0},{9,1},... | collective-permute-start | bytes 983048 | tf_op jit(solution)/shard_map/ppermute | solution.py:179
  545.0 29.9 %collective-permute-start.44 = (bf16[2,2,2,2,32,768]{5,4,3,2,1,0:T(8,128)(2,1)}, bf16[2,2,2,2,32,768]{5,4,3,2,1,0:T(8,128)(2,1)}, u32[]{:S(2)}, u32[]{:S(2)}) collective-permute-start(bf16[2,2,2,2,32,768]{5,4,3,2,1,0:T(8,128)(2,1)} %get-tuple-element.291), channel_id=1, source_target_pairs={{0,1},{1,0},{2,3},{3,2},{4,5},{5,4},{6,7},{7,6},{8,9},{9,8},{10,11... | collective-permute-start | bytes 2359304 | tf_op jit(solution)/shard_map/ppermute | solution.py:179
  545.1 27.8 %collective-permute-start.43 = (bf16[2,2,2,32,1024]{4,3,1,2,0:T(8,128)(2,1)}, bf16[2,2,2,32,1024]{4,3,1,2,0:T(8,128)(2,1)}, u32[]{:S(2)}, u32[]{:S(2)}) collective-permute-start(bf16[2,2,2,32,1024]{4,3,1,2,0:T(8,128)(2,1)} %fusion.133), channel_id=1, source_target_pairs={{0,8},{1,9},{2,10},{3,11},{4,12},{5,13},{6,14},{7,15},{8,0},{9,1},... | collective-permute-start | bytes 1572872 | tf_op jit(solution)/shard_map/ppermute | solution.py:179
  549.1 22.1 %collective-permute-start.42 = (bf16[2,32,1536]{2,1,0:T(8,128)(2,1)}, bf16[2,32,1536]{2,1,0:T(8,128)(2,1)}, u32[]{:S(2)}, u32[]{:S(2)}) collective-permute-start(bf16[2,32,1536]{2,1,0:T(8,128)(2,1)} %fusion.146), channel_id=1, source_target_pairs={{0,8},{1,9},{2,10},{3,11},{4,12},{5,13},{6,14},{7,15},{8,0},{9,1},... | collective-permute-start | bytes 589832 | tf_op jit(solution)/shard_map/ppermute | solution.py:179
  549.7 19.2 %collective-permute-start.40 = (bf16[2,32,1280]{2,1,0:T(8,128)(2,1)}, bf16[2,32,1280]{2,1,0:T(8,128)(2,1)}, u32[]{:S(2)}, u32[]{:S(2)}) collective-permute-start(bf16[2,32,1280]{2,1,0:T(8,128)(2,1)} %fusion.151), channel_id=1, source_target_pairs={{0,16},{1,17},{2,18},{3,19},{4,20},{5,21},{6,22},{7,23},{8,24},{9,... | collective-permute-start | bytes 491528 | tf_op jit(solution)/shard_map/ppermute | solution.py:179
  608.5 23.5 %collective-permute-start.50 = (bf16[2,2,2,2,32,768]{5,4,3,0,1,2:T(8,128)(2,1)S(1)}, bf16[2,2,2,2,32,768]{5,4,3,0,1,2:T(8,128)(2,1)S(1)}, u32[]{:S(2)}, u32[]{:S(2)}) collective-permute-start(bf16[2,2,2,2,32,768]{5,4,3,0,1,2:T(8,128)(2,1)S(1)} %copy.170), channel_id=1, source_target_pairs={{0,1},{1,0},{2,3},{3,2},{4,5},{5,4},{6,7},{7,6},{8,9},{9,8},{10,11... | collective-permute-start | bytes 2359304 | tf_op jit(solution)/shard_map/ppermute | solution.py:179
  608.5 22.6 %collective-permute-start.49 = (bf16[2,2,2,32,768]{4,3,2,1,0:T(8,128)(2,1)S(1)}, bf16[2,2,2,32,768]{4,3,2,1,0:T(8,128)(2,1)S(1)}, u32[]{:S(2)}, u32[]{:S(2)}) collective-permute-start(bf16[2,2,2,32,768]{4,3,2,1,0:T(8,128)(2,1)S(1)} %copy-done.63), channel_id=1, source_target_pairs={{0,2},{1,3},{2,0},{3,1},{4,6},{5,7},{6,4},{7,5},{8,10},{9,11},{10,... | collective-permute-start | bytes 1179656 | tf_op jit(solution)/shard_map/ppermute | solution.py:179
  609.1 20.5 %collective-permute-start.48 = (bf16[2,2,32,1024]{3,2,0,1:T(8,128)(2,1)S(1)}, bf16[2,2,32,1024]{3,2,0,1:T(8,128)(2,1)S(1)}, u32[]{:S(2)}, u32[]{:S(2)}) collective-permute-start(bf16[2,2,32,1024]{3,2,0,1:T(8,128)(2,1)S(1)} %copy-done.65), channel_id=1, source_target_pairs={{0,16},{1,17},{2,18},{3,19},{4,20},{5,21},{6,22},{7,23},{8,24},{9,... | collective-permute-start | bytes 786440 | tf_op jit(solution)/shard_map/ppermute | solution.py:179
  680.9 20.3 %collective-permute-start.59 = (bf16[2,2,2,2,32,768]{5,4,0,1,2,3:T(8,128)(2,1)S(1)}, bf16[2,2,2,2,32,768]{5,4,0,1,2,3:T(8,128)(2,1)S(1)}, u32[]{:S(2)}, u32[]{:S(2)}) collective-permute-start(bf16[2,2,2,2,32,768]{5,4,0,1,2,3:T(8,128)(2,1)S(1)} %copy.180), channel_id=1, source_target_pairs={{0,1},{1,0},{2,3},{3,2},{4,5},{5,4},{6,7},{7,6},{8,9},{9,8},{10,11... | collective-permute-start | bytes 2359304 | tf_op jit(solution)/shard_map/ppermute | solution.py:179
  681.1 19.2 %collective-permute-start.58 = (bf16[2,2,2,32,768]{4,3,1,2,0:T(8,128)(2,1)S(1)}, bf16[2,2,2,32,768]{4,3,1,2,0:T(8,128)(2,1)S(1)}, u32[]{:S(2)}, u32[]{:S(2)}) collective-permute-start(bf16[2,2,2,32,768]{4,3,1,2,0:T(8,128)(2,1)S(1)} %fusion.138), channel_id=1, source_target_pairs={{0,8},{1,9},{2,10},{3,11},{4,12},{5,13},{6,14},{7,15},{8,0},{9,1},... | collective-permute-start | bytes 1179656 | tf_op jit(solution)/shard_map/ppermute | solution.py:179
  681.1 18.4 %collective-permute-start.57 = (bf16[2,2,32,768]{3,2,1,0:T(8,128)(2,1)S(1)}, bf16[2,2,32,768]{3,2,1,0:T(8,128)(2,1)S(1)}, u32[]{:S(2)}, u32[]{:S(2)}) collective-permute-start(bf16[2,2,32,768]{3,2,1,0:T(8,128)(2,1)S(1)} %fusion.148), channel_id=1, source_target_pairs={{0,8},{1,9},{2,10},{3,11},{4,12},{5,13},{6,14},{7,15},{8,0},{9,1},... | collective-permute-start | bytes 589832 | tf_op jit(solution)/shard_map/ppermute | solution.py:179
  702.2 21.7 %collective-permute-start.65 = (f32[2,2,2,1,384]{4,3,2,1,0:T(1,128)S(1)}, f32[2,2,2,1,384]{4,3,2,1,0:T(1,128)}, u32[]{:S(2)}, u32[]{:S(2)}) collective-permute-start(f32[2,2,2,1,384]{4,3,2,1,0:T(1,128)S(1)} %get-tuple-element.358), channel_id=1, source_target_pairs={{0,2},{1,3},{2,0},{3,1},{4,6},{5,7},{6,4},{7,5},{8,10},{9,11},{10,... | collective-permute-start | bytes 36872 | tf_op jit(solution)/shard_map/ppermute | solution.py:179
  719.3 18.9 %collective-permute-start.64 = (bf16[2,2,2,32,768]{4,3,0,1,2:T(8,128)(2,1)S(1)}, bf16[2,2,2,32,768]{4,3,0,1,2:T(8,128)(2,1)S(1)}, u32[]{:S(2)}, u32[]{:S(2)}) collective-permute-start(bf16[2,2,2,32,768]{4,3,0,1,2:T(8,128)(2,1)S(1)} %copy-done.64), channel_id=1, source_target_pairs={{0,2},{1,3},{2,0},{3,1},{4,6},{5,7},{6,4},{7,5},{8,10},{9,11},{10,... | collective-permute-start | bytes 1179656 | tf_op jit(solution)/shard_map/ppermute | solution.py:179
  (152 other events, 2308.1 us)
Sparse Core Ops, SparseCore 0:
  54.2 86.4 all-gather.2
  143.6 75.3 all-gather.4
where the time goes:
time: 778 us; the launch traced here: 768 us
  matrix products  175 us (22%)
  waiting for transfers between devices  162 us (21%)
  Pallas kernels  137 us (18%)
  local copies, waits for them, and re-layouts  124 us (16%)
  other arithmetic  79.6 us (10%)
  starting transfers between devices  74.2 us (10%)
  between operations  16.8 us (2%)
    ppermute x75, waiting for transfers between devices, swap(): lax.ppermute(value, AXES, [(i, i ^ 1 << bit) for i in range(devices)])  162 us
    pallas_call x4, Pallas kernels, attend_back(): pl.pallas_call(backward_kernel, grid=(count,), name='attend_back', in_spe...  77 us
    dot_general x4, matrix products, matmul(): return jnp.dot(left, right, preferred_element_type=F32)  75.4 us
    ppermute x75, starting transfers between devices, swap(): lax.ppermute(value, AXES, [(i, i ^ 1 << bit) for i in range(devices)])  74.1 us
    pallas_call x1, Pallas kernels, attend(): pl.pallas_call(forward_kernel, grid=(pairs,), name='attend', in_specs=seg...  59.7 us
    dot_general x4, matrix products, contract_cols(): lax.dot_general(left, right, (((1,), (1,)), ((), ())), preferred_element_...  58.2 us
    dot_general x15, matrix products, contract_rows(): lax.dot_general(left, right, (((0,), (0,)), ((), ())), preferred_element_...  41.7 us
    unnamed x227, local copies, waits for them, and re-layouts  41.6 us
  transfers between devices with their start and end apart: 77, of which 29 were waited for; matrix products, arithmetic and copies ran while one was open for 32% of the time, Pallas kernels for 8%

commit v1 on v0

--- a/solution.py
+++ b/solution.py
@@ -15,6 +15,7 @@
 SCALE = 0.125
 EPS = 1e-05
 NEG = -1e30
+BELL = (2.0 * 3.141592653589793) ** -0.5
 AXES = ("fsdp", "rep")
 BF = jnp.bfloat16
 F32 = jnp.float32
@@ -175,6 +176,114 @@
     )(segments.reshape(tokens, 1), segments.reshape(1, tokens), packed, packed, packed, grad, logsum)
 
 
+WIDE = 512
+
+
+def up_kernel(x_ref, w_ref, b_ref, hidden_ref, slope_ref):
+    weight = w_ref[...]
+    bias = b_ref[...]
+    for tile in range(x_ref.shape[0] // TILE):
+        at = slice(tile * TILE, (tile + 1) * TILE)
+        pre = matmul(x_ref[at, :], weight) + bias
+        area = 0.5 * lax.erf(pre * (0.5 ** 0.5)) + 0.5
+        hidden_ref[at, :] = (pre * area).astype(BF)
+        bell = jnp.exp(pre * pre * -0.5) * BELL
+        slope_ref[at, :] = (area + pre * bell).astype(BF)
+
+
+def up_back_kernel(dz_ref, w_ref, slope_ref, du_ref, sum_ref):
+    weight = w_ref[...]
+    total = jnp.zeros(sum_ref.shape, F32)
+    for tile in range(dz_ref.shape[0] // TILE):
+        at = slice(tile * TILE, (tile + 1) * TILE)
+        du = (contract_cols(dz_ref[at, :], weight) * slope_ref[at, :].astype(F32)).astype(BF)
+        du_ref[at, :] = du
+        total += jnp.sum(du.astype(F32), axis=0, keepdims=True)
+    sum_ref[...] = total
+
+
+def up_call(x, packed, bias):
+    tokens, width = x.shape
+    hidden = bias.shape[0]
+    tile = pl.BlockSpec((tokens, WIDE), lambda j: (0, j))
+    return pl.pallas_call(up_kernel, grid=(hidden // WIDE,), name="feed",
+        in_specs=[pl.BlockSpec((tokens, width), lambda j: (0, 0)),
+                  pl.BlockSpec((width, WIDE), lambda j: (0, width // WIDE + j)),
+                  pl.BlockSpec((1, WIDE), lambda j: (0, j))],
+        out_specs=[tile, tile],
+        out_shape=[jax.ShapeDtypeStruct((tokens, hidden), BF)] * 2, compiler_params=PARAMS)(x, packed, bias.reshape(1, hidden))
+
+
+def up_back_call(dz, weight, slope):
+    tokens, width = dz.shape
+    hidden = weight.shape[0]
+    tile = pl.BlockSpec((tokens, WIDE), lambda j: (0, j))
+    return pl.pallas_call(up_back_kernel, grid=(hidden // WIDE,), name="feed_back",
+        in_specs=[pl.BlockSpec((tokens, width), lambda j: (0, 0)), pl.BlockSpec((WIDE, width), lambda j: (j, 0)), tile],
+        out_specs=[tile, pl.BlockSpec((1, WIDE), lambda j: (0, j))],
+        out_shape=[jax.ShapeDtypeStruct((tokens, hidden), BF), jax.ShapeDtypeStruct((1, hidden), F32)], compiler_params=PARAMS)(dz, weight, slope)
+
+
+def weight_kernel(own_ref, rows_t_ref, q_ref, k_ref, v_ref, keep_ref, send_ref):
+    rows_t = rows_t_ref[...]
+    share = keep_ref.shape[1]
+    step = q_ref.shape[1]
+    for part, ref in enumerate((q_ref, k_ref, v_ref)):
+        grad = matmul(rows_t, ref[...]).astype(BF).reshape(-1, 2, share, step)
+        at = slice(part * step, (part + 1) * step)
+
+        @pl.when(own_ref[0] == 0)
+        def _():
+            keep_ref[:, :, at] = grad[:, 0]
+            send_ref[:, :, at] = grad[:, 1]
+
+        @pl.when(own_ref[0] == 1)
+        def _():
+            keep_ref[:, :, at] = grad[:, 1]
+            send_ref[:, :, at] = grad[:, 0]
+
+
+def weight_halves(rows_t, parts, devices):
+    width, step = rows_t.shape[0], parts[0].shape[1]
+    own = (lax.axis_index(AXES) & 1).astype(jnp.int32).reshape(1)
+    half = jax.ShapeDtypeStruct((devices // 2, width // devices, 3 * step), BF)
+    return pl.pallas_call(
+        weight_kernel,
+        name="weight_halves",
+        in_specs=[pl.BlockSpec(memory_space=pltpu.SMEM)] + [pl.BlockSpec(memory_space=pltpu.VMEM)] * 4,
+        out_specs=[pl.BlockSpec(memory_space=pltpu.VMEM)] * 2,
+        out_shape=[half, half],
+        compiler_params=pltpu.CompilerParams(vmem_limit_bytes=56 * 2**20),
+    )(own, rows_t, *parts)
+
+
+def input_kernel(*refs):
+    base_ref, weight_ref, pieces, out_ref = refs[0], refs[1], refs[2:-1], refs[-1]
+    width = base_ref.shape[1]
+    step = pieces[0].shape[1]
+    total = base_ref[...]
+    for i, ref in enumerate(pieces):
+        first = PAIR + (i % 3) * width + (i // 3) * step
+        total += contract_cols(ref[...], weight_ref[:, first : first + step])
+    out_ref[...] = total.astype(BF)
+
+
+def input_call(base, head, pieces):
+    tokens, width = base.shape
+    step = pieces[0].shape[1]
+    row = pl.BlockSpec((TILE, width), lambda i: (i, 0))
+    return pl.pallas_call(
+        input_kernel,
+        grid=(tokens // TILE,),
+        name="input_grad",
+        in_specs=[row, pl.BlockSpec(head.shape, lambda i: (0, 0))]
+        + [pl.BlockSpec((TILE, step), lambda i: (i, 0))] * len(pieces),
+        out_specs=row,
+        out_shape=jax.ShapeDtypeStruct((tokens, width), BF),
+        compiler_params=PARAMS,
+    )(base, head, *pieces)
+
+
 def swap(value, bit, devices):
     return lax.ppermute(value, AXES, [(i, i ^ (1 << bit)) for i in range(devices)])
 
@@ -192,30 +301,38 @@
 
 
 class Chain:
-    def __init__(self, value, order, devices, kind=BF):
+    def __init__(self, value, order, devices, kind=BF, pair=None):
         self.devices, self.kind, self.order = devices, kind, list(order)
         self.left = list(range(devices.bit_length() - 1))
-        self.halve(value.reshape((2,) * len(self.left) + (value.shape[0] // devices, value.shape[1])))
+        self.bits = len(self.left)
+        shape = (2,) * self.bits + (value.shape[0] // devices, value.shape[1])
         self.got = None
-
-    def halve(self, work):
+        if pair is None:
+            self.halve([value.reshape(shape)])
+        else:
+            self.left.pop()
+            self.keep, self.send = (half.reshape(shape[1:]) for half in pair)
+
+    def halve(self, terms):
         bit = self.order[0]
-        axis = self.left.index(len(range(self.devices.bit_length() - 1)) - 1 - bit)
+        axis = self.left.index(self.bits - 1 - bit)
         own = (lax.axis_index(AXES) >> bit) & 1
-        self.keep = lax.dynamic_index_in_dim(work, own, axis, keepdims=False)
-        self.send = lax.dynamic_index_in_dim(work, 1 - own, axis, keepdims=False).astype(self.kind)
+        mine = [lax.dynamic_index_in_dim(t, own, axis, keepdims=False) for t in terms]
+        theirs = [lax.dynamic_index_in_dim(t, 1 - own, axis, keepdims=False) for t in terms]
+        self.keep = mine[0] if len(terms) == 1 else mine[0].astype(F32) + mine[1].astype(F32)
+        send = theirs[0] if len(terms) == 1 else theirs[0].astype(F32) + theirs[1].astype(F32)
+        self.send = send.astype(self.kind)
         self.left.pop(axis)
 
     def begin(self):
         self.got = swap(self.send, self.order.pop(0), self.devices)
 
     def finish(self):
-        total = self.keep.astype(F32) + self.got.astype(F32)
-        self.got = None
+        got, self.got = self.got, None
         if self.order:
-            self.halve(total)
+            self.halve([self.keep, got])
         else:
-            self.keep, self.send = total, None
+            self.keep, self.send = self.keep.astype(F32) + got.astype(F32), None
 
     @property
     def over(self):
@@ -277,6 +394,7 @@
 ):
     blocks, length, width = tokens.shape
     rows = tokens.reshape(blocks * length, width)
+    rows_t = rows.T
     own = w_query.shape[0]
     ratio = b_up.shape[0] // own
     vectors = [b_query, b_value, b_out, gain_attn, shift_attn, b_down, gain_ffn, shift_ffn]
@@ -304,8 +422,7 @@
     attended = matmul(context, out_full) + out_bias
     first, normed_one, inverse_one = normalize(rows.astype(F32) + attended, attn_gain, attn_shift)
     first_low = first.astype(BF)
-    pre = matmul(first_low, up_full) + up_bias
-    hidden = jax.nn.gelu(pre, approximate=False).astype(BF)
+    hidden, slope = up_call(first_low, out_up, up_bias)
     branch = matmul(hidden, down_full) + down_bias
     output, normed_two, inverse_two = normalize(first + branch, ffn_gain, ffn_shift)
     encoder_output = output.astype(BF).reshape(tokens.shape)
@@ -313,17 +430,15 @@
     incoming = cotangent.reshape(blocks * length, width).astype(F32)
     grad_two, ffn_gain_grad, ffn_shift_grad = normalize_back(incoming, normed_two, inverse_two, ffn_gain)
     grad_branch = grad_two.astype(BF)
-    down = chains_of(contract_rows(hidden, grad_branch).astype(BF), devices)
+    down = chains_of(contract_rows(hidden, grad_branch).astype(BF), devices, parts=2)
     down_bias_grad = jnp.sum(grad_branch.astype(F32), axis=0)
     running = list(down)
     grad_branch = tick(running, grad_branch)
-    grad_hidden = contract_cols(grad_branch, down_full)
-    _, gelu_pull = jax.vjp(partial(jax.nn.gelu, approximate=False), pre)
-    grad_pre = gelu_pull(grad_hidden)[0].astype(BF)
-    up_bias_grad = jnp.sum(grad_pre.astype(F32), axis=0)
+    grad_pre, up_bias_grad = up_back_call(grad_branch, down_full, slope)
+    up_bias_grad = up_bias_grad[0]
     grad_pre = tick(running, grad_pre)
     up_product = contract_rows(first_low, grad_pre).astype(BF)
-    up = chains_of(up_product, devices, turn=1)
+    up = chains_of(up_product, devices, parts=2, turn=2)
     running += up
     grad_pre = tick(running, grad_pre)
     grad_first = grad_two + contract_cols(grad_pre, up_full)
@@ -343,10 +458,16 @@
         if chunk + 1 < CHUNKS:
             grad_context, piece = lax.optimization_barrier((grad_context, piece))
         pieces.append(piece)
-        grads = jnp.concatenate([contract_rows(rows, part).astype(BF) for part in piece[:3]], axis=1)
-        shares.append(chains_of(grads, devices, parts=1, turn=chunk))
+        if own % 32 == 0:
+            pair = weight_halves(rows_t, piece[:3], devices)
+            order = bit_orders(devices.bit_length() - 1)[chunk % 3]
+            grads = jax.ShapeDtypeStruct((width, pair[0].shape[2]), BF)
+            shares.append([Chain(grads, order, devices, pair=pair)])
+        else:
+            grads = jnp.concatenate([matmul(rows_t, part).astype(BF) for part in piece[:3]], axis=1)
+            shares.append(chains_of(grads, devices, parts=1, turn=chunk))
         running += shares[-1]
-    joined = [jnp.concatenate([piece[part] for piece in pieces], axis=1) for part in range(5)]
+    joined = {part: jnp.concatenate([piece[part] for piece in pieces], axis=1) for part in (3, 4)}
     vector_grads = [
         joined[3][0], joined[4][0], out_bias_grad, attn_gain_grad, attn_shift_grad,
         down_bias_grad, ffn_gain_grad, ffn_shift_grad,
@@ -357,9 +478,9 @@
     )
     side = chains_of(side_grad, devices, parts=1, kind=F32)
     running += side
-    total = tick(running, jnp.concatenate(joined[:3], axis=1))
-    total_input = grad_one + contract_cols(total, packed_full)
-    layer_input_gradient = total_input.astype(BF).reshape(tokens.shape)
+    pieces = tick(running, [part for piece in pieces for part in piece[:3]])
+    total_input = input_call(grad_one, head, pieces)
+    layer_input_gradient = total_input.reshape(tokens.shape)
     while not all(c.over for c in running):
         tick(running, ())
 

time: 778 us -> 656 us (0.84)
  matrix products: 175 us -> 76.2 us
  local copies, waits for them, and re-layouts: 124 us -> 38.5 us
  Pallas kernels: 137 us -> 211 us
  starting transfers between devices: 74.2 us -> 60.6 us
  waiting for transfers between devices: 162 us -> 174 us
    pallas_call x0 -> x7, Pallas kernels: none -> 74.9 us  [the longest x4 25.9 us: weight_halves(): pl.pallas_call(weight_kernel, name='weight_halves', in_specs=[pl.BlockSpe...]
    dot_general x4 -> x3, matrix products: 75.4 us -> 28 us  [matmul(): return jnp.dot(left, right, preferred_element_type=F32)]
    unnamed x227 -> x83, local copies, waits for them, and re-layouts: 41.6 us -> 6.85 us
    dot_general x4 -> x2, matrix products: 58.2 us -> 24.6 us  [contract_cols(): lax.dot_general(left, right, (((1,), (1,)), ((), ())), preferred_element_...]
    all_gather x1, waiting for transfers between devices: 0.01 us -> 33.6 us  [local(): down_full = lax.all_gather(later[1], AXES, axis=0, tiled=True)]
    convert_element_type x1 -> x37, other arithmetic: 0.66 us -> 31.3 us  [the longest x36 29.2 us: halve(): self.send = send.astype(self.kind)]
    squeeze x53 -> x1, local copies, waits for them, and re-layouts: 23.7 us -> 0.02 us  [halve(): lax.dynamic_index_in_dim(t, 1 - own, axis, keepdims=False)]
    add x60 -> x15, other arithmetic: 24.1 us -> 1.61 us  [the longest x10 1.52 us: finish(): self.keep, self.send = (self.keep.astype(F32) + got.astype(F32), None)]
  transfers between devices with their start and end apart: 77 -> 67, of which waited for: 29 -> 21; matrix products, arithmetic and copies ran while one was open for 32% -> 17% of each run, Pallas kernels for 8% -> 33%
where the time goes in v1:
time: 656 us; the launch traced here: 649 us
  Pallas kernels  211 us (32%)
  waiting for transfers between devices  174 us (27%)
  matrix products  76.2 us (12%)
  other arithmetic  73.4 us (11%)
  starting transfers between devices  60.6 us (9%)
  local copies, waits for them, and re-layouts  38.5 us (6%)
  between operations  15.7 us (2%)
    ppermute x65, waiting for transfers between devices, swap(): lax.ppermute(value, AXES, [(i, i ^ 1 << bit) for i in range(devices)])  139 us
    pallas_call x4, Pallas kernels, attend_back(): pl.pallas_call(backward_kernel, grid=(count,), name='attend_back', in_spe...  76.9 us
    ppermute x65, starting transfers between devices, swap(): lax.ppermute(value, AXES, [(i, i ^ 1 << bit) for i in range(devices)])  60.5 us
    pallas_call x1, Pallas kernels, attend(): pl.pallas_call(forward_kernel, grid=(pairs,), name='attend', in_specs=seg...  59.5 us
    all_gather x1, waiting for transfers between devices, local(): down_full = lax.all_gather(later[1], AXES, axis=0, tiled=True)  33.6 us
    convert_element_type x36, other arithmetic, halve(): self.send = send.astype(self.kind)  29.2 us
    dot_general x3, matrix products, matmul(): return jnp.dot(left, right, preferred_element_type=F32)  28 us
    pallas_call x4, Pallas kernels, weight_halves(): pl.pallas_call(weight_kernel, name='weight_halves', in_specs=[pl.BlockSpe...  25.9 us
  transfers between devices with their start and end apart: 67, of which 21 were waited for; matrix products, arithmetic and copies ran while one was open for 17% of the time, Pallas kernels for 33%

profile of v1, /device:TPU:0, one launch (start us, length us, event | category | flops | bytes accessed | tf_op | source)
XLA Modules:
  0.0 649.5 jit_solution(17239494434520484302)
XLA Ops:
  31.6 5.3 collective-permute-done.4
  39.8 8.2 %collective-permute-done.5 = bf16[2,2,32,1024]{3,2,1,0:T(8,128)(2,1)S(1)} collective-permute-done((bf16[2,2,32,1024]{3,2,1,0:T(8,128)(2,1)S(1)}, bf16[2,2,32,1024]{3,2,1,0:T(8,128)(2,1)S(1)}, u32[]{:S(2)}, u32[]{:S(2)}) %collective-permute-start.5) | collective-permute-done | bytes 262176 | tf_op jit(solution)/shard_map/ppermute | solution.py:288
  56.6 5.7 collective-permute-done.11
  64.6 10.0 %collective-permute-done.13 = bf16[2,2,2,32,1152]{4,3,1,2,0:T(8,128)(2,1)S(1)} collective-permute-done((bf16[2,2,2,32,1152]{4,3,1,2,0:T(8,128)(2,1)S(1)}, bf16[2,2,2,32,1152]{4,3,1,2,0:T(8,128)(2,1)S(1)}, u32[]{:S(2)}, u32[]{:S(2)}) %collective-permute-start.13) | collective-permute-done | bytes 589856 | tf_op jit(solution)/shard_map/ppermute | solution.py:288
  88.9 8.6 %fusion.2.q_ref.k_ref.v_ref = bf16[1024,3072]{1,0:T(8,128)(2,1)} fusion(f32[3072]{0:T(1024)S(1)} %pad_maximum_fusion.11, bf16[1024,3200]{1,0:T(8,128)(2,1)S(1)} %pad_maximum_fusion.refs_1_, bf16[1,1024,1024]{2,1,0:T(8,128)(2,1)S(1)} %copy-done.14), kind=kOutput, calls=%fused_computation.6 | convolution fusion | flops 6448742400 | bytes 14692352 | tf_op jit(solution)/shard_map/dot_general | solution.py:25
  97.5 59.5 %attend.1 = (bf16[1024,1024]{1,0:T(8,128)(2,1)}, f32[8,2,1024]{2,1,0:T(2,128)}) custom-call(s32[1024,1]{1,0:T(8,128)} %copy.162.seg_col, s32[1,1024]{1,0:T(1,128)} %seg_row.9, bf16[1024,3072]{1,0:T(8,128)(2,1)} %fusion.2.q_ref.k_ref.v_ref, bf16[1024,3072]{1,0:T(8,128)(2,1)} %fusion.2.q_ref.k_ref.v_ref, bf16[1024,3072]{1,0:T(8,128)(2,1)} %fusion.2.q_ref.k_ref.v_ref), custom_call_target="tpu_custom_call" | custom-call | tf_op jit(solution)/shard_map/attend/pallas_call | solution.py:137
  156.9 4.7 fusion.91
  165.7 20.1 %feed.1 = (bf16[1024,4096]{1,0:T(8,128)(2,1)}, bf16[1024,4096]{1,0:T(8,128)(2,1)}) custom-call(bf16[1024,1024]{1,0:T(8,128)(2,1)} %fusion.16.x_ref, bf16[1024,5120]{1,0:T(8,128)(2,1)} %all-gather.3.cloned.1.call-done.w_ref, f32[1,4096]{1,0:T(1,128)} %reshape.1338.b_ref), custom_call_target="tpu_custom_call" | custom-call | tf_op jit(solution)/shard_map/feed/pallas_call | solution.py:209
  185.9 33.6 %all-gather.5.cloned.1.call-done.w_ref = bf16[4096,1024]{1,0:T(8,128)(2,1)} async-done(((bf16[128,1024]{1,0:T(8,128)(2,1)}), bf16[4096,1024]{1,0:T(8,128)(2,1)}) %all-gather.5.cloned.1.call-update) | async-done | bytes 8388624 | tf_op jit(solution)/shard_map/all_gather | solution.py:415
  219.4 14.8 %fusion.92 = (f32[1024]{0:T(1024)S(1)}, f32[1024,1024]{1,0:T(8,128)S(1)}) fusion(f32[1024]{0:T(1024)S(1)} %get-tuple-element.400, bf16[1024,4096]{1,0:T(8,128)(2,1)} %get-tuple-element.209, bf16[4096,1024]{1,0:T(8,128)(2,1)} %all-gather.5.cloned.1.call-done.w_ref, f32[1024]{0:T(1024)S(1)} %get-tuple-element.401, f32[1024]{0:T(1024)S(1)} %get-tuple-element.402, ...), kind=kOutput, calls=%fused_computation.303 | convolution fusion | flops 8597273600 | bytes 25190400 | tf_op jit(solution)/shard_map/dot_general | solution.py:25
  243.7 9.8 %convolution_convert_fusion.1 = bf16[4096,1024]{1,0:T(8,128)(2,1)S(1)} fusion(bf16[1024,4096]{1,0:T(8,128)(2,1)S(1)} %bitcast.437, bf16[1024,1024]{1,0:T(8,128)(2,1)S(1)} %get-tuple-element.211.dz_ref), kind=kOutput, calls=%fused_computation.4 | convolution fusion | flops 8594128896 | bytes 18874368 | tf_op jit(solution)/shard_map/dot_general | solution.py:29
  260.6 16.7 %feed_back.1 = (bf16[1024,4096]{1,0:T(8,128)(2,1)}, f32[1,4096]{1,0:T(1,128)}) custom-call(bf16[1024,1024]{1,0:T(8,128)(2,1)} %copy-done.8, bf16[4096,1024]{1,0:T(8,128)(2,1)} %all-gather.5.cloned.1.call-done.w_ref, bf16[1024,4096]{1,0:T(8,128)(2,1)} %get-tuple-element.212.slope_ref), custom_call_target="tpu_custom_call" | custom-call | tf_op jit(solution)/shard_map/feed_back/pallas_call | solution.py:221
  281.9 11.4 %convolution_convert_fusion = bf16[1024,4096]{1,0:T(8,128)(2,1)S(1)} fusion(bf16[1024,1024]{1,0:T(8,128)(2,1)S(1)} %copy-done.7, bf16[1024,4096]{1,0:T(8,128)(2,1)} %get-tuple-element.223), kind=kOutput, calls=%fused_computation.3 | convolution fusion | flops 8594128896 | bytes 18874368 | tf_op jit(solution)/shard_map/dot_general | solution.py:29
  304.2 15.7 %collective-permute-done.17 = bf16[2,2,2,128,512]{4,3,0,1,2:T(8,128)(2,1)S(1)} collective-permute-done((bf16[2,2,2,128,512]{4,3,0,1,2:T(8,128)(2,1)S(1)}, bf16[2,2,2,128,512]{4,3,0,1,2:T(8,128)(2,1)S(1)}, u32[]{:S(2)}, u32[]{:S(2)}) %collective-permute-start.17) | collective-permute-done | bytes 1048608 | tf_op jit(solution)/shard_map/ppermute | solution.py:288
  325.3 19.3 %multiply_reduce_fusion = (f32[1024]{0:T(1024)S(1)}, f32[1024]{0:T(1024)S(1)}, f32[1024]{0:T(1024)S(1)}, f32[1024]{0:T(1024)}, f32[1024,1024]{1,0:T(8,128)}) fusion(f32[1024,1024]{1,0:T(8,128)} %copy-done.2, f32[1024]{0:T(1024)S(1)} %add_rsqrt_fusion.1, f32[1024]{0:T(1024)S(1)} %broadcast_multiply_fusion.5, f32[1024]{0:T(1024)S(1)} %get-tuple-element.402, ...), kind=kOutput, calls=%fused_computation.21 | convolution fusion | flops 8608804864 | bytes 31506432 | tf_op jit(solution)/shard_map/dot_general | solution.py:33
  344.6 5.6 convert_reduce_fusion.2
  364.8 5.3 convolution_convert_fusion.3.do_ref
  371.4 20.0 %collective-permute-done.24 = bf16[2,128,512]{2,1,0:T(8,128)(2,1)S(1)} collective-permute-done((bf16[2,128,512]{2,1,0:T(8,128)(2,1)S(1)}, bf16[2,128,512]{2,1,0:T(8,128)(2,1)S(1)}, u32[]{:S(2)}, u32[]{:S(2)}) %collective-permute-start.24) | collective-permute-done | bytes 262176 | tf_op jit(solution)/shard_map/ppermute | solution.py:288
  392.2 5.0 collective-permute-done.23
  406.2 19.5 %attend_back.4 = (bf16[1024,256]{1,0:T(8,128)(2,1)}, bf16[1024,256]{1,0:T(8,128)(2,1)}, bf16[1024,256]{1,0:T(8,128)(2,1)}, f32[1,256]{1,0:T(1,128)}, f32[1,256]{1,0:T(1,128)}) custom-call(s32[1024,1]{1,0:T(8,128)} %copy.162.seg_col, s32[1,1024]{1,0:T(1,128)} %seg_row.9, bf16[1024,3072]{1,0:T(8,128)(2,1)} %fusion.2.q_ref.k_ref.v_ref, ...), custom_call_target="tpu_custom_call" | custom-call | tf_op jit(solution)/shard_map/attend_back/pallas_call | solution.py:159
  428.6 6.5 weight_halves.4
  435.2 22.3 %collective-permute-done.27 = bf16[128,512]{1,0:T(8,128)(2,1)S(1)} collective-permute-done((bf16[128,512]{1,0:T(8,128)(2,1)}, bf16[128,512]{1,0:T(8,128)(2,1)S(1)}, u32[]{:S(2)}, u32[]{:S(2)}) %collective-permute-start.27) | collective-permute-done | bytes 131104 | tf_op jit(solution)/shard_map/ppermute | solution.py:288
  464.7 19.0 %attend_back.5 = (bf16[1024,256]{1,0:T(8,128)(2,1)}, bf16[1024,256]{1,0:T(8,128)(2,1)}, bf16[1024,256]{1,0:T(8,128)(2,1)}, f32[1,256]{1,0:T(1,128)}, f32[1,256]{1,0:T(1,128)}) custom-call(s32[1024,1]{1,0:T(8,128)} %copy.162.seg_col, s32[1,1024]{1,0:T(1,128)} %seg_row.9, bf16[1024,3072]{1,0:T(8,128)(2,1)} %fusion.2.q_ref.k_ref.v_ref, ...), custom_call_target="tpu_custom_call" | custom-call | tf_op jit(solution)/shard_map/attend_back/pallas_call | solution.py:159
  483.7 6.5 %weight_halves.5 = (bf16[16,32,768]{2,1,0:T(8,128)(2,1)}, bf16[16,32,768]{2,1,0:T(8,128)(2,1)}) custom-call(s32[1]{0:T(128)} %bitcast.104.own_ref, bf16[1024,1024]{1,0:T(8,128)(2,1)} %copy.175.rows_t_ref, bf16[1024,256]{1,0:T(8,128)(2,1)} %get-tuple-element.332.q_ref.refs_5_, bf16[1024,256]{1,0:T(8,128)(2,1)} %get-tuple-element.333.k_ref.refs_6_, ...), custom_call_target="tpu_custom_call" | custom-call | tf_op jit(solution)/shard_map/weight_halves/pallas_call | solution.py:250
  491.3 19.1 %attend_back.6 = (bf16[1024,256]{1,0:T(8,128)(2,1)}, bf16[1024,256]{1,0:T(8,128)(2,1)}, bf16[1024,256]{1,0:T(8,128)(2,1)}, f32[1,256]{1,0:T(1,128)}, f32[1,256]{1,0:T(1,128)}) custom-call(s32[1024,1]{1,0:T(8,128)} %copy.162.seg_col, s32[1,1024]{1,0:T(1,128)} %seg_row.9, bf16[1024,3072]{1,0:T(8,128)(2,1)} %fusion.2.q_ref.k_ref.v_ref, ...), custom_call_target="tpu_custom_call" | custom-call | tf_op jit(solution)/shard_map/attend_back/pallas_call | solution.py:159
  515.1 6.4 weight_halves.6
  521.6 5.4 collective-permute-done.38
  533.3 19.3 %attend_back.7 = (bf16[1024,256]{1,0:T(8,128)(2,1)}, bf16[1024,256]{1,0:T(8,128)(2,1)}, bf16[1024,256]{1,0:T(8,128)(2,1)}, f32[1,256]{1,0:T(1,128)}, f32[1,256]{1,0:T(1,128)}) custom-call(s32[1024,1]{1,0:T(8,128)} %copy.162.seg_col, s32[1,1024]{1,0:T(1,128)} %seg_row.9, bf16[1024,3072]{1,0:T(8,128)(2,1)} %fusion.2.q_ref.k_ref.v_ref, ...), custom_call_target="tpu_custom_call" | custom-call | tf_op jit(solution)/shard_map/attend_back/pallas_call | solution.py:159
  556.0 6.4 weight_halves.7
  575.9 10.4 %collective-permute-done.46 = bf16[2,32,768]{2,1,0:T(8,128)(2,1)S(1)} collective-permute-done((bf16[2,32,768]{2,1,0:T(8,128)(2,1)S(1)}, bf16[2,32,768]{2,1,0:T(8,128)(2,1)S(1)}, u32[]{:S(2)}, u32[]{:S(2)}) %collective-permute-start.46) | collective-permute-done | bytes 98336 | tf_op jit(solution)/shard_map/ppermute | solution.py:288
  589.1 12.2 %input_grad.1 = bf16[1024,1024]{1,0:T(8,128)(2,1)} custom-call(f32[1024,1024]{1,0:T(8,128)} %get-tuple-element.410.refs_0_, bf16[1024,3200]{1,0:T(8,128)(2,1)} %copy-done.3, bf16[1024,256]{1,0:T(8,128)(2,1)} %get-tuple-element.329.q_ref.refs_2_, bf16[1024,256]{1,0:T(8,128)(2,1)} %get-tuple-element.330.k_ref.refs_3_, ...), custom_call_target="tpu_custom_call" | custom-call | tf_op jit(solution)/shard_map/input_grad/pallas_call | solution.py:275
  605.6 13.1 %collective-permute-done.51 = bf16[32,768]{1,0:T(8,128)(2,1)S(1)} collective-permute-done((bf16[32,768]{1,0:T(8,128)(2,1)S(1)}, bf16[32,768]{1,0:T(8,128)(2,1)S(1)}, u32[]{:S(2)}, u32[]{:S(2)}) %collective-permute-start.51) | collective-permute-done | bytes 49184 | tf_op jit(solution)/shard_map/ppermute | solution.py:288
  (396 shorter events, 188.3 us)
Async XLA Ops:
  7.2 149.7 %all-gather.3.cloned.1.call-start = ((), (), s32[]{:S(2)}) async-start(), calls=%async_computation | async-start | bytes 10813440 | tf_op jit(solution)/shard_map/all_gather | solution.py:414
  52.2 167.2 %all-gather.5.cloned.1.call-start = ((), (), s32[]{:S(2)}) async-start(), calls=%async_computation.1 | async-start | bytes 8650752 | tf_op jit(solution)/shard_map/all_gather | solution.py:415
  56.1 18.4 %collective-permute-start.13 = (bf16[2,2,2,32,1152]{4,3,1,2,0:T(8,128)(2,1)S(1)}, bf16[2,2,2,32,1152]{4,3,1,2,0:T(8,128)(2,1)S(1)}, u32[]{:S(2)}, u32[]{:S(2)}) collective-permute-start(bf16[2,2,2,32,1152]{4,3,1,2,0:T(8,128)(2,1)S(1)} %maximum_select_fusion.8), channel_id=1, source_target_pairs={{0,8},{1,9},{2,10},{3,11},{4,12},{5,13},{6,14},{7,15},{8,0},{9,1},... | collective-permute-start | bytes 1769480 | tf_op jit(solution)/shard_map/ppermute | solution.py:288
  260.3 19.2 %collective-permute-start.15 = (bf16[2,2,2,2,128,512]{5,4,0,1,2,3:T(8,128)(2,1)}, bf16[2,2,2,2,128,512]{5,4,0,1,2,3:T(8,128)(2,1)}, u32[]{:S(2)}, u32[]{:S(2)}) collective-permute-start(bf16[2,2,2,2,128,512]{5,4,0,1,2,3:T(8,128)(2,1)} %bitcast.362), channel_id=1, source_target_pairs={{0,1},{1,0},{2,3},{3,2},{4,5},{5,4},{6,7},{7,6},{8,9},{9,8},{10,11... | collective-permute-start | bytes 6291464 | tf_op jit(solution)/shard_map/ppermute | solution.py:288
  293.3 27.9 %collective-permute-start.18 = (bf16[2,2,2,128,512]{4,3,2,0,1:T(8,128)(2,1)S(1)}, bf16[2,2,2,128,512]{4,3,2,0,1:T(8,128)(2,1)S(1)}, u32[]{:S(2)}, u32[]{:S(2)}) collective-permute-start(bf16[2,2,2,128,512]{4,3,2,0,1:T(8,128)(2,1)S(1)} %get-tuple-element.222), channel_id=1, source_target_pairs={{0,4},{1,5},{2,6},{3,7},{4,0},{5,1},{6,2},{7,3},{8,12},{9,13},{10,... | collective-permute-start | bytes 3145736 | tf_op jit(solution)/shard_map/ppermute | solution.py:288
  294.9 25.0 %collective-permute-start.17 = (bf16[2,2,2,128,512]{4,3,0,1,2:T(8,128)(2,1)S(1)}, bf16[2,2,2,128,512]{4,3,0,1,2:T(8,128)(2,1)S(1)}, u32[]{:S(2)}, u32[]{:S(2)}) collective-permute-start(bf16[2,2,2,128,512]{4,3,0,1,2:T(8,128)(2,1)S(1)} %get-tuple-element.220), channel_id=1, source_target_pairs={{0,2},{1,3},{2,0},{3,1},{4,6},{5,7},{6,4},{7,5},{8,10},{9,11},{10,... | collective-permute-start | bytes 3145736 | tf_op jit(solution)/shard_map/ppermute | solution.py:288
  322.8 30.1 %collective-permute-start.22 = (bf16[2,2,2,2,32,2048]{5,4,0,1,2,3:T(8,128)(2,1)}, bf16[2,2,2,2,32,2048]{5,4,0,1,2,3:T(8,128)(2,1)}, u32[]{:S(2)}, u32[]{:S(2)}) collective-permute-start(bf16[2,2,2,2,32,2048]{5,4,0,1,2,3:T(8,128)(2,1)} %bitcast.356), channel_id=1, source_target_pairs={{0,1},{1,0},{2,3},{3,2},{4,5},{5,4},{6,7},{7,6},{8,9},{9,8},{10,11... | collective-permute-start | bytes 6291464 | tf_op jit(solution)/shard_map/ppermute | solution.py:288
  322.8 32.6 %collective-permute-start.21 = (bf16[2,2,2,2,32,2048]{5,4,2,3,0,1:T(8,128)(2,1)}, bf16[2,2,2,2,32,2048]{5,4,2,3,0,1:T(8,128)(2,1)}, u32[]{:S(2)}, u32[]{:S(2)}) collective-permute-start(bf16[2,2,2,2,32,2048]{5,4,2,3,0,1:T(8,128)(2,1)} %bitcast.358), channel_id=1, source_target_pairs={{0,1},{1,0},{2,3},{3,2},{4,5},{5,4},{6,7},{7,6},{8,9},{9,8},{10,11... | collective-permute-start | bytes 6291464 | tf_op jit(solution)/shard_map/ppermute | solution.py:288
  323.3 28.4 %collective-permute-start.20 = (bf16[2,2,128,512]{3,2,1,0:T(8,128)(2,1)}, bf16[2,2,128,512]{3,2,1,0:T(8,128)(2,1)}, u32[]{:S(2)}, u32[]{:S(2)}) collective-permute-start(bf16[2,2,128,512]{3,2,1,0:T(8,128)(2,1)} %get-tuple-element.227), channel_id=1, source_target_pairs={{0,8},{1,9},{2,10},{3,11},{4,12},{5,13},{6,14},{7,15},{8,0},{9,1},... | collective-permute-start | bytes 1572872 | tf_op jit(solution)/shard_map/ppermute | solution.py:288
  324.8 25.5 %collective-permute-start.19 = (bf16[2,2,128,512]{3,2,0,1:T(8,128)(2,1)S(1)}, bf16[2,2,128,512]{3,2,0,1:T(8,128)(2,1)}, u32[]{:S(2)}, u32[]{:S(2)}) collective-permute-start(bf16[2,2,128,512]{3,2,0,1:T(8,128)(2,1)S(1)} %get-tuple-element.225), channel_id=1, source_target_pairs={{0,4},{1,5},{2,6},{3,7},{4,0},{5,1},{6,2},{7,3},{8,12},{9,13},{10,... | collective-permute-start | bytes 1572872 | tf_op jit(solution)/shard_map/ppermute | solution.py:288
  357.7 40.3 %collective-permute-start.26 = (bf16[2,2,2,32,2048]{4,3,0,1,2:T(8,128)(2,1)S(1)}, bf16[2,2,2,32,2048]{4,3,0,1,2:T(8,128)(2,1)S(1)}, u32[]{:S(2)}, u32[]{:S(2)}) collective-permute-start(bf16[2,2,2,32,2048]{4,3,0,1,2:T(8,128)(2,1)S(1)} %get-tuple-element.240), channel_id=1, source_target_pairs={{0,2},{1,3},{2,0},{3,1},{4,6},{5,7},{6,4},{7,5},{8,10},{9,11},{10,... | collective-permute-start | bytes 3145736 | tf_op jit(solution)/shard_map/ppermute | solution.py:288
  361.7 37.4 %collective-permute-start.25 = (bf16[2,2,2,32,2048]{4,3,1,2,0:T(8,128)(2,1)S(1)}, bf16[2,2,2,32,2048]{4,3,1,2,0:T(8,128)(2,1)S(1)}, u32[]{:S(2)}, u32[]{:S(2)}) collective-permute-start(bf16[2,2,2,32,2048]{4,3,1,2,0:T(8,128)(2,1)S(1)} %get-tuple-element.238), channel_id=1, source_target_pairs={{0,8},{1,9},{2,10},{3,11},{4,12},{5,13},{6,14},{7,15},{8,0},{9,1},... | collective-permute-start | bytes 3145736 | tf_op jit(solution)/shard_map/ppermute | solution.py:288
  362.3 29.2 %collective-permute-start.24 = (bf16[2,128,512]{2,1,0:T(8,128)(2,1)S(1)}, bf16[2,128,512]{2,1,0:T(8,128)(2,1)S(1)}, u32[]{:S(2)}, u32[]{:S(2)}) collective-permute-start(bf16[2,128,512]{2,1,0:T(8,128)(2,1)S(1)} %get-tuple-element.236), channel_id=1, source_target_pairs={{0,16},{1,17},{2,18},{3,19},{4,20},{5,21},{6,22},{7,23},{8,24},{9,... | collective-permute-start | bytes 786440 | tf_op jit(solution)/shard_map/ppermute | solution.py:288
  364.2 33.0 %collective-permute-start.23 = (bf16[2,128,512]{2,1,0:T(8,128)(2,1)S(1)}, bf16[2,128,512]{2,1,0:T(8,128)(2,1)S(1)}, u32[]{:S(2)}, u32[]{:S(2)}) collective-permute-start(bf16[2,128,512]{2,1,0:T(8,128)(2,1)S(1)} %get-tuple-element.234), channel_id=1, source_target_pairs={{0,8},{1,9},{2,10},{3,11},{4,12},{5,13},{6,14},{7,15},{8,0},{9,1},... | collective-permute-start | bytes 786440 | tf_op jit(solution)/shard_map/ppermute | solution.py:288
  400.1 35.0 %collective-permute-start.28 = (bf16[128,512]{1,0:T(8,128)(2,1)S(1)}, bf16[128,512]{1,0:T(8,128)(2,1)S(1)}, u32[]{:S(2)}, u32[]{:S(2)}) collective-permute-start(bf16[128,512]{1,0:T(8,128)(2,1)S(1)} %get-tuple-element.255), channel_id=1, source_target_pairs={{0,2},{1,3},{2,0},{3,1},{4,6},{5,7},{6,4},{7,5},{8,10},{9,11},{10,... | collective-permute-start | bytes 393224 | tf_op jit(solution)/shard_map/ppermute | solution.py:288
  400.7 59.5 %collective-permute-start.31 = (bf16[2,2,2,2,32,1024]{5,4,2,3,0,1:T(8,128)(2,1)}, bf16[2,2,2,2,32,1024]{5,4,2,3,0,1:T(8,128)(2,1)}, u32[]{:S(2)}, u32[]{:S(2)}) collective-permute-start(bf16[2,2,2,2,32,1024]{5,4,2,3,0,1:T(8,128)(2,1)} %bitcast.364), channel_id=1, source_target_pairs={{0,1},{1,0},{2,3},{3,2},{4,5},{5,4},{6,7},{7,6},{8,9},{9,8},{10,11... | collective-permute-start | bytes 3145736 | tf_op jit(solution)/shard_map/ppermute | solution.py:288
  400.7 57.5 %collective-permute-start.30 = (bf16[2,2,32,2048]{3,2,0,1:T(8,128)(2,1)}, bf16[2,2,32,2048]{3,2,0,1:T(8,128)(2,1)}, u32[]{:S(2)}, u32[]{:S(2)}) collective-permute-start(bf16[2,2,32,2048]{3,2,0,1:T(8,128)(2,1)} %get-tuple-element.259), channel_id=1, source_target_pairs={{0,4},{1,5},{2,6},{3,7},{4,0},{5,1},{6,2},{7,3},{8,12},{9,13},{10,... | collective-permute-start | bytes 1572872 | tf_op jit(solution)/shard_map/ppermute | solution.py:288
  425.6 34.5 %collective-permute-start.29 = (bf16[2,2,32,2048]{3,2,0,1:T(8,128)(2,1)S(1)}, bf16[2,2,32,2048]{3,2,0,1:T(8,128)(2,1)S(1)}, u32[]{:S(2)}, u32[]{:S(2)}) collective-permute-start(bf16[2,2,32,2048]{3,2,0,1:T(8,128)(2,1)S(1)} %copy-done.26), channel_id=1, source_target_pairs={{0,16},{1,17},{2,18},{3,19},{4,20},{5,21},{6,22},{7,23},{8,24},{9,... | collective-permute-start | bytes 1572872 | tf_op jit(solution)/shard_map/ppermute | solution.py:288
  426.7 30.8 %collective-permute-start.27 = (bf16[128,512]{1,0:T(8,128)(2,1)}, bf16[128,512]{1,0:T(8,128)(2,1)S(1)}, u32[]{:S(2)}, u32[]{:S(2)}) collective-permute-start(bf16[128,512]{1,0:T(8,128)(2,1)} %get-tuple-element.253), channel_id=1, source_target_pairs={{0,16},{1,17},{2,18},{3,19},{4,20},{5,21},{6,22},{7,23},{8,24},{9,... | collective-permute-start | bytes 393224 | tf_op jit(solution)/shard_map/ppermute | solution.py:288
  461.8 28.5 %collective-permute-start.33 = (bf16[2,32,2048]{2,1,0:T(8,128)(2,1)}, bf16[2,32,2048]{2,1,0:T(8,128)(2,1)S(1)}, u32[]{:S(2)}, u32[]{:S(2)}) collective-permute-start(bf16[2,32,2048]{2,1,0:T(8,128)(2,1)} %get-tuple-element.277), channel_id=1, source_target_pairs={{0,8},{1,9},{2,10},{3,11},{4,12},{5,13},{6,14},{7,15},{8,0},{9,1},... | collective-permute-start | bytes 786440 | tf_op jit(solution)/shard_map/ppermute | solution.py:288
  461.9 28.6 %collective-permute-start.35 = (bf16[2,2,2,2,32,768]{5,4,0,1,2,3:T(8,128)(2,1)S(1)}, bf16[2,2,2,2,32,768]{5,4,0,1,2,3:T(8,128)(2,1)S(1)}, u32[]{:S(2)}, u32[]{:S(2)}) collective-permute-start(bf16[2,2,2,2,32,768]{5,4,0,1,2,3:T(8,128)(2,1)S(1)} %copy.178), channel_id=1, source_target_pairs={{0,1},{1,0},{2,3},{3,2},{4,5},{5,4},{6,7},{7,6},{8,9},{9,8},{10,11... | collective-permute-start | bytes 2359304 | tf_op jit(solution)/shard_map/ppermute | solution.py:288
  462.1 28.3 %collective-permute-start.34 = (bf16[2,2,2,32,1024]{4,3,1,2,0:T(8,128)(2,1)S(1)}, bf16[2,2,2,32,1024]{4,3,1,2,0:T(8,128)(2,1)S(1)}, u32[]{:S(2)}, u32[]{:S(2)}) collective-permute-start(bf16[2,2,2,32,1024]{4,3,1,2,0:T(8,128)(2,1)S(1)} %get-tuple-element.279), channel_id=1, source_target_pairs={{0,8},{1,9},{2,10},{3,11},{4,12},{5,13},{6,14},{7,15},{8,0},{9,1},... | collective-permute-start | bytes 1572872 | tf_op jit(solution)/shard_map/ppermute | solution.py:288
  464.1 26.2 %collective-permute-start.32 = (bf16[2,32,2048]{2,1,0:T(8,128)(2,1)S(1)}, bf16[2,32,2048]{2,1,0:T(8,128)(2,1)S(1)}, u32[]{:S(2)}, u32[]{:S(2)}) collective-permute-start(bf16[2,32,2048]{2,1,0:T(8,128)(2,1)S(1)} %get-tuple-element.275), channel_id=1, source_target_pairs={{0,2},{1,3},{2,0},{3,1},{4,6},{5,7},{6,4},{7,5},{8,10},{9,11},{10,... | collective-permute-start | bytes 786440 | tf_op jit(solution)/shard_map/ppermute | solution.py:288
  490.7 30.8 %collective-permute-start.37 = (bf16[32,2048]{1,0:T(8,128)(2,1)S(1)}, bf16[32,2048]{1,0:T(8,128)(2,1)S(1)}, u32[]{:S(2)}, u32[]{:S(2)}) collective-permute-start(bf16[32,2048]{1,0:T(8,128)(2,1)S(1)} %get-tuple-element.297), channel_id=1, source_target_pairs={{0,16},{1,17},{2,18},{3,19},{4,20},{5,21},{6,22},{7,23},{8,24},{9,... | collective-permute-start | bytes 393224 | tf_op jit(solution)/shard_map/ppermute | solution.py:288
  510.5 18.0 %collective-permute-start.40 = (bf16[2,2,2,2,32,768]{5,4,3,0,1,2:T(8,128)(2,1)S(1)}, bf16[2,2,2,2,32,768]{5,4,3,0,1,2:T(8,128)(2,1)S(1)}, u32[]{:S(2)}, u32[]{:S(2)}) collective-permute-start(bf16[2,2,2,2,32,768]{5,4,3,0,1,2:T(8,128)(2,1)S(1)} %copy.183), channel_id=1, source_target_pairs={{0,1},{1,0},{2,3},{3,2},{4,5},{5,4},{6,7},{7,6},{8,9},{9,8},{10,11... | collective-permute-start | bytes 2359304 | tf_op jit(solution)/shard_map/ppermute | solution.py:288
  529.5 36.3 %collective-permute-start.44 = (bf16[2,2,2,2,32,768]{5,4,2,3,0,1:T(8,128)(2,1)S(1)}, bf16[2,2,2,2,32,768]{5,4,2,3,0,1:T(8,128)(2,1)}, u32[]{:S(2)}, u32[]{:S(2)}) collective-permute-start(bf16[2,2,2,2,32,768]{5,4,2,3,0,1:T(8,128)(2,1)S(1)} %copy.188), channel_id=1, source_target_pairs={{0,1},{1,0},{2,3},{3,2},{4,5},{5,4},{6,7},{7,6},{8,9},{9,8},{10,11... | collective-permute-start | bytes 2359304 | tf_op jit(solution)/shard_map/ppermute | solution.py:288
  529.6 35.1 %collective-permute-start.43 = (bf16[2,2,2,32,768]{4,3,2,0,1:T(8,128)(2,1)}, bf16[2,2,2,32,768]{4,3,2,0,1:T(8,128)(2,1)}, u32[]{:S(2)}, u32[]{:S(2)}) collective-permute-start(bf16[2,2,2,32,768]{4,3,2,0,1:T(8,128)(2,1)} %get-tuple-element.315), channel_id=1, source_target_pairs={{0,4},{1,5},{2,6},{3,7},{4,0},{5,1},{6,2},{7,3},{8,12},{9,13},{10,... | collective-permute-start | bytes 1179656 | tf_op jit(solution)/shard_map/ppermute | solution.py:288
  530.2 33.4 %collective-permute-start.41 = (bf16[2,32,1024]{2,1,0:T(8,128)(2,1)}, bf16[2,32,1024]{2,1,0:T(8,128)(2,1)S(1)}, u32[]{:S(2)}, u32[]{:S(2)}) collective-permute-start(bf16[2,32,1024]{2,1,0:T(8,128)(2,1)} %get-tuple-element.311), channel_id=1, source_target_pairs={{0,2},{1,3},{2,0},{3,1},{4,6},{5,7},{6,4},{7,5},{8,10},{9,11},{10,... | collective-permute-start | bytes 393224 | tf_op jit(solution)/shard_map/ppermute | solution.py:288
  567.5 18.9 %collective-permute-start.49 = (bf16[2,2,2,2,32,768]{5,4,0,1,2,3:T(8,128)(2,1)S(1)}, bf16[2,2,2,2,32,768]{5,4,0,1,2,3:T(8,128)(2,1)S(1)}, u32[]{:S(2)}, u32[]{:S(2)}) collective-permute-start(bf16[2,2,2,2,32,768]{5,4,0,1,2,3:T(8,128)(2,1)S(1)} %copy.201), channel_id=1, source_target_pairs={{0,1},{1,0},{2,3},{3,2},{4,5},{5,4},{6,7},{7,6},{8,9},{9,8},{10,11... | collective-permute-start | bytes 2359304 | tf_op jit(solution)/shard_map/ppermute | solution.py:288
  568.9 17.4 %collective-permute-start.48 = (bf16[2,2,2,32,768]{4,3,1,2,0:T(8,128)(2,1)S(1)}, bf16[2,2,2,32,768]{4,3,1,2,0:T(8,128)(2,1)S(1)}, u32[]{:S(2)}, u32[]{:S(2)}) collective-permute-start(bf16[2,2,2,32,768]{4,3,1,2,0:T(8,128)(2,1)S(1)} %get-tuple-element.348), channel_id=1, source_target_pairs={{0,8},{1,9},{2,10},{3,11},{4,12},{5,13},{6,14},{7,15},{8,0},{9,1},... | collective-permute-start | bytes 1179656 | tf_op jit(solution)/shard_map/ppermute | solution.py:288
  586.7 18.9 %collective-permute-start.55 = (f32[2,2,2,1,384]{4,1,0,3,2:T(2,128)S(1)}, f32[2,2,2,1,384]{4,1,0,3,2:T(2,128)S(1)}, u32[]{:S(2)}, u32[]{:S(2)}) collective-permute-start(f32[2,2,2,1,384]{4,1,0,3,2:T(2,128)S(1)} %copy.204), channel_id=1, source_target_pairs={{0,2},{1,3},{2,0},{3,1},{4,6},{5,7},{6,4},{7,5},{8,10},{9,11},{10,... | collective-permute-start | bytes 36872 | tf_op jit(solution)/shard_map/ppermute | solution.py:288
  601.3 17.6 %collective-permute-start.54 = (bf16[2,2,2,32,768]{4,3,0,1,2:T(8,128)(2,1)S(1)}, bf16[2,2,2,32,768]{4,3,0,1,2:T(8,128)(2,1)S(1)}, u32[]{:S(2)}, u32[]{:S(2)}) collective-permute-start(bf16[2,2,2,32,768]{4,3,0,1,2:T(8,128)(2,1)S(1)} %get-tuple-element.360), channel_id=1, source_target_pairs={{0,2},{1,3},{2,0},{3,1},{4,6},{5,7},{6,4},{7,5},{8,10},{9,11},{10,... | collective-permute-start | bytes 1179656 | tf_op jit(solution)/shard_map/ppermute | solution.py:288
  (76 other events, 824.8 us)
Sparse Core Ops, SparseCore 0:
  52.3 88.5 all-gather.2
  143.8 75.6 all-gather.4

commit v2 on v1

--- a/solution.py
+++ b/solution.py
@@ -72,16 +72,15 @@
             top = jnp.max(scores, axis=0, keepdims=True)
             weights = jnp.exp(scores - top)
             total = jnp.sum(weights, axis=0, keepdims=True)
-            probs = (weights * (1.0 / total)).astype(BF)
             rows = slice(head * HEAD_DIM, (head + 1) * HEAD_DIM)
-            out_t[rows, at] = matmul(values_t[rows, :], probs)
+            out_t[rows, at] = matmul(values_t[rows, :], weights.astype(BF)) * (1.0 / total)
             lse_ref[0, head : head + 1, at] = top + jnp.log(total)
     o_ref[...] = out_t[...].T.astype(BF)
 
 
 def backward_kernel(
     seg_col, seg_row, q_ref, k_ref, v_ref, do_ref, lse_ref,
-    dq_ref, dk_ref, dv_ref, bq_ref, bv_ref, bias, dq_t, dk_sum, dv_sum,
+    grads_ref, bq_ref, bv_ref, bias, dq_t, dk_sum, dv_sum,
 ):
     fill_bias(seg_col, seg_row, bias)
     keys = k_ref[...]
@@ -112,9 +111,9 @@
                 dv_sum[...] += dv_part
     dq = (dq_t[...].T * SCALE).astype(BF)
     dv = dv_sum[...].astype(BF)
-    dq_ref[...] = dq
-    dk_ref[...] = (dk_sum[...] * SCALE).astype(BF)
-    dv_ref[...] = dv
+    grads_ref[0] = dq
+    grads_ref[1] = (dk_sum[...] * SCALE).astype(BF)
+    grads_ref[2] = dv
     bq_ref[...] = jnp.sum(dq.astype(F32), axis=0, keepdims=True)
     bv_ref[...] = jnp.sum(dv.astype(F32), axis=0, keepdims=True)
 
@@ -163,8 +162,8 @@
         in_specs=segment_specs(tokens)
         + [columns(tokens, part * pairs + first) for part in range(3)]
         + [columns(tokens, first), pl.BlockSpec((1, 2, tokens), lambda i: (first + i, 0, 0))],
-        out_specs=[columns(tokens, 0)] * 3 + [row] * 2,
-        out_shape=[jax.ShapeDtypeStruct((tokens, count * PAIR), BF)] * 3
+        out_specs=[pl.BlockSpec((3, tokens, PAIR), lambda i: (0, 0, i))] + [row] * 2,
+        out_shape=[jax.ShapeDtypeStruct((3, tokens, count * PAIR), BF)]
         + [jax.ShapeDtypeStruct((1, count * PAIR), F32)] * 2,
         scratch_shapes=[
             pltpu.VMEM((tokens, tokens), F32),
@@ -224,60 +223,63 @@
         out_shape=[jax.ShapeDtypeStruct((tokens, hidden), BF), jax.ShapeDtypeStruct((1, hidden), F32)], compiler_params=PARAMS)(dz, weight, slope)
 
 
-def weight_kernel(own_ref, rows_t_ref, q_ref, k_ref, v_ref, keep_ref, send_ref):
-    rows_t = rows_t_ref[...]
-    share = keep_ref.shape[1]
-    step = q_ref.shape[1]
-    for part, ref in enumerate((q_ref, k_ref, v_ref)):
-        grad = matmul(rows_t, ref[...]).astype(BF).reshape(-1, 2, share, step)
-        at = slice(part * step, (part + 1) * step)
-
-        @pl.when(own_ref[0] == 0)
-        def _():
-            keep_ref[:, :, at] = grad[:, 0]
-            send_ref[:, :, at] = grad[:, 1]
-
-        @pl.when(own_ref[0] == 1)
-        def _():
-            keep_ref[:, :, at] = grad[:, 1]
-            send_ref[:, :, at] = grad[:, 0]
+def weight_kernel(own_ref, rows_t_ref, part_ref, keep_ref, send_ref):
+    share, step = keep_ref.shape[1:]
+    grad = matmul(rows_t_ref[...], part_ref[0]).astype(BF).reshape(-1, 2, share, step)
+
+    @pl.when(own_ref[0] == 0)
+    def _():
+        keep_ref[...] = grad[:, 0]
+        send_ref[...] = grad[:, 1]
+
+    @pl.when(own_ref[0] == 1)
+    def _():
+        keep_ref[...] = grad[:, 1]
+        send_ref[...] = grad[:, 0]
 
 
 def weight_halves(rows_t, parts, devices):
-    width, step = rows_t.shape[0], parts[0].shape[1]
+    (width, tokens), step = rows_t.shape, parts.shape[2]
     own = (lax.axis_index(AXES) & 1).astype(jnp.int32).reshape(1)
-    half = jax.ShapeDtypeStruct((devices // 2, width // devices, 3 * step), BF)
+    half = (devices // 2, width // devices)
+    spec = pl.BlockSpec(half + (step,), lambda i: (0, 0, i))
     return pl.pallas_call(
         weight_kernel,
+        grid=(3,),
         name="weight_halves",
-        in_specs=[pl.BlockSpec(memory_space=pltpu.SMEM)] + [pl.BlockSpec(memory_space=pltpu.VMEM)] * 4,
-        out_specs=[pl.BlockSpec(memory_space=pltpu.VMEM)] * 2,
-        out_shape=[half, half],
-        compiler_params=pltpu.CompilerParams(vmem_limit_bytes=56 * 2**20),
-    )(own, rows_t, *parts)
+        in_specs=[
+            pl.BlockSpec(memory_space=pltpu.SMEM),
+            pl.BlockSpec((width, tokens), lambda i: (0, 0)),
+            pl.BlockSpec((1, tokens, step), lambda i: (i, 0, 0)),
+        ],
+        out_specs=[spec, spec],
+        out_shape=[jax.ShapeDtypeStruct(half + (3 * step,), BF)] * 2,
+        compiler_params=PARAMS,
+    )(own, rows_t, parts)
 
 
 def input_kernel(*refs):
     base_ref, weight_ref, pieces, out_ref = refs[0], refs[1], refs[2:-1], refs[-1]
     width = base_ref.shape[1]
-    step = pieces[0].shape[1]
+    step = pieces[0].shape[2]
     total = base_ref[...]
     for i, ref in enumerate(pieces):
-        first = PAIR + (i % 3) * width + (i // 3) * step
-        total += contract_cols(ref[...], weight_ref[:, first : first + step])
+        for part in range(3):
+            first = PAIR + part * width + i * step
+            total += contract_cols(ref[part], weight_ref[:, first : first + step])
     out_ref[...] = total.astype(BF)
 
 
 def input_call(base, head, pieces):
     tokens, width = base.shape
-    step = pieces[0].shape[1]
+    step = pieces[0].shape[2]
     row = pl.BlockSpec((TILE, width), lambda i: (i, 0))
     return pl.pallas_call(
         input_kernel,
         grid=(tokens // TILE,),
         name="input_grad",
         in_specs=[row, pl.BlockSpec(head.shape, lambda i: (0, 0))]
-        + [pl.BlockSpec((TILE, step), lambda i: (i, 0))] * len(pieces),
+        + [pl.BlockSpec((3, TILE, step), lambda i: (0, i, 0))] * len(pieces),
         out_specs=row,
         out_shape=jax.ShapeDtypeStruct((tokens, width), BF),
         compiler_params=PARAMS,
@@ -442,10 +444,11 @@
     running += up
     grad_pre = tick(running, grad_pre)
     grad_first = grad_two + contract_cols(grad_pre, up_full)
-    grad_one, attn_gain_grad, attn_shift_grad = normalize_back(grad_first, normed_one, inverse_one, attn_gain)
+    grad_one, attn_gain_grad, attn_shift_grad = normalize_back(
+        grad_first, normed_one, inverse_one, attn_gain
+    )
     grad_attended = grad_one.astype(BF)
     out_bias_grad = jnp.sum(grad_attended.astype(F32), axis=0)
-    grad_attended = tick(running, grad_attended)
     out_product = contract_rows(context, grad_attended).astype(BF)
     out = chains_of(out_product, devices, parts=1, turn=2)
     grad_context = contract_cols(grad_attended, out_full).astype(BF)
@@ -459,17 +462,17 @@
             grad_context, piece = lax.optimization_barrier((grad_context, piece))
         pieces.append(piece)
         if own % 32 == 0:
-            pair = weight_halves(rows_t, piece[:3], devices)
+            pair = weight_halves(rows_t, piece[0], devices)
             order = bit_orders(devices.bit_length() - 1)[chunk % 3]
             grads = jax.ShapeDtypeStruct((width, pair[0].shape[2]), BF)
             shares.append([Chain(grads, order, devices, pair=pair)])
         else:
-            grads = jnp.concatenate([matmul(rows_t, part).astype(BF) for part in piece[:3]], axis=1)
+            grads = jnp.concatenate([matmul(rows_t, piece[0][part]).astype(BF) for part in range(3)], axis=1)
             shares.append(chains_of(grads, devices, parts=1, turn=chunk))
         running += shares[-1]
-    joined = {part: jnp.concatenate([piece[part] for piece in pieces], axis=1) for part in (3, 4)}
+    joined = [jnp.concatenate([piece[part] for piece in pieces], axis=1) for part in (1, 2)]
     vector_grads = [
-        joined[3][0], joined[4][0], out_bias_grad, attn_gain_grad, attn_shift_grad,
+        joined[0][0], joined[1][0], out_bias_grad, attn_gain_grad, attn_shift_grad,
         down_bias_grad, ffn_gain_grad, ffn_shift_grad,
     ]
     side_grad = jnp.concatenate(
@@ -478,7 +481,8 @@
     )
     side = chains_of(side_grad, devices, parts=1, kind=F32)
     running += side
-    pieces = tick(running, [part for piece in pieces for part in piece[:3]])
+    tick(running, ())
+    pieces = tick(running, [piece[0] for piece in pieces])
     total_input = input_call(grad_one, head, pieces)
     layer_input_gradient = total_input.reshape(tokens.shape)
     while not all(c.over for c in running):

time: 656 us -> 656 us (level)
  Pallas kernels: 211 us -> 198 us
  waiting for transfers between devices: 174 us -> 181 us
    all_gather x1, waiting for transfers between devices: 33.6 us -> 42.7 us  [local(): down_full = lax.all_gather(later[1], AXES, axis=0, tiled=True)]
    pallas_call x1, Pallas kernels: 59.5 us -> 50.4 us  [attend(): pl.pallas_call(forward_kernel, grid=(pairs,), name='attend', in_specs=seg...]
  transfers between devices with their start and end apart: 67 -> 67, of which waited for: 21 -> 20; matrix products, arithmetic and copies ran while one was open for 17% -> 14% of each run, Pallas kernels for 33% -> 30%
where the time goes in v2:
time: 656 us; the launch traced here: 649 us
  Pallas kernels  198 us (30%)
  waiting for transfers between devices  181 us (28%)
  matrix products  76.3 us (12%)
  other arithmetic  74 us (11%)
  starting transfers between devices  61.6 us (9%)
  local copies, waits for them, and re-layouts  42.5 us (6%)
  between operations  15.9 us (2%)
    ppermute x65, waiting for transfers between devices, swap(): lax.ppermute(value, AXES, [(i, i ^ 1 << bit) for i in range(devices)])  138 us
    pallas_call x4, Pallas kernels, attend_back(): pl.pallas_call(backward_kernel, grid=(count,), name='attend_back', in_spe...  77 us
    ppermute x65, starting transfers between devices, swap(): lax.ppermute(value, AXES, [(i, i ^ 1 << bit) for i in range(devices)])  61.5 us
    pallas_call x1, Pallas kernels, attend(): pl.pallas_call(forward_kernel, grid=(pairs,), name='attend', in_specs=seg...  50.4 us
    all_gather x1, waiting for transfers between devices, local(): down_full = lax.all_gather(later[1], AXES, axis=0, tiled=True)  42.7 us
    convert_element_type x36, other arithmetic, halve(): self.send = send.astype(self.kind)  31.7 us
    dot_general x3, matrix products, matmul(): return jnp.dot(left, right, preferred_element_type=F32)  28 us
    dot_general x2, matrix products, contract_cols(): lax.dot_general(left, right, (((1,), (1,)), ((), ())), preferred_element_...  24.7 us
  transfers between devices with their start and end apart: 67, of which 20 were waited for; matrix products, arithmetic and copies ran while one was open for 14% of the time, Pallas kernels for 30%

profile of v2, /device:TPU:0, one launch (start us, length us, event | category | flops | bytes accessed | tf_op | source)
XLA Modules:
  0.0 649.1 jit_solution(15885929309349636877)
XLA Ops:
  31.6 5.3 collective-permute-done.4
  39.7 8.2 %collective-permute-done.5 = bf16[2,2,32,1024]{3,2,1,0:T(8,128)(2,1)S(1)} collective-permute-done((bf16[2,2,32,1024]{3,2,1,0:T(8,128)(2,1)S(1)}, bf16[2,2,32,1024]{3,2,1,0:T(8,128)(2,1)S(1)}, u32[]{:S(2)}, u32[]{:S(2)}) %collective-permute-start.5) | collective-permute-done | bytes 262176 | tf_op jit(solution)/shard_map/ppermute | solution.py:290
  48.2 3.9 collective-permute-done.8
  56.5 5.7 collective-permute-done.11
  64.6 10.0 %collective-permute-done.13 = bf16[2,2,2,32,1152]{4,3,1,2,0:T(8,128)(2,1)S(1)} collective-permute-done((bf16[2,2,2,32,1152]{4,3,1,2,0:T(8,128)(2,1)S(1)}, bf16[2,2,2,32,1152]{4,3,1,2,0:T(8,128)(2,1)S(1)}, u32[]{:S(2)}, u32[]{:S(2)}) %collective-permute-start.13) | collective-permute-done | bytes 589856 | tf_op jit(solution)/shard_map/ppermute | solution.py:290
  88.8 8.5 %fusion.2.q_ref.k_ref.v_ref = bf16[1024,3072]{1,0:T(8,128)(2,1)} fusion(f32[3072]{0:T(1024)S(1)} %pad_maximum_fusion.11, bf16[1024,3200]{1,0:T(8,128)(2,1)S(1)} %pad_maximum_fusion.refs_1_, bf16[1,1024,1024]{2,1,0:T(8,128)(2,1)S(1)} %copy-done.16), kind=kOutput, calls=%fused_computation.6 | convolution fusion | flops 6448742400 | bytes 14692352 | tf_op jit(solution)/shard_map/dot_general | solution.py:25
  97.4 50.4 %attend.1 = (bf16[1024,1024]{1,0:T(8,128)(2,1)}, f32[8,2,1024]{2,1,0:T(2,128)}) custom-call(s32[1024,1]{1,0:T(8,128)} %copy.162.seg_col, s32[1,1024]{1,0:T(1,128)} %seg_row.9, bf16[1024,3072]{1,0:T(8,128)(2,1)} %fusion.2.q_ref.k_ref.v_ref, bf16[1024,3072]{1,0:T(8,128)(2,1)} %fusion.2.q_ref.k_ref.v_ref, bf16[1024,3072]{1,0:T(8,128)(2,1)} %fusion.2.q_ref.k_ref.v_ref), custom_call_target="tpu_custom_call" | custom-call | tf_op jit(solution)/shard_map/attend/pallas_call | solution.py:136
  147.8 4.7 fusion.93
  156.7 20.0 %feed.1 = (bf16[1024,4096]{1,0:T(8,128)(2,1)}, bf16[1024,4096]{1,0:T(8,128)(2,1)}) custom-call(bf16[1024,1024]{1,0:T(8,128)(2,1)} %fusion.16.x_ref, bf16[1024,5120]{1,0:T(8,128)(2,1)} %all-gather.3.cloned.1.call-done.w_ref, f32[1,4096]{1,0:T(1,128)} %reshape.1338.b_ref), custom_call_target="tpu_custom_call" | custom-call | tf_op jit(solution)/shard_map/feed/pallas_call | solution.py:208
  176.7 42.7 %all-gather.5.cloned.1.call-done.w_ref = bf16[4096,1024]{1,0:T(8,128)(2,1)} async-done(((bf16[128,1024]{1,0:T(8,128)(2,1)}), bf16[4096,1024]{1,0:T(8,128)(2,1)}) %all-gather.5.cloned.1.call-update) | async-done | bytes 8388624 | tf_op jit(solution)/shard_map/all_gather | solution.py:417
  219.4 14.8 %fusion.94 = (f32[1024]{0:T(1024)S(1)}, f32[1024,1024]{1,0:T(8,128)S(1)}) fusion(f32[1024]{0:T(1024)S(1)} %get-tuple-element.354, bf16[1024,4096]{1,0:T(8,128)(2,1)} %get-tuple-element.186, bf16[4096,1024]{1,0:T(8,128)(2,1)} %all-gather.5.cloned.1.call-done.w_ref, f32[1024]{0:T(1024)S(1)} %get-tuple-element.355, f32[1024]{0:T(1024)S(1)} %get-tuple-element.356, ...), kind=kOutput, calls=%fused_computation.305 | convolution fusion | flops 8597273600 | bytes 25190400 | tf_op jit(solution)/shard_map/dot_general | solution.py:25
  243.6 9.8 %convolution_convert_fusion.1 = bf16[4096,1024]{1,0:T(8,128)(2,1)S(1)} fusion(bf16[1024,4096]{1,0:T(8,128)(2,1)S(1)} %bitcast.437, bf16[1024,1024]{1,0:T(8,128)(2,1)S(1)} %get-tuple-element.188.dz_ref), kind=kOutput, calls=%fused_computation.4 | convolution fusion | flops 8594128896 | bytes 18874368 | tf_op jit(solution)/shard_map/dot_general | solution.py:29
  260.6 16.6 %feed_back.1 = (bf16[1024,4096]{1,0:T(8,128)(2,1)}, f32[1,4096]{1,0:T(1,128)}) custom-call(bf16[1024,1024]{1,0:T(8,128)(2,1)} %copy-done.9, bf16[4096,1024]{1,0:T(8,128)(2,1)} %all-gather.5.cloned.1.call-done.w_ref, bf16[1024,4096]{1,0:T(8,128)(2,1)} %get-tuple-element.189.slope_ref), custom_call_target="tpu_custom_call" | custom-call | tf_op jit(solution)/shard_map/feed_back/pallas_call | solution.py:220
  281.9 11.5 %convolution_convert_fusion = bf16[1024,4096]{1,0:T(8,128)(2,1)S(1)} fusion(bf16[1024,1024]{1,0:T(8,128)(2,1)S(1)} %copy-done.8, bf16[1024,4096]{1,0:T(8,128)(2,1)} %get-tuple-element.200), kind=kOutput, calls=%fused_computation.3 | convolution fusion | flops 8594128896 | bytes 18874368 | tf_op jit(solution)/shard_map/dot_general | solution.py:29
  304.1 15.8 %collective-permute-done.17 = bf16[2,2,2,128,512]{4,3,0,1,2:T(8,128)(2,1)S(1)} collective-permute-done((bf16[2,2,2,128,512]{4,3,0,1,2:T(8,128)(2,1)S(1)}, bf16[2,2,2,128,512]{4,3,0,1,2:T(8,128)(2,1)S(1)}, u32[]{:S(2)}, u32[]{:S(2)}) %collective-permute-start.17) | collective-permute-done | bytes 1048608 | tf_op jit(solution)/shard_map/ppermute | solution.py:290
  322.9 19.4 %multiply_reduce_fusion = (f32[1024]{0:T(1024)}, f32[1024]{0:T(1024)S(1)}, f32[1024]{0:T(1024)S(1)}, f32[1024]{0:T(1024)}, f32[1024,1024]{1,0:T(8,128)}) fusion(f32[1024,1024]{1,0:T(8,128)S(1)} %copy-done.1, f32[1024]{0:T(1024)S(1)} %add_rsqrt_fusion.1, f32[1024]{0:T(1024)S(1)} %broadcast_multiply_fusion.5, f32[1024]{0:T(1024)S(1)} %get-tuple-element.356, ...), kind=kOutput, calls=%fused_computation.21 | convolution fusion | flops 8608804864 | bytes 31506432 | tf_op jit(solution)/shard_map/dot_general | solution.py:33
  352.5 5.3 convolution_convert_fusion.3.do_ref
  357.7 7.8 %collective-permute-done.19 = bf16[2,2,128,512]{3,2,0,1:T(8,128)(2,1)S(1)} collective-permute-done((bf16[2,2,128,512]{3,2,0,1:T(8,128)(2,1)S(1)}, bf16[2,2,128,512]{3,2,0,1:T(8,128)(2,1)S(1)}, u32[]{:S(2)}, u32[]{:S(2)}) %collective-permute-start.19) | collective-permute-done | bytes 524320 | tf_op jit(solution)/shard_map/ppermute | solution.py:290
  375.1 3.9 copy.175.rows_t_ref
  379.0 19.4 %attend_back.4 = (bf16[3,1024,256]{2,1,0:T(8,128)(2,1)}, f32[1,256]{1,0:T(1,128)}, f32[1,256]{1,0:T(1,128)}) custom-call(s32[1024,1]{1,0:T(8,128)} %copy.162.seg_col, s32[1,1024]{1,0:T(1,128)} %seg_row.9, bf16[1024,3072]{1,0:T(8,128)(2,1)} %fusion.2.q_ref.k_ref.v_ref, bf16[1024,3072]{1,0:T(8,128)(2,1)} %fusion.2.q_ref.k_ref.v_ref, ...), custom_call_target="tpu_custom_call" | custom-call | tf_op jit(solution)/shard_map/attend_back/pallas_call | solution.py:158
  398.5 5.4 weight_halves.4
  418.4 19.2 %attend_back.5 = (bf16[3,1024,256]{2,1,0:T(8,128)(2,1)}, f32[1,256]{1,0:T(1,128)}, f32[1,256]{1,0:T(1,128)}) custom-call(s32[1024,1]{1,0:T(8,128)} %copy.162.seg_col, s32[1,1024]{1,0:T(1,128)} %seg_row.9, bf16[1024,3072]{1,0:T(8,128)(2,1)} %fusion.2.q_ref.k_ref.v_ref, bf16[1024,3072]{1,0:T(8,128)(2,1)} %fusion.2.q_ref.k_ref.v_ref, ...), custom_call_target="tpu_custom_call" | custom-call | tf_op jit(solution)/shard_map/attend_back/pallas_call | solution.py:158
  437.5 5.4 weight_halves.5
  446.4 28.8 %collective-permute-done.28 = bf16[128,512]{1,0:T(8,128)(2,1)S(1)} collective-permute-done((bf16[128,512]{1,0:T(8,128)(2,1)S(1)}, bf16[128,512]{1,0:T(8,128)(2,1)S(1)}, u32[]{:S(2)}, u32[]{:S(2)}) %collective-permute-start.28) | collective-permute-done | bytes 131104 | tf_op jit(solution)/shard_map/ppermute | solution.py:290
  479.3 19.2 %attend_back.6 = (bf16[3,1024,256]{2,1,0:T(8,128)(2,1)}, f32[1,256]{1,0:T(1,128)}, f32[1,256]{1,0:T(1,128)}) custom-call(s32[1024,1]{1,0:T(8,128)} %copy.162.seg_col, s32[1,1024]{1,0:T(1,128)} %seg_row.9, bf16[1024,3072]{1,0:T(8,128)(2,1)} %fusion.2.q_ref.k_ref.v_ref, bf16[1024,3072]{1,0:T(8,128)(2,1)} %fusion.2.q_ref.k_ref.v_ref, ...), custom_call_target="tpu_custom_call" | custom-call | tf_op jit(solution)/shard_map/attend_back/pallas_call | solution.py:158
  498.5 5.5 weight_halves.6
  507.4 13.3 %collective-permute-done.34 = bf16[2,32,2048]{2,1,0:T(8,128)(2,1)S(1)} collective-permute-done((bf16[2,32,2048]{2,1,0:T(8,128)(2,1)S(1)}, bf16[2,32,2048]{2,1,0:T(8,128)(2,1)S(1)}, u32[]{:S(2)}, u32[]{:S(2)}) %collective-permute-start.34) | collective-permute-done | bytes 262176 | tf_op jit(solution)/shard_map/ppermute | solution.py:290
  527.5 19.2 %attend_back.7 = (bf16[3,1024,256]{2,1,0:T(8,128)(2,1)}, f32[1,256]{1,0:T(1,128)}, f32[1,256]{1,0:T(1,128)}) custom-call(s32[1024,1]{1,0:T(8,128)} %copy.162.seg_col, s32[1,1024]{1,0:T(1,128)} %seg_row.9, bf16[1024,3072]{1,0:T(8,128)(2,1)} %fusion.2.q_ref.k_ref.v_ref, bf16[1024,3072]{1,0:T(8,128)(2,1)} %fusion.2.q_ref.k_ref.v_ref, ...), custom_call_target="tpu_custom_call" | custom-call | tf_op jit(solution)/shard_map/attend_back/pallas_call | solution.py:158
  550.5 5.4 weight_halves.7
  562.0 12.6 %collective-permute-done.39 = bf16[32,2048]{1,0:T(8,128)(2,1)S(1)} collective-permute-done((bf16[32,2048]{1,0:T(8,128)(2,1)}, bf16[32,2048]{1,0:T(8,128)(2,1)S(1)}, u32[]{:S(2)}, u32[]{:S(2)}) %collective-permute-start.39) | collective-permute-done | bytes 131104 | tf_op jit(solution)/shard_map/ppermute | solution.py:290
  588.9 9.0 %collective-permute-done.46 = bf16[2,32,768]{2,1,0:T(8,128)(2,1)S(1)} collective-permute-done((bf16[2,32,768]{2,1,0:T(8,128)(2,1)S(1)}, bf16[2,32,768]{2,1,0:T(8,128)(2,1)S(1)}, u32[]{:S(2)}, u32[]{:S(2)}) %collective-permute-start.46) | collective-permute-done | bytes 98336 | tf_op jit(solution)/shard_map/ppermute | solution.py:290
  606.1 12.2 %input_grad.1 = bf16[1024,1024]{1,0:T(8,128)(2,1)} custom-call(f32[1024,1024]{1,0:T(8,128)} %copy-done.6, bf16[1024,3200]{1,0:T(8,128)(2,1)} %copy-done.3, bf16[3,1024,256]{2,1,0:T(8,128)(2,1)} %get-tuple-element.303.part_ref.refs_2_, bf16[3,1024,256]{2,1,0:T(8,128)(2,1)} %get-tuple-element.304.part_ref.refs_3_, ...), custom_call_target="tpu_custom_call" | custom-call | tf_op jit(solution)/shard_map/input_grad/pallas_call | solution.py:277
  (408 shorter events, 194.4 us)
Async XLA Ops:
  7.2 140.6 %all-gather.3.cloned.1.call-start = ((), (), s32[]{:S(2)}) async-start(), calls=%async_computation | async-start | bytes 10813440 | tf_op jit(solution)/shard_map/all_gather | solution.py:416
  52.2 167.2 %all-gather.5.cloned.1.call-start = ((), (), s32[]{:S(2)}) async-start(), calls=%async_computation.1 | async-start | bytes 8650752 | tf_op jit(solution)/shard_map/all_gather | solution.py:417
  56.1 18.4 %collective-permute-start.13 = (bf16[2,2,2,32,1152]{4,3,1,2,0:T(8,128)(2,1)S(1)}, bf16[2,2,2,32,1152]{4,3,1,2,0:T(8,128)(2,1)S(1)}, u32[]{:S(2)}, u32[]{:S(2)}) collective-permute-start(bf16[2,2,2,32,1152]{4,3,1,2,0:T(8,128)(2,1)S(1)} %maximum_select_fusion.8), channel_id=1, source_target_pairs={{0,8},{1,9},{2,10},{3,11},{4,12},{5,13},{6,14},{7,15},{8,0},{9,1},... | collective-permute-start | bytes 1769480 | tf_op jit(solution)/shard_map/ppermute | solution.py:290
  260.1 17.1 %collective-permute-start.16 = (bf16[2,2,2,2,128,512]{5,4,3,0,1,2:T(8,128)(2,1)}, bf16[2,2,2,2,128,512]{5,4,3,0,1,2:T(8,128)(2,1)}, u32[]{:S(2)}, u32[]{:S(2)}) collective-permute-start(bf16[2,2,2,2,128,512]{5,4,3,0,1,2:T(8,128)(2,1)} %bitcast.358), channel_id=1, source_target_pairs={{0,1},{1,0},{2,3},{3,2},{4,5},{5,4},{6,7},{7,6},{8,9},{9,8},{10,11... | collective-permute-start | bytes 6291464 | tf_op jit(solution)/shard_map/ppermute | solution.py:290
  260.4 19.2 %collective-permute-start.15 = (bf16[2,2,2,2,128,512]{5,4,0,1,2,3:T(8,128)(2,1)}, bf16[2,2,2,2,128,512]{5,4,0,1,2,3:T(8,128)(2,1)}, u32[]{:S(2)}, u32[]{:S(2)}) collective-permute-start(bf16[2,2,2,2,128,512]{5,4,0,1,2,3:T(8,128)(2,1)} %bitcast.360), channel_id=1, source_target_pairs={{0,1},{1,0},{2,3},{3,2},{4,5},{5,4},{6,7},{7,6},{8,9},{9,8},{10,11... | collective-permute-start | bytes 6291464 | tf_op jit(solution)/shard_map/ppermute | solution.py:290
  293.4 28.1 %collective-permute-start.18 = (bf16[2,2,2,128,512]{4,3,2,0,1:T(8,128)(2,1)S(1)}, bf16[2,2,2,128,512]{4,3,2,0,1:T(8,128)(2,1)S(1)}, u32[]{:S(2)}, u32[]{:S(2)}) collective-permute-start(bf16[2,2,2,128,512]{4,3,2,0,1:T(8,128)(2,1)S(1)} %get-tuple-element.199), channel_id=1, source_target_pairs={{0,4},{1,5},{2,6},{3,7},{4,0},{5,1},{6,2},{7,3},{8,12},{9,13},{10,... | collective-permute-start | bytes 3145736 | tf_op jit(solution)/shard_map/ppermute | solution.py:290
  294.9 25.0 %collective-permute-start.17 = (bf16[2,2,2,128,512]{4,3,0,1,2:T(8,128)(2,1)S(1)}, bf16[2,2,2,128,512]{4,3,0,1,2:T(8,128)(2,1)S(1)}, u32[]{:S(2)}, u32[]{:S(2)}) collective-permute-start(bf16[2,2,2,128,512]{4,3,0,1,2:T(8,128)(2,1)S(1)} %get-tuple-element.197), channel_id=1, source_target_pairs={{0,2},{1,3},{2,0},{3,1},{4,6},{5,7},{6,4},{7,5},{8,10},{9,11},{10,... | collective-permute-start | bytes 3145736 | tf_op jit(solution)/shard_map/ppermute | solution.py:290
  342.3 25.2 %collective-permute-start.22 = (bf16[2,2,2,2,32,2048]{5,4,0,1,2,3:T(8,128)(2,1)}, bf16[2,2,2,2,32,2048]{5,4,0,1,2,3:T(8,128)(2,1)S(1)}, u32[]{:S(2)}, u32[]{:S(2)}) collective-permute-start(bf16[2,2,2,2,32,2048]{5,4,0,1,2,3:T(8,128)(2,1)} %bitcast.392), channel_id=1, source_target_pairs={{0,1},{1,0},{2,3},{3,2},{4,5},{5,4},{6,7},{7,6},{8,9},{9,8},{10,11... | collective-permute-start | bytes 6291464 | tf_op jit(solution)/shard_map/ppermute | solution.py:290
  342.3 26.9 %collective-permute-start.21 = (bf16[2,2,2,2,32,2048]{5,4,2,3,0,1:T(8,128)(2,1)}, bf16[2,2,2,2,32,2048]{5,4,2,3,0,1:T(8,128)(2,1)S(1)}, u32[]{:S(2)}, u32[]{:S(2)}) collective-permute-start(bf16[2,2,2,2,32,2048]{5,4,2,3,0,1:T(8,128)(2,1)} %bitcast.393), channel_id=1, source_target_pairs={{0,1},{1,0},{2,3},{3,2},{4,5},{5,4},{6,7},{7,6},{8,9},{9,8},{10,11... | collective-permute-start | bytes 6291464 | tf_op jit(solution)/shard_map/ppermute | solution.py:290
  371.5 39.1 %collective-permute-start.27 = (bf16[2,2,2,2,32,1024]{5,4,2,3,0,1:T(8,128)(2,1)}, bf16[2,2,2,2,32,1024]{5,4,2,3,0,1:T(8,128)(2,1)}, u32[]{:S(2)}, u32[]{:S(2)}) collective-permute-start(bf16[2,2,2,2,32,1024]{5,4,2,3,0,1:T(8,128)(2,1)} %bitcast.362), channel_id=1, source_target_pairs={{0,1},{1,0},{2,3},{3,2},{4,5},{5,4},{6,7},{7,6},{8,9},{9,8},{10,11... | collective-permute-start | bytes 3145736 | tf_op jit(solution)/shard_map/ppermute | solution.py:290
  371.5 41.6 %collective-permute-start.26 = (bf16[2,2,2,32,2048]{4,3,0,1,2:T(8,128)(2,1)}, bf16[2,2,2,32,2048]{4,3,0,1,2:T(8,128)(2,1)}, u32[]{:S(2)}, u32[]{:S(2)}) collective-permute-start(bf16[2,2,2,32,2048]{4,3,0,1,2:T(8,128)(2,1)} %get-tuple-element.223), channel_id=1, source_target_pairs={{0,2},{1,3},{2,0},{3,1},{4,6},{5,7},{6,4},{7,5},{8,10},{9,11},{10,... | collective-permute-start | bytes 3145736 | tf_op jit(solution)/shard_map/ppermute | solution.py:290
  372.1 42.6 %collective-permute-start.25 = (bf16[2,2,2,32,2048]{4,3,1,2,0:T(8,128)(2,1)}, bf16[2,2,2,32,2048]{4,3,1,2,0:T(8,128)(2,1)}, u32[]{:S(2)}, u32[]{:S(2)}) collective-permute-start(bf16[2,2,2,32,2048]{4,3,1,2,0:T(8,128)(2,1)} %get-tuple-element.221), channel_id=1, source_target_pairs={{0,8},{1,9},{2,10},{3,11},{4,12},{5,13},{6,14},{7,15},{8,0},{9,1},... | collective-permute-start | bytes 3145736 | tf_op jit(solution)/shard_map/ppermute | solution.py:290
  372.6 31.3 %collective-permute-start.24 = (bf16[2,128,512]{2,1,0:T(8,128)(2,1)}, bf16[2,128,512]{2,1,0:T(8,128)(2,1)}, u32[]{:S(2)}, u32[]{:S(2)}) collective-permute-start(bf16[2,128,512]{2,1,0:T(8,128)(2,1)} %get-tuple-element.219), channel_id=1, source_target_pairs={{0,16},{1,17},{2,18},{3,19},{4,20},{5,21},{6,22},{7,23},{8,24},{9,... | collective-permute-start | bytes 786440 | tf_op jit(solution)/shard_map/ppermute | solution.py:290
  374.5 34.4 %collective-permute-start.23 = (bf16[2,128,512]{2,1,0:T(8,128)(2,1)S(1)}, bf16[2,128,512]{2,1,0:T(8,128)(2,1)}, u32[]{:S(2)}, u32[]{:S(2)}) collective-permute-start(bf16[2,128,512]{2,1,0:T(8,128)(2,1)S(1)} %get-tuple-element.217), channel_id=1, source_target_pairs={{0,8},{1,9},{2,10},{3,11},{4,12},{5,13},{6,14},{7,15},{8,0},{9,1},... | collective-permute-start | bytes 786440 | tf_op jit(solution)/shard_map/ppermute | solution.py:290
  416.2 29.2 %collective-permute-start.29 = (bf16[128,512]{1,0:T(8,128)(2,1)}, bf16[128,512]{1,0:T(8,128)(2,1)S(1)}, u32[]{:S(2)}, u32[]{:S(2)}) collective-permute-start(bf16[128,512]{1,0:T(8,128)(2,1)} %get-tuple-element.237), channel_id=1, source_target_pairs={{0,2},{1,3},{2,0},{3,1},{4,6},{5,7},{6,4},{7,5},{8,10},{9,11},{10,... | collective-permute-start | bytes 393224 | tf_op jit(solution)/shard_map/ppermute | solution.py:290
  417.7 57.5 %collective-permute-start.32 = (bf16[2,2,2,32,1024]{4,3,1,2,0:T(8,128)(2,1)}, bf16[2,2,2,32,1024]{4,3,1,2,0:T(8,128)(2,1)S(1)}, u32[]{:S(2)}, u32[]{:S(2)}) collective-permute-start(bf16[2,2,2,32,1024]{4,3,1,2,0:T(8,128)(2,1)} %get-tuple-element.243), channel_id=1, source_target_pairs={{0,8},{1,9},{2,10},{3,11},{4,12},{5,13},{6,14},{7,15},{8,0},{9,1},... | collective-permute-start | bytes 1572872 | tf_op jit(solution)/shard_map/ppermute | solution.py:290
  418.3 58.0 %collective-permute-start.33 = (bf16[2,2,2,2,32,768]{5,4,0,1,2,3:T(8,128)(2,1)S(1)}, bf16[2,2,2,2,32,768]{5,4,0,1,2,3:T(8,128)(2,1)S(1)}, u32[]{:S(2)}, u32[]{:S(2)}) collective-permute-start(bf16[2,2,2,2,32,768]{5,4,0,1,2,3:T(8,128)(2,1)S(1)} %copy.178), channel_id=1, source_target_pairs={{0,1},{1,0},{2,3},{3,2},{4,5},{5,4},{6,7},{7,6},{8,9},{9,8},{10,11... | collective-permute-start | bytes 2359304 | tf_op jit(solution)/shard_map/ppermute | solution.py:290
  442.9 33.2 %collective-permute-start.31 = (bf16[2,2,32,2048]{3,2,0,1:T(8,128)(2,1)S(1)}, bf16[2,2,32,2048]{3,2,0,1:T(8,128)(2,1)S(1)}, u32[]{:S(2)}, u32[]{:S(2)}) collective-permute-start(bf16[2,2,32,2048]{3,2,0,1:T(8,128)(2,1)S(1)} %get-tuple-element.241), channel_id=1, source_target_pairs={{0,4},{1,5},{2,6},{3,7},{4,0},{5,1},{6,2},{7,3},{8,12},{9,13},{10,... | collective-permute-start | bytes 1572872 | tf_op jit(solution)/shard_map/ppermute | solution.py:290
  443.4 32.8 %collective-permute-start.30 = (bf16[2,2,32,2048]{3,2,0,1:T(8,128)(2,1)S(1)}, bf16[2,2,32,2048]{3,2,0,1:T(8,128)(2,1)S(1)}, u32[]{:S(2)}, u32[]{:S(2)}) collective-permute-start(bf16[2,2,32,2048]{3,2,0,1:T(8,128)(2,1)S(1)} %get-tuple-element.239), channel_id=1, source_target_pairs={{0,16},{1,17},{2,18},{3,19},{4,20},{5,21},{6,22},{7,23},{8,24},{9,... | collective-permute-start | bytes 1572872 | tf_op jit(solution)/shard_map/ppermute | solution.py:290
  445.4 29.8 %collective-permute-start.28 = (bf16[128,512]{1,0:T(8,128)(2,1)S(1)}, bf16[128,512]{1,0:T(8,128)(2,1)S(1)}, u32[]{:S(2)}, u32[]{:S(2)}) collective-permute-start(bf16[128,512]{1,0:T(8,128)(2,1)S(1)} %copy-done.31), channel_id=1, source_target_pairs={{0,16},{1,17},{2,18},{3,19},{4,20},{5,21},{6,22},{7,23},{8,24},{9,... | collective-permute-start | bytes 393224 | tf_op jit(solution)/shard_map/ppermute | solution.py:290
  476.5 29.5 %collective-permute-start.35 = (bf16[2,32,2048]{2,1,0:T(8,128)(2,1)S(1)}, bf16[2,32,2048]{2,1,0:T(8,128)(2,1)S(1)}, u32[]{:S(2)}, u32[]{:S(2)}) collective-permute-start(bf16[2,32,2048]{2,1,0:T(8,128)(2,1)S(1)} %get-tuple-element.257), channel_id=1, source_target_pairs={{0,8},{1,9},{2,10},{3,11},{4,12},{5,13},{6,14},{7,15},{8,0},{9,1},... | collective-permute-start | bytes 786440 | tf_op jit(solution)/shard_map/ppermute | solution.py:290
  477.3 44.2 %collective-permute-start.38 = (bf16[2,2,2,2,32,768]{5,4,3,0,1,2:T(8,128)(2,1)S(1)}, bf16[2,2,2,2,32,768]{5,4,3,0,1,2:T(8,128)(2,1)S(1)}, u32[]{:S(2)}, u32[]{:S(2)}) collective-permute-start(bf16[2,2,2,2,32,768]{5,4,3,0,1,2:T(8,128)(2,1)S(1)} %copy.183), channel_id=1, source_target_pairs={{0,1},{1,0},{2,3},{3,2},{4,5},{5,4},{6,7},{7,6},{8,9},{9,8},{10,11... | collective-permute-start | bytes 2359304 | tf_op jit(solution)/shard_map/ppermute | solution.py:290
  477.4 29.3 %collective-permute-start.36 = (bf16[2,2,32,1024]{3,2,0,1:T(8,128)(2,1)}, bf16[2,2,32,1024]{3,2,0,1:T(8,128)(2,1)S(1)}, u32[]{:S(2)}, u32[]{:S(2)}) collective-permute-start(bf16[2,2,32,1024]{3,2,0,1:T(8,128)(2,1)} %get-tuple-element.259), channel_id=1, source_target_pairs={{0,16},{1,17},{2,18},{3,19},{4,20},{5,21},{6,22},{7,23},{8,24},{9,... | collective-permute-start | bytes 786440 | tf_op jit(solution)/shard_map/ppermute | solution.py:290
  504.0 17.5 %collective-permute-start.37 = (bf16[2,2,2,32,768]{4,3,0,1,2:T(8,128)(2,1)S(1)}, bf16[2,2,2,32,768]{4,3,0,1,2:T(8,128)(2,1)S(1)}, u32[]{:S(2)}, u32[]{:S(2)}) collective-permute-start(bf16[2,2,2,32,768]{4,3,0,1,2:T(8,128)(2,1)S(1)} %get-tuple-element.261), channel_id=1, source_target_pairs={{0,2},{1,3},{2,0},{3,1},{4,6},{5,7},{6,4},{7,5},{8,10},{9,11},{10,... | collective-permute-start | bytes 1179656 | tf_op jit(solution)/shard_map/ppermute | solution.py:290
  522.5 37.9 %collective-permute-start.40 = (bf16[32,2048]{1,0:T(8,128)(2,1)}, bf16[32,2048]{1,0:T(8,128)(2,1)}, u32[]{:S(2)}, u32[]{:S(2)}) collective-permute-start(bf16[32,2048]{1,0:T(8,128)(2,1)} %get-tuple-element.271), channel_id=1, source_target_pairs={{0,16},{1,17},{2,18},{3,19},{4,20},{5,21},{6,22},{7,23},{8,24},{9,... | collective-permute-start | bytes 393224 | tf_op jit(solution)/shard_map/ppermute | solution.py:290
  550.5 27.2 %collective-permute-start.44 = (bf16[2,2,2,2,32,768]{5,4,2,3,0,1:T(8,128)(2,1)}, bf16[2,2,2,2,32,768]{5,4,2,3,0,1:T(8,128)(2,1)}, u32[]{:S(2)}, u32[]{:S(2)}) collective-permute-start(bf16[2,2,2,2,32,768]{5,4,2,3,0,1:T(8,128)(2,1)} %copy.188), channel_id=1, source_target_pairs={{0,1},{1,0},{2,3},{3,2},{4,5},{5,4},{6,7},{7,6},{8,9},{9,8},{10,11... | collective-permute-start | bytes 2359304 | tf_op jit(solution)/shard_map/ppermute | solution.py:290
  555.8 20.7 %collective-permute-start.43 = (bf16[2,2,2,32,768]{4,3,2,0,1:T(8,128)(2,1)}, bf16[2,2,2,32,768]{4,3,2,0,1:T(8,128)(2,1)}, u32[]{:S(2)}, u32[]{:S(2)}) collective-permute-start(bf16[2,2,2,32,768]{4,3,2,0,1:T(8,128)(2,1)} %get-tuple-element.277), channel_id=1, source_target_pairs={{0,4},{1,5},{2,6},{3,7},{4,0},{5,1},{6,2},{7,3},{8,12},{9,13},{10,... | collective-permute-start | bytes 1179656 | tf_op jit(solution)/shard_map/ppermute | solution.py:290
  557.3 18.2 %collective-permute-start.42 = (bf16[2,2,32,768]{3,2,0,1:T(8,128)(2,1)S(1)}, bf16[2,2,32,768]{3,2,0,1:T(8,128)(2,1)}, u32[]{:S(2)}, u32[]{:S(2)}) collective-permute-start(bf16[2,2,32,768]{3,2,0,1:T(8,128)(2,1)S(1)} %get-tuple-element.275), channel_id=1, source_target_pairs={{0,4},{1,5},{2,6},{3,7},{4,0},{5,1},{6,2},{7,3},{8,12},{9,13},{10,... | collective-permute-start | bytes 589832 | tf_op jit(solution)/shard_map/ppermute | solution.py:290
  579.2 18.9 %collective-permute-start.49 = (bf16[2,2,2,2,32,768]{5,4,0,1,2,3:T(8,128)(2,1)S(1)}, bf16[2,2,2,2,32,768]{5,4,0,1,2,3:T(8,128)(2,1)S(1)}, u32[]{:S(2)}, u32[]{:S(2)}) collective-permute-start(bf16[2,2,2,2,32,768]{5,4,0,1,2,3:T(8,128)(2,1)S(1)} %copy.201), channel_id=1, source_target_pairs={{0,1},{1,0},{2,3},{3,2},{4,5},{5,4},{6,7},{7,6},{8,9},{9,8},{10,11... | collective-permute-start | bytes 2359304 | tf_op jit(solution)/shard_map/ppermute | solution.py:290
  580.6 17.4 %collective-permute-start.48 = (bf16[2,2,2,32,768]{4,3,1,2,0:T(8,128)(2,1)S(1)}, bf16[2,2,2,32,768]{4,3,1,2,0:T(8,128)(2,1)S(1)}, u32[]{:S(2)}, u32[]{:S(2)}) collective-permute-start(bf16[2,2,2,32,768]{4,3,1,2,0:T(8,128)(2,1)S(1)} %get-tuple-element.298), channel_id=1, source_target_pairs={{0,8},{1,9},{2,10},{3,11},{4,12},{5,13},{6,14},{7,15},{8,0},{9,1},... | collective-permute-start | bytes 1179656 | tf_op jit(solution)/shard_map/ppermute | solution.py:290
  598.3 19.9 %collective-permute-start.55 = (f32[2,2,2,1,384]{4,1,0,3,2:T(2,128)S(1)}, f32[2,2,2,1,384]{4,1,0,3,2:T(2,128)S(1)}, u32[]{:S(2)}, u32[]{:S(2)}) collective-permute-start(f32[2,2,2,1,384]{4,1,0,3,2:T(2,128)S(1)} %copy.204), channel_id=1, source_target_pairs={{0,2},{1,3},{2,0},{3,1},{4,6},{5,7},{6,4},{7,5},{8,10},{9,11},{10,... | collective-permute-start | bytes 36872 | tf_op jit(solution)/shard_map/ppermute | solution.py:290
  600.7 17.8 %collective-permute-start.54 = (bf16[2,2,2,32,768]{4,3,0,1,2:T(8,128)(2,1)S(1)}, bf16[2,2,2,32,768]{4,3,0,1,2:T(8,128)(2,1)S(1)}, u32[]{:S(2)}, u32[]{:S(2)}) collective-permute-start(bf16[2,2,2,32,768]{4,3,0,1,2:T(8,128)(2,1)S(1)} %get-tuple-element.314), channel_id=1, source_target_pairs={{0,2},{1,3},{2,0},{3,1},{4,6},{5,7},{6,4},{7,5},{8,10},{9,11},{10,... | collective-permute-start | bytes 1179656 | tf_op jit(solution)/shard_map/ppermute | solution.py:290
  (82 other events, 1001.3 us)
Sparse Core Ops, SparseCore 0:
  52.3 88.5 all-gather.2
  143.8 75.6 all-gather.4

commit v3 on v2

--- a/solution.py
+++ b/solution.py
@@ -207,7 +207,7 @@
     tile = pl.BlockSpec((tokens, WIDE), lambda j: (0, j))
     return pl.pallas_call(up_kernel, grid=(hidden // WIDE,), name="feed",
         in_specs=[pl.BlockSpec((tokens, width), lambda j: (0, 0)),
-                  pl.BlockSpec((width, WIDE), lambda j: (0, width // WIDE + j)),
+                  pl.BlockSpec((width, WIDE), lambda j: (0, hidden // WIDE + j)),
                   pl.BlockSpec((1, WIDE), lambda j: (0, j))],
         out_specs=[tile, tile],
         out_shape=[jax.ShapeDtypeStruct((tokens, hidden), BF)] * 2, compiler_params=PARAMS)(x, packed, bias.reshape(1, hidden))
@@ -215,12 +215,69 @@
 
 def up_back_call(dz, weight, slope):
     tokens, width = dz.shape
-    hidden = weight.shape[0]
+    hidden = slope.shape[1]
+    halves = width // WIDE
     tile = pl.BlockSpec((tokens, WIDE), lambda j: (0, j))
     return pl.pallas_call(up_back_kernel, grid=(hidden // WIDE,), name="feed_back",
-        in_specs=[pl.BlockSpec((tokens, width), lambda j: (0, 0)), pl.BlockSpec((WIDE, width), lambda j: (j, 0)), tile],
+        in_specs=[pl.BlockSpec((tokens, width), lambda j: (0, 0)), pl.BlockSpec((WIDE, width), lambda j: (j % halves, j // halves)), tile],
         out_specs=[tile, pl.BlockSpec((1, WIDE), lambda j: (0, j))],
         out_shape=[jax.ShapeDtypeStruct((tokens, hidden), BF), jax.ShapeDtypeStruct((1, hidden), F32)], compiler_params=PARAMS)(dz, weight, slope)
+
+
+def settle_kernel(
+    hidden_ref, w_ref, bias_ref, first_ref, gain_ref, shift_ref, cot_ref,
+    out_ref, grad_ref, low_ref, gain_sum, shift_sum, bias_sum,
+):
+    width = first_ref.shape[1]
+    gain = gain_ref[...]
+    total = first_ref[...] + bias_ref[...]
+    for block in range(hidden_ref.shape[1] // width):
+        at = slice(block * width, (block + 1) * width)
+        total += matmul(hidden_ref[:, at], w_ref[:, at])
+    output, normed, inverse = normalize(total, gain, shift_ref[...])
+    out_ref[...] = output.astype(BF)
+    incoming = cot_ref[...].astype(F32)
+    scaled = incoming * gain
+    inner = scaled - jnp.mean(scaled, axis=-1, keepdims=True)
+    inner = inner - normed * jnp.mean(scaled * normed, axis=-1, keepdims=True)
+    grad = inverse * inner
+    low = grad.astype(BF)
+    grad_ref[...] = grad
+    low_ref[...] = low
+
+    @pl.when(pl.program_id(0) == 0)
+    def _():
+        for ref in (gain_sum, shift_sum, bias_sum):
+            ref[...] = jnp.zeros(ref.shape, F32)
+
+    gain_sum[...] += jnp.sum(incoming * normed, axis=0, keepdims=True)
+    shift_sum[...] += jnp.sum(incoming, axis=0, keepdims=True)
+    bias_sum[...] += jnp.sum(low.astype(F32), axis=0, keepdims=True)
+
+
+def settle(hidden, packed, bias, first, gain, shift, cotangent):
+    tokens, width = first.shape
+    units = hidden.shape[1]
+    row = pl.BlockSpec((TILE, width), lambda i: (i, 0))
+    vector = pl.BlockSpec((1, width), lambda i: (0, 0))
+    return pl.pallas_call(
+        settle_kernel,
+        grid=(tokens // TILE,),
+        name="settle",
+        in_specs=[
+            pl.BlockSpec((TILE, units), lambda i: (i, 0)),
+            pl.BlockSpec((width, units), lambda i: (0, 0)),
+            vector, row, vector, vector, row,
+        ],
+        out_specs=[row, row, row, vector, vector, vector],
+        out_shape=[
+            jax.ShapeDtypeStruct((tokens, width), BF),
+            jax.ShapeDtypeStruct((tokens, width), F32),
+            jax.ShapeDtypeStruct((tokens, width), BF),
+        ]
+        + [jax.ShapeDtypeStruct((1, width), F32)] * 3,
+        compiler_params=PARAMS,
+    )(hidden, packed, bias.reshape(1, -1), first, gain.reshape(1, -1), shift.reshape(1, -1), cotangent)
 
 
 def weight_kernel(own_ref, rows_t_ref, part_ref, keep_ref, send_ref):
@@ -307,7 +364,8 @@
         self.devices, self.kind, self.order = devices, kind, list(order)
         self.left = list(range(devices.bit_length() - 1))
         self.bits = len(self.left)
-        shape = (2,) * self.bits + (value.shape[0] // devices, value.shape[1])
+        self.lead = value.shape[:-2]
+        shape = self.lead + (2,) * self.bits + (value.shape[-2] // devices, value.shape[-1])
         self.got = None
         if pair is None:
             self.halve([value.reshape(shape)])
@@ -317,14 +375,14 @@
 
     def halve(self, terms):
         bit = self.order[0]
-        axis = self.left.index(self.bits - 1 - bit)
+        axis = len(self.lead) + self.left.index(self.bits - 1 - bit)
         own = (lax.axis_index(AXES) >> bit) & 1
         mine = [lax.dynamic_index_in_dim(t, own, axis, keepdims=False) for t in terms]
         theirs = [lax.dynamic_index_in_dim(t, 1 - own, axis, keepdims=False) for t in terms]
         self.keep = mine[0] if len(terms) == 1 else mine[0].astype(F32) + mine[1].astype(F32)
         send = theirs[0] if len(terms) == 1 else theirs[0].astype(F32) + theirs[1].astype(F32)
         self.send = send.astype(self.kind)
-        self.left.pop(axis)
+        self.left.pop(axis - len(self.lead))
 
     def begin(self):
         self.got = swap(self.send, self.order.pop(0), self.devices)
@@ -405,7 +463,11 @@
     side = jnp.concatenate([side, b_up.reshape(own, ratio)], axis=1)
     side = jnp.pad(side, ((0, 0), (0, PAIR - names - ratio)))
     head = jnp.concatenate([side, w_query, w_key, w_value], axis=1).astype(BF)
-    later = (jnp.concatenate([w_out, w_up], axis=1).astype(BF), w_down.astype(BF))
+    down_side = w_down.reshape(ratio, own, width).transpose(1, 0, 2).reshape(own, ratio * width)
+    up_side = w_up.astype(BF).reshape(own, devices, ratio, own).transpose(0, 2, 1, 3)
+    later = jnp.concatenate(
+        [down_side.astype(BF), up_side.reshape(own, -1), w_out.astype(BF)], axis=1
+    )
     head, later = gather_pairs(head, devices, later)
     head = jnp.concatenate(head, axis=1)
     packed_full = head[:, PAIR:]
@@ -413,9 +475,10 @@
         widen(head[:, i]) for i in range(names)
     ]
     up_bias = widen(head[:, names : names + ratio].reshape(-1))
-    out_up = lax.all_gather(later[0], AXES, axis=0, tiled=True)
-    down_full = lax.all_gather(later[1], AXES, axis=0, tiled=True)
-    out_full, up_full = out_up[:, :width], out_up[:, width:]
+    up_bias = up_bias.reshape(devices, ratio, own).transpose(1, 0, 2).reshape(-1)
+    rest = lax.all_gather(later, AXES, axis=0, tiled=True)
+    units = ratio * width
+    up_full, out_full = rest[:, units : 2 * units], rest[:, 2 * units :]
 
     packed_bias = jnp.concatenate([query_bias, jnp.zeros_like(query_bias), value_bias])
     packed = (matmul(rows, packed_full) + packed_bias).astype(BF)
@@ -424,19 +487,21 @@
     attended = matmul(context, out_full) + out_bias
     first, normed_one, inverse_one = normalize(rows.astype(F32) + attended, attn_gain, attn_shift)
     first_low = first.astype(BF)
-    hidden, slope = up_call(first_low, out_up, up_bias)
-    branch = matmul(hidden, down_full) + down_bias
-    output, normed_two, inverse_two = normalize(first + branch, ffn_gain, ffn_shift)
-    encoder_output = output.astype(BF).reshape(tokens.shape)
-
-    incoming = cotangent.reshape(blocks * length, width).astype(F32)
-    grad_two, ffn_gain_grad, ffn_shift_grad = normalize_back(incoming, normed_two, inverse_two, ffn_gain)
-    grad_branch = grad_two.astype(BF)
-    down = chains_of(contract_rows(hidden, grad_branch).astype(BF), devices, parts=2)
-    down_bias_grad = jnp.sum(grad_branch.astype(F32), axis=0)
+    hidden, slope = up_call(first_low, rest, up_bias)
+    output, grad_two, grad_branch, ffn_gain_grad, ffn_shift_grad, down_bias_grad = settle(
+        hidden, rest, down_bias, first, ffn_gain, ffn_shift, cotangent.reshape(blocks * length, width)
+    )
+    encoder_output = output.reshape(tokens.shape)
+    ffn_gain_grad, ffn_shift_grad, down_bias_grad = ffn_gain_grad[0], ffn_shift_grad[0], down_bias_grad[0]
+
+    down_product = contract_rows(hidden, grad_branch).astype(BF).reshape(ratio, width, width)
+    orders = bit_orders(devices.bit_length() - 1)
+    down = [
+        Chain(down_product[p * ratio // 2 : (p + 1) * ratio // 2], orders[p], devices) for p in range(2)
+    ]
     running = list(down)
     grad_branch = tick(running, grad_branch)
-    grad_pre, up_bias_grad = up_back_call(grad_branch, down_full, slope)
+    grad_pre, up_bias_grad = up_back_call(grad_branch, rest, slope)
     up_bias_grad = up_bias_grad[0]
     grad_pre = tick(running, grad_pre)
     up_product = contract_rows(first_low, grad_pre).astype(BF)
@@ -476,7 +541,7 @@
         down_bias_grad, ffn_gain_grad, ffn_shift_grad,
     ]
     side_grad = jnp.concatenate(
-        [v.reshape(devices, own) for v in vector_grads] + [up_bias_grad.reshape(devices, own * ratio)],
+        [v.reshape(devices, own) for v in vector_grads] + [up_bias_grad.reshape(ratio, devices, own).transpose(1, 0, 2).reshape(devices, -1)],
         axis=1,
     )
     side = chains_of(side_grad, devices, parts=1, kind=F32)
@@ -488,7 +553,9 @@
     while not all(c.over for c in running):
         tick(running, ())
 
-    down_grad, up_grad, out_grad = result(down), result(up), result(out)
+    up_grad, out_grad = result(up), result(out)
+    up_grad = up_grad.reshape(own, ratio, devices, own).transpose(0, 2, 1, 3).reshape(own, -1)
+    down_grad = jnp.concatenate([c.keep for c in down], axis=0).reshape(ratio * own, width)
     shares = [result(share) for share in shares]
     step = width // CHUNKS
     query_grad, key_grad, value_grad = [

time: 656 us -> 611 us (0.931)
  waiting for transfers between devices: 181 us -> 112 us
  Pallas kernels: 198 us -> 217 us
  matrix products: 76.3 us -> 65.7 us
  local copies, waits for them, and re-layouts: 42.5 us -> 52.7 us
    ppermute x65, waiting for transfers between devices: 138 us -> 89.5 us  [swap(): lax.ppermute(value, AXES, [(i, i ^ 1 << bit) for i in range(devices)])]
    all_gather x2 -> x1, waiting for transfers between devices: 42.7 us -> 22.4 us  [local(): rest = lax.all_gather(later, AXES, axis=0, tiled=True)]
    pallas_call x0 -> x1, Pallas kernels: none -> 19.5 us  [settle(): pl.pallas_call(settle_kernel, grid=(tokens // TILE,), name='settle', in_s...]
    dot_general x3 -> x2, matrix products: 28 us -> 13.3 us  [matmul(): return jnp.dot(left, right, preferred_element_type=F32)]
    dynamic_slice x10 -> x3, local copies, waits for them, and re-layouts: 9.41 us -> 1.3 us  [halve(): lax.dynamic_index_in_dim(t, 1 - own, axis, keepdims=False)]
    reshape x0 -> x5, local copies, waits for them, and re-layouts: none -> 7.27 us  [the longest x2 5.15 us: local(): up_grad.reshape(own, ratio, devices, own).transpose(0, 2, 1, 3)]
    reduce_sum x3 -> x0, other arithmetic: 6.67 us -> none  [the longest x1 3.55 us: local(): down_bias_grad = jnp.sum(grad_branch.astype(F32), axis=0)]
  transfers between devices with their start and end apart: 67 -> 66, of which waited for: 20 -> 19; matrix products, arithmetic and copies ran while one was open for 14% -> 20% of each run, Pallas kernels for 30% -> 30%
where the time goes in v3:
time: 611 us; the launch traced here: 602 us
  Pallas kernels  217 us (36%)
  waiting for transfers between devices  112 us (18%)
  other arithmetic  78.3 us (13%)
  matrix products  65.7 us (11%)
  starting transfers between devices  60.5 us (10%)
  local copies, waits for them, and re-layouts  52.7 us (9%)
  between operations  15.8 us (3%)
    ppermute x65, waiting for transfers between devices, swap(): lax.ppermute(value, AXES, [(i, i ^ 1 << bit) for i in range(devices)])  89.5 us
    pallas_call x4, Pallas kernels, attend_back(): pl.pallas_call(backward_kernel, grid=(count,), name='attend_back', in_spe...  77 us
    ppermute x65, starting transfers between devices, swap(): lax.ppermute(value, AXES, [(i, i ^ 1 << bit) for i in range(devices)])  60.5 us
    pallas_call x1, Pallas kernels, attend(): pl.pallas_call(forward_kernel, grid=(pairs,), name='attend', in_specs=seg...  50.4 us
    convert_element_type x36, other arithmetic, halve(): self.send = send.astype(self.kind)  34.3 us
    dot_general x3, matrix products, contract_rows(): lax.dot_general(left, right, (((0,), (0,)), ((), ())), preferred_element_...  29.9 us
    dot_general x2, matrix products, contract_cols(): lax.dot_general(left, right, (((1,), (1,)), ((), ())), preferred_element_...  22.5 us
    all_gather x1, waiting for transfers between devices, local(): rest = lax.all_gather(later, AXES, axis=0, tiled=True)  22.4 us
  transfers between devices with their start and end apart: 66, of which 19 were waited for; matrix products, arithmetic and copies ran while one was open for 20% of the time, Pallas kernels for 30%

profile of v3, /device:TPU:0, one launch (start us, length us, event | category | flops | bytes accessed | tf_op | source)
XLA Modules:
  0.0 601.9 jit_solution(9991736651655250075)
XLA Ops:
  16.1 4.1 collective-permute-start
  42.1 8.0 %collective-permute-done.5 = bf16[2,2,32,1024]{3,2,1,0:T(8,128)(2,1)S(1)} collective-permute-done((bf16[2,2,32,1024]{3,2,1,0:T(8,128)(2,1)S(1)}, bf16[2,2,32,1024]{3,2,1,0:T(8,128)(2,1)S(1)}, u32[]{:S(2)}, u32[]{:S(2)}) %collective-permute-start.5) | collective-permute-done | bytes 262176 | tf_op jit(solution)/shard_map/ppermute | solution.py:347
  50.2 4.6 collective-permute-done.8
  57.2 14.5 %collective-permute-done.9 = bf16[2,2,2,32,1024]{4,3,0,1,2:T(8,128)(2,1)S(1)} collective-permute-done((bf16[2,2,2,32,1024]{4,3,0,1,2:T(8,128)(2,1)S(1)}, bf16[2,2,2,32,1024]{4,3,0,1,2:T(8,128)(2,1)S(1)}, u32[]{:S(2)}, u32[]{:S(2)}) %collective-permute-start.9) | collective-permute-done | bytes 524320 | tf_op jit(solution)/shard_map/ppermute | solution.py:347
  73.1 10.2 %collective-permute-done.13 = bf16[2,2,2,32,1152]{4,3,1,2,0:T(8,128)(2,1)S(1)} collective-permute-done((bf16[2,2,2,32,1152]{4,3,1,2,0:T(8,128)(2,1)S(1)}, bf16[2,2,2,32,1152]{4,3,1,2,0:T(8,128)(2,1)S(1)}, u32[]{:S(2)}, u32[]{:S(2)}) %collective-permute-start.13) | collective-permute-done | bytes 589856 | tf_op jit(solution)/shard_map/ppermute | solution.py:347
  99.4 8.7 %fusion.2.q_ref.k_ref.v_ref = bf16[1024,3072]{1,0:T(8,128)(2,1)} fusion(f32[3072]{0:T(1024)S(1)} %pad_maximum_fusion.11, bf16[1024,3200]{1,0:T(8,128)(2,1)S(1)} %pad_maximum_fusion.refs_1_, bf16[1,1024,1024]{2,1,0:T(8,128)(2,1)S(1)} %copy-done.12), kind=kOutput, calls=%fused_computation.6 | convolution fusion | flops 6448742400 | bytes 14692352 | tf_op jit(solution)/shard_map/dot_general | solution.py:25
  108.1 50.4 %attend.1 = (bf16[1024,1024]{1,0:T(8,128)(2,1)}, f32[8,2,1024]{2,1,0:T(2,128)}) custom-call(s32[1024,1]{1,0:T(8,128)} %copy.197.seg_col, s32[1,1024]{1,0:T(1,128)} %seg_row.9, bf16[1024,3072]{1,0:T(8,128)(2,1)} %fusion.2.q_ref.k_ref.v_ref, bf16[1024,3072]{1,0:T(8,128)(2,1)} %fusion.2.q_ref.k_ref.v_ref, bf16[1024,3072]{1,0:T(8,128)(2,1)} %fusion.2.q_ref.k_ref.v_ref), custom_call_target="tpu_custom_call" | custom-call | tf_op jit(solution)/shard_map/attend/pallas_call | solution.py:136
  158.5 22.4 %all-gather.2.cloned.1.call-done.w_ref = bf16[1024,9216]{1,0:T(8,128)(2,1)} async-done(((bf16[32,9216]{1,0:T(8,128)(2,1)}), bf16[1024,9216]{1,0:T(8,128)(2,1)}) %all-gather.2.cloned.1.call-update) | async-done | bytes 18874384 | tf_op jit(solution)/shard_map/all_gather | solution.py:479
  180.9 4.7 fusion.84
  191.1 19.8 %feed.1 = (bf16[1024,4096]{1,0:T(8,128)(2,1)}, bf16[1024,4096]{1,0:T(8,128)(2,1)}) custom-call(bf16[1024,1024]{1,0:T(8,128)(2,1)} %get-tuple-element.369.x_ref, bf16[1024,9216]{1,0:T(8,128)(2,1)} %all-gather.2.cloned.1.call-done.w_ref, f32[1,4096]{1,0:T(1,128)} %reshape.1356.b_ref), custom_call_target="tpu_custom_call" | custom-call | tf_op jit(solution)/shard_map/feed/pallas_call | solution.py:208
  211.0 19.5 %settle.1 = (bf16[1024,1024]{1,0:T(8,128)(2,1)}, f32[1024,1024]{1,0:T(8,128)}, bf16[1024,1024]{1,0:T(8,128)(2,1)}, f32[1,1024]{1,0:T(1,128)}, f32[1,1024]{1,0:T(1,128)}, /*index=5*/f32[1,1024]{1,0:T(1,128)}) custom-call(bf16[1024,4096]{1,0:T(8,128)(2,1)} %get-tuple-element.191.hidden_ref, bf16[1024,9216]{1,0:T(8,128)(2,1)} %all-gather.2.cloned.1.call-done.w_ref, ...), custom_call_target="tpu_custom_call" | custom-call | tf_op jit(solution)/shard_map/settle/pallas_call | solution.py:263
  230.4 12.9 %convolution_convert_fusion.1 = bf16[4096,1024]{1,0:T(8,128)(2,1)S(1)} fusion(bf16[1024,4096]{1,0:T(8,128)(2,1)} %get-tuple-element.191.hidden_ref, bf16[1024,1024]{1,0:T(8,128)(2,1)} %get-tuple-element.195.dz_ref), kind=kOutput, calls=%fused_computation.4 | convolution fusion | flops 8594128896 | bytes 18874368 | tf_op jit(solution)/shard_map/dot_general | solution.py:29
  250.5 16.5 %feed_back.1 = (bf16[1024,4096]{1,0:T(8,128)(2,1)}, f32[1,4096]{1,0:T(1,128)}) custom-call(bf16[1024,1024]{1,0:T(8,128)(2,1)} %get-tuple-element.195.dz_ref, bf16[1024,9216]{1,0:T(8,128)(2,1)} %all-gather.2.cloned.1.call-done.w_ref, bf16[1024,4096]{1,0:T(8,128)(2,1)} %get-tuple-element.196.slope_ref), custom_call_target="tpu_custom_call" | custom-call | tf_op jit(solution)/shard_map/feed_back/pallas_call | solution.py:221
  271.8 4.3 fusion.15
  278.1 14.6 %convolution_convert_fusion = bf16[1024,4096]{1,0:T(8,128)(2,1)} fusion(bf16[1024,1024]{1,0:T(8,128)(2,1)S(1)} %copy-done.4, bf16[1024,4096]{1,0:T(8,128)(2,1)} %get-tuple-element.207), kind=kOutput, calls=%fused_computation.3 | convolution fusion | flops 8594128896 | bytes 18874368 | tf_op jit(solution)/shard_map/dot_general | solution.py:29
  292.7 3.8 fusion.78
  297.8 3.7 collective-permute-done.17
  308.8 17.1 %multiply_reduce_fusion = (f32[1024]{0:T(1024)S(1)}, f32[1024]{0:T(1024)S(1)}, f32[1024]{0:T(1024)S(1)}, f32[1024]{0:T(1024)S(1)}, f32[1024,1024]{1,0:T(8,128)}) fusion(f32[1024,1024]{1,0:T(8,128)S(1)} %copy-done.1, f32[1024]{0:T(1024)S(1)} %add_rsqrt_fusion, f32[1024]{0:T(1024)S(1)} %broadcast_multiply_fusion.2, f32[1024]{0:T(1024)S(1)} %get-tuple-element.363, ...), kind=kOutput, calls=%fused_computation.9 | convolution fusion | flops 8600416256 | bytes 29388800 | tf_op jit(solution)/shard_map/dot_general | solution.py:33
  336.8 5.4 convolution_convert_fusion.3.do_ref
  352.5 3.9 copy.234.rows_t_ref
  356.5 19.3 %attend_back.4 = (bf16[3,1024,256]{2,1,0:T(8,128)(2,1)}, f32[1,256]{1,0:T(1,128)}, f32[1,256]{1,0:T(1,128)}) custom-call(s32[1024,1]{1,0:T(8,128)} %copy.197.seg_col, s32[1,1024]{1,0:T(1,128)} %seg_row.9, bf16[1024,3072]{1,0:T(8,128)(2,1)} %fusion.2.q_ref.k_ref.v_ref, bf16[1024,3072]{1,0:T(8,128)(2,1)} %fusion.2.q_ref.k_ref.v_ref, ...), custom_call_target="tpu_custom_call" | custom-call | tf_op jit(solution)/shard_map/attend_back/pallas_call | solution.py:158
  375.8 5.5 weight_halves.4
  397.2 19.1 %attend_back.5 = (bf16[3,1024,256]{2,1,0:T(8,128)(2,1)}, f32[1,256]{1,0:T(1,128)}, f32[1,256]{1,0:T(1,128)}) custom-call(s32[1024,1]{1,0:T(8,128)} %copy.197.seg_col, s32[1,1024]{1,0:T(1,128)} %seg_row.9, bf16[1024,3072]{1,0:T(8,128)(2,1)} %fusion.2.q_ref.k_ref.v_ref, bf16[1024,3072]{1,0:T(8,128)(2,1)} %fusion.2.q_ref.k_ref.v_ref, ...), custom_call_target="tpu_custom_call" | custom-call | tf_op jit(solution)/shard_map/attend_back/pallas_call | solution.py:158
  419.9 5.4 weight_halves.5
  426.6 14.3 %collective-permute-done.30 = bf16[2,2,32,2048]{3,2,1,0:T(8,128)(2,1)S(1)} collective-permute-done((bf16[2,2,32,2048]{3,2,1,0:T(8,128)(2,1)S(1)}, bf16[2,2,32,2048]{3,2,1,0:T(8,128)(2,1)S(1)}, u32[]{:S(2)}, u32[]{:S(2)}) %collective-permute-start.30) | collective-permute-done | bytes 524320 | tf_op jit(solution)/shard_map/ppermute | solution.py:347
  443.2 19.4 %attend_back.6 = (bf16[3,1024,256]{2,1,0:T(8,128)(2,1)}, f32[1,256]{1,0:T(1,128)}, f32[1,256]{1,0:T(1,128)}) custom-call(s32[1024,1]{1,0:T(8,128)} %copy.197.seg_col, s32[1,1024]{1,0:T(1,128)} %seg_row.9, bf16[1024,3072]{1,0:T(8,128)(2,1)} %fusion.2.q_ref.k_ref.v_ref, bf16[1024,3072]{1,0:T(8,128)(2,1)} %fusion.2.q_ref.k_ref.v_ref, ...), custom_call_target="tpu_custom_call" | custom-call | tf_op jit(solution)/shard_map/attend_back/pallas_call | solution.py:158
  466.2 5.4 weight_halves.6
  485.0 19.2 %attend_back.7 = (bf16[3,1024,256]{2,1,0:T(8,128)(2,1)}, f32[1,256]{1,0:T(1,128)}, f32[1,256]{1,0:T(1,128)}) custom-call(s32[1024,1]{1,0:T(8,128)} %copy.197.seg_col, s32[1,1024]{1,0:T(1,128)} %seg_row.9, bf16[1024,3072]{1,0:T(8,128)(2,1)} %fusion.2.q_ref.k_ref.v_ref, bf16[1024,3072]{1,0:T(8,128)(2,1)} %fusion.2.q_ref.k_ref.v_ref, ...), custom_call_target="tpu_custom_call" | custom-call | tf_op jit(solution)/shard_map/attend_back/pallas_call | solution.py:158
  508.2 5.6 weight_halves.7
  535.4 7.0 %collective-permute-done.48 = bf16[2,2,2,32,768]{4,3,1,2,0:T(8,128)(2,1)S(1)} collective-permute-done((bf16[2,2,2,32,768]{4,3,1,2,0:T(8,128)(2,1)S(1)}, bf16[2,2,2,32,768]{4,3,1,2,0:T(8,128)(2,1)S(1)}, u32[]{:S(2)}, u32[]{:S(2)}) %collective-permute-start.48) | collective-permute-done | bytes 393248 | tf_op jit(solution)/shard_map/ppermute | solution.py:347
  548.6 4.5 reshape.1349
  559.2 12.0 %input_grad.1 = bf16[1024,1024]{1,0:T(8,128)(2,1)} custom-call(f32[1024,1024]{1,0:T(8,128)} %copy-done.3, bf16[1024,3200]{1,0:T(8,128)(2,1)} %copy-done.2, bf16[3,1024,256]{2,1,0:T(8,128)(2,1)} %get-tuple-element.313.part_ref.refs_2_, bf16[3,1024,256]{2,1,0:T(8,128)(2,1)} %get-tuple-element.314.part_ref.refs_3_, ...), custom_call_target="tpu_custom_call" | custom-call | tf_op jit(solution)/shard_map/input_grad/pallas_call | solution.py:334
  (412 shorter events, 200.6 us)
Async XLA Ops:
  7.2 173.7 %all-gather.2.cloned.1.call-start = ((), (), s32[]{:S(2)}) async-start(), calls=%async_computation | async-start | bytes 19464192 | tf_op jit(solution)/shard_map/all_gather | solution.py:479
  39.4 15.4 %collective-permute-start.8 = (bf16[2,2,32,1152]{3,2,0,1:T(8,128)(2,1)S(1)}, bf16[2,2,32,1152]{3,2,0,1:T(8,128)(2,1)S(1)}, u32[]{:S(2)}, u32[]{:S(2)}) collective-permute-start(bf16[2,2,32,1152]{3,2,0,1:T(8,128)(2,1)S(1)} %maximum_select_fusion.12), channel_id=1, source_target_pairs={{0,16},{1,17},{2,18},{3,19},{4,20},{5,21},{6,22},{7,23},{8,24},{9,... | collective-permute-start | bytes 884744 | tf_op jit(solution)/shard_map/ppermute | solution.py:347
  54.9 16.8 %collective-permute-start.9 = (bf16[2,2,2,32,1024]{4,3,0,1,2:T(8,128)(2,1)S(1)}, bf16[2,2,2,32,1024]{4,3,0,1,2:T(8,128)(2,1)S(1)}, u32[]{:S(2)}, u32[]{:S(2)}) collective-permute-start(bf16[2,2,2,32,1024]{4,3,0,1,2:T(8,128)(2,1)S(1)} %maximum_select_fusion.9), channel_id=1, source_target_pairs={{0,2},{1,3},{2,0},{3,1},{4,6},{5,7},{6,4},{7,5},{8,10},{9,11},{10,... | collective-permute-start | bytes 1572872 | tf_op jit(solution)/shard_map/ppermute | solution.py:347
  55.5 16.4 %collective-permute-start.11 = (bf16[2,2,2,32,1024]{4,3,2,0,1:T(8,128)(2,1)S(1)}, bf16[2,2,2,32,1024]{4,3,2,0,1:T(8,128)(2,1)S(1)}, u32[]{:S(2)}, u32[]{:S(2)}) collective-permute-start(bf16[2,2,2,32,1024]{4,3,2,0,1:T(8,128)(2,1)S(1)} %maximum_select_fusion.10), channel_id=1, source_target_pairs={{0,4},{1,5},{2,6},{3,7},{4,0},{5,1},{6,2},{7,3},{8,12},{9,13},{10,... | collective-permute-start | bytes 1572872 | tf_op jit(solution)/shard_map/ppermute | solution.py:347
  57.2 26.1 %collective-permute-start.13 = (bf16[2,2,2,32,1152]{4,3,1,2,0:T(8,128)(2,1)S(1)}, bf16[2,2,2,32,1152]{4,3,1,2,0:T(8,128)(2,1)S(1)}, u32[]{:S(2)}, u32[]{:S(2)}) collective-permute-start(bf16[2,2,2,32,1152]{4,3,1,2,0:T(8,128)(2,1)S(1)} %maximum_select_fusion.8), channel_id=1, source_target_pairs={{0,8},{1,9},{2,10},{3,11},{4,12},{5,13},{6,14},{7,15},{8,0},{9,1},... | collective-permute-start | bytes 1769480 | tf_op jit(solution)/shard_map/ppermute | solution.py:347
  248.4 18.6 %collective-permute-start.15 = (bf16[2,2,2,2,2,32,1024]{6,5,0,1,2,3,4:T(8,128)(2,1)}, bf16[2,2,2,2,2,32,1024]{6,5,0,1,2,3,4:T(8,128)(2,1)}, u32[]{:S(2)}, u32[]{:S(2)}) collective-permute-start(bf16[2,2,2,2,2,32,1024]{6,5,0,1,2,3,4:T(8,128)(2,1)} %copy.205), channel_id=1, source_target_pairs={{0,1},{1,0},{2,3},{3,2},{4,5},{5,4},{6,7},{7,6},{8,9},{9,8},{10,11... | collective-permute-start | bytes 6291464 | tf_op jit(solution)/shard_map/ppermute | solution.py:347
  250.3 21.5 %collective-permute-start.16 = (bf16[2,2,2,2,2,32,1024]{6,5,0,4,1,2,3:T(8,128)(2,1)}, bf16[2,2,2,2,2,32,1024]{6,5,0,4,1,2,3:T(8,128)(2,1)}, u32[]{:S(2)}, u32[]{:S(2)}) collective-permute-start(bf16[2,2,2,2,2,32,1024]{6,5,0,4,1,2,3:T(8,128)(2,1)} %copy.208), channel_id=1, source_target_pairs={{0,1},{1,0},{2,3},{3,2},{4,5},{5,4},{6,7},{7,6},{8,9},{9,8},{10,11... | collective-permute-start | bytes 6291464 | tf_op jit(solution)/shard_map/ppermute | solution.py:347
  276.1 25.4 %collective-permute-start.17 = (bf16[2,2,2,2,32,1024]{5,4,3,2,1,0:T(8,128)(2,1)S(1)}, bf16[2,2,2,2,32,1024]{5,4,3,2,1,0:T(8,128)(2,1)}, u32[]{:S(2)}, u32[]{:S(2)}) collective-permute-start(bf16[2,2,2,2,32,1024]{5,4,3,2,1,0:T(8,128)(2,1)S(1)} %fusion.16), channel_id=1, source_target_pairs={{0,2},{1,3},{2,0},{3,1},{4,6},{5,7},{6,4},{7,5},{8,10},{9,11},{10,... | collective-permute-start | bytes 3145736 | tf_op jit(solution)/shard_map/ppermute | solution.py:347
  277.5 28.4 %collective-permute-start.18 = (bf16[2,2,2,2,32,1024]{5,4,0,3,1,2:T(8,128)(2,1)}, bf16[2,2,2,2,32,1024]{5,4,0,3,1,2:T(8,128)(2,1)}, u32[]{:S(2)}, u32[]{:S(2)}) collective-permute-start(bf16[2,2,2,2,32,1024]{5,4,0,3,1,2:T(8,128)(2,1)} %get-tuple-element.206), channel_id=1, source_target_pairs={{0,4},{1,5},{2,6},{3,7},{4,0},{5,1},{6,2},{7,3},{8,12},{9,13},{10,... | collective-permute-start | bytes 3145736 | tf_op jit(solution)/shard_map/ppermute | solution.py:347
  325.9 16.3 %collective-permute-start.19 = (bf16[2,2,2,32,1024]{4,3,2,1,0:T(8,128)(2,1)S(1)}, bf16[2,2,2,32,1024]{4,3,2,1,0:T(8,128)(2,1)S(1)}, u32[]{:S(2)}, u32[]{:S(2)}) collective-permute-start(bf16[2,2,2,32,1024]{4,3,2,1,0:T(8,128)(2,1)S(1)} %fusion.22), channel_id=1, source_target_pairs={{0,4},{1,5},{2,6},{3,7},{4,0},{5,1},{6,2},{7,3},{8,12},{9,13},{10,... | collective-permute-start | bytes 1572872 | tf_op jit(solution)/shard_map/ppermute | solution.py:347
  328.1 17.4 %collective-permute-start.21 = (bf16[2,2,2,2,32,2048]{5,4,2,3,0,1:T(8,128)(2,1)S(1)}, bf16[2,2,2,2,32,2048]{5,4,2,3,0,1:T(8,128)(2,1)S(1)}, u32[]{:S(2)}, u32[]{:S(2)}) collective-permute-start(bf16[2,2,2,2,32,2048]{5,4,2,3,0,1:T(8,128)(2,1)S(1)} %copy.219), channel_id=1, source_target_pairs={{0,1},{1,0},{2,3},{3,2},{4,5},{5,4},{6,7},{7,6},{8,9},{9,8},{10,11... | collective-permute-start | bytes 6291464 | tf_op jit(solution)/shard_map/ppermute | solution.py:347
  328.3 15.1 %collective-permute-start.22 = (bf16[2,2,2,2,32,2048]{5,4,0,1,2,3:T(8,128)(2,1)S(1)}, bf16[2,2,2,2,32,2048]{5,4,0,1,2,3:T(8,128)(2,1)S(1)}, u32[]{:S(2)}, u32[]{:S(2)}) collective-permute-start(bf16[2,2,2,2,32,2048]{5,4,0,1,2,3:T(8,128)(2,1)S(1)} %copy.222), channel_id=1, source_target_pairs={{0,1},{1,0},{2,3},{3,2},{4,5},{5,4},{6,7},{7,6},{8,9},{9,8},{10,11... | collective-permute-start | bytes 6291464 | tf_op jit(solution)/shard_map/ppermute | solution.py:347
  348.3 39.3 %collective-permute-start.26 = (bf16[2,2,2,32,2048]{4,3,0,1,2:T(8,128)(2,1)}, bf16[2,2,2,32,2048]{4,3,0,1,2:T(8,128)(2,1)}, u32[]{:S(2)}, u32[]{:S(2)}) collective-permute-start(bf16[2,2,2,32,2048]{4,3,0,1,2:T(8,128)(2,1)} %copy.232), channel_id=1, source_target_pairs={{0,2},{1,3},{2,0},{3,1},{4,6},{5,7},{6,4},{7,5},{8,10},{9,11},{10,... | collective-permute-start | bytes 3145736 | tf_op jit(solution)/shard_map/ppermute | solution.py:347
  348.8 40.3 %collective-permute-start.25 = (bf16[2,2,2,32,2048]{4,3,2,1,0:T(8,128)(2,1)}, bf16[2,2,2,32,2048]{4,3,2,1,0:T(8,128)(2,1)}, u32[]{:S(2)}, u32[]{:S(2)}) collective-permute-start(bf16[2,2,2,32,2048]{4,3,2,1,0:T(8,128)(2,1)} %fusion.17), channel_id=1, source_target_pairs={{0,8},{1,9},{2,10},{3,11},{4,12},{5,13},{6,14},{7,15},{8,0},{9,1},... | collective-permute-start | bytes 3145736 | tf_op jit(solution)/shard_map/ppermute | solution.py:347
  350.4 33.6 %collective-permute-start.23 = (bf16[2,2,32,1024]{3,2,1,0:T(8,128)(2,1)S(1)}, bf16[2,2,32,1024]{3,2,1,0:T(8,128)(2,1)}, u32[]{:S(2)}, u32[]{:S(2)}) collective-permute-start(bf16[2,2,32,1024]{3,2,1,0:T(8,128)(2,1)S(1)} %fusion.33), channel_id=1, source_target_pairs={{0,8},{1,9},{2,10},{3,11},{4,12},{5,13},{6,14},{7,15},{8,0},{9,1},... | collective-permute-start | bytes 786440 | tf_op jit(solution)/shard_map/ppermute | solution.py:347
  350.8 34.1 %collective-permute-start.24 = (bf16[2,2,32,1024]{3,2,0,1:T(8,128)(2,1)S(1)}, bf16[2,2,32,1024]{3,2,0,1:T(8,128)(2,1)}, u32[]{:S(2)}, u32[]{:S(2)}) collective-permute-start(bf16[2,2,32,1024]{3,2,0,1:T(8,128)(2,1)S(1)} %get-tuple-element.226), channel_id=1, source_target_pairs={{0,16},{1,17},{2,18},{3,19},{4,20},{5,21},{6,22},{7,23},{8,24},{9,... | collective-permute-start | bytes 786440 | tf_op jit(solution)/shard_map/ppermute | solution.py:347
  375.8 15.9 %collective-permute-start.27 = (bf16[2,2,2,2,32,1024]{5,4,2,3,0,1:T(8,128)(2,1)S(1)}, bf16[2,2,2,2,32,1024]{5,4,2,3,0,1:T(8,128)(2,1)}, u32[]{:S(2)}, u32[]{:S(2)}) collective-permute-start(bf16[2,2,2,2,32,1024]{5,4,2,3,0,1:T(8,128)(2,1)S(1)} %bitcast.419), channel_id=1, source_target_pairs={{0,1},{1,0},{2,3},{3,2},{4,5},{5,4},{6,7},{7,6},{8,9},{9,8},{10,11... | collective-permute-start | bytes 3145736 | tf_op jit(solution)/shard_map/ppermute | solution.py:347
  394.1 31.2 %collective-permute-start.28 = (bf16[2,32,1024]{2,1,0:T(8,128)(2,1)S(1)}, bf16[2,32,1024]{2,1,0:T(8,128)(2,1)S(1)}, u32[]{:S(2)}, u32[]{:S(2)}) collective-permute-start(bf16[2,32,1024]{2,1,0:T(8,128)(2,1)S(1)} %fusion.45), channel_id=1, source_target_pairs={{0,16},{1,17},{2,18},{3,19},{4,20},{5,21},{6,22},{7,23},{8,24},{9,... | collective-permute-start | bytes 393224 | tf_op jit(solution)/shard_map/ppermute | solution.py:347
  395.6 29.8 %collective-permute-start.32 = (bf16[2,2,2,32,1024]{4,3,1,2,0:T(8,128)(2,1)}, bf16[2,2,2,32,1024]{4,3,1,2,0:T(8,128)(2,1)}, u32[]{:S(2)}, u32[]{:S(2)}) collective-permute-start(bf16[2,2,2,32,1024]{4,3,1,2,0:T(8,128)(2,1)} %get-tuple-element.250), channel_id=1, source_target_pairs={{0,8},{1,9},{2,10},{3,11},{4,12},{5,13},{6,14},{7,15},{8,0},{9,1},... | collective-permute-start | bytes 1572872 | tf_op jit(solution)/shard_map/ppermute | solution.py:347
  418.0 22.9 %collective-permute-start.30 = (bf16[2,2,32,2048]{3,2,1,0:T(8,128)(2,1)S(1)}, bf16[2,2,32,2048]{3,2,1,0:T(8,128)(2,1)S(1)}, u32[]{:S(2)}, u32[]{:S(2)}) collective-permute-start(bf16[2,2,32,2048]{3,2,1,0:T(8,128)(2,1)S(1)} %fusion.23), channel_id=1, source_target_pairs={{0,16},{1,17},{2,18},{3,19},{4,20},{5,21},{6,22},{7,23},{8,24},{9,... | collective-permute-start | bytes 1572872 | tf_op jit(solution)/shard_map/ppermute | solution.py:347
  419.3 21.7 %collective-permute-start.31 = (bf16[2,2,32,2048]{3,2,0,1:T(8,128)(2,1)}, bf16[2,2,32,2048]{3,2,0,1:T(8,128)(2,1)}, u32[]{:S(2)}, u32[]{:S(2)}) collective-permute-start(bf16[2,2,32,2048]{3,2,0,1:T(8,128)(2,1)} %copy.238), channel_id=1, source_target_pairs={{0,4},{1,5},{2,6},{3,7},{4,0},{5,1},{6,2},{7,3},{8,12},{9,13},{10,... | collective-permute-start | bytes 1572872 | tf_op jit(solution)/shard_map/ppermute | solution.py:347
  425.3 17.0 %collective-permute-start.33 = (bf16[2,2,2,2,32,768]{5,4,0,1,2,3:T(8,128)(2,1)S(1)}, bf16[2,2,2,2,32,768]{5,4,0,1,2,3:T(8,128)(2,1)S(1)}, u32[]{:S(2)}, u32[]{:S(2)}) collective-permute-start(bf16[2,2,2,2,32,768]{5,4,0,1,2,3:T(8,128)(2,1)S(1)} %copy.240), channel_id=1, source_target_pairs={{0,1},{1,0},{2,3},{3,2},{4,5},{5,4},{6,7},{7,6},{8,9},{9,8},{10,11... | collective-permute-start | bytes 2359304 | tf_op jit(solution)/shard_map/ppermute | solution.py:347
  442.5 29.1 %collective-permute-start.34 = (bf16[2,32,2048]{2,1,0:T(8,128)(2,1)S(1)}, bf16[2,32,2048]{2,1,0:T(8,128)(2,1)S(1)}, u32[]{:S(2)}, u32[]{:S(2)}) collective-permute-start(bf16[2,32,2048]{2,1,0:T(8,128)(2,1)S(1)} %fusion.34), channel_id=1, source_target_pairs={{0,2},{1,3},{2,0},{3,1},{4,6},{5,7},{6,4},{7,5},{8,10},{9,11},{10,... | collective-permute-start | bytes 786440 | tf_op jit(solution)/shard_map/ppermute | solution.py:347
  443.1 32.6 %collective-permute-start.38 = (bf16[2,2,2,2,32,768]{5,4,3,0,1,2:T(8,128)(2,1)S(1)}, bf16[2,2,2,2,32,768]{5,4,3,0,1,2:T(8,128)(2,1)S(1)}, u32[]{:S(2)}, u32[]{:S(2)}) collective-permute-start(bf16[2,2,2,2,32,768]{5,4,3,0,1,2:T(8,128)(2,1)S(1)} %copy.245), channel_id=1, source_target_pairs={{0,1},{1,0},{2,3},{3,2},{4,5},{5,4},{6,7},{7,6},{8,9},{9,8},{10,11... | collective-permute-start | bytes 2359304 | tf_op jit(solution)/shard_map/ppermute | solution.py:347
  443.2 29.1 %collective-permute-start.36 = (bf16[2,2,32,1024]{3,2,0,1:T(8,128)(2,1)S(1)}, bf16[2,2,32,1024]{3,2,0,1:T(8,128)(2,1)S(1)}, u32[]{:S(2)}, u32[]{:S(2)}) collective-permute-start(bf16[2,2,32,1024]{3,2,0,1:T(8,128)(2,1)S(1)} %get-tuple-element.266), channel_id=1, source_target_pairs={{0,16},{1,17},{2,18},{3,19},{4,20},{5,21},{6,22},{7,23},{8,24},{9,... | collective-permute-start | bytes 786440 | tf_op jit(solution)/shard_map/ppermute | solution.py:347
  476.6 39.8 %collective-permute-start.39 = (bf16[32,2048]{1,0:T(8,128)(2,1)}, bf16[32,2048]{1,0:T(8,128)(2,1)}, u32[]{:S(2)}, u32[]{:S(2)}) collective-permute-start(bf16[32,2048]{1,0:T(8,128)(2,1)} %get-tuple-element.276), channel_id=1, source_target_pairs={{0,4},{1,5},{2,6},{3,7},{4,0},{5,1},{6,2},{7,3},{8,12},{9,13},{10,... | collective-permute-start | bytes 393224 | tf_op jit(solution)/shard_map/ppermute | solution.py:347
  521.8 21.5 %collective-permute-start.49 = (bf16[2,2,2,2,32,768]{5,4,0,1,2,3:T(8,128)(2,1)S(1)}, bf16[2,2,2,2,32,768]{5,4,0,1,2,3:T(8,128)(2,1)S(1)}, u32[]{:S(2)}, u32[]{:S(2)}) collective-permute-start(bf16[2,2,2,2,32,768]{5,4,0,1,2,3:T(8,128)(2,1)S(1)} %copy.255), channel_id=1, source_target_pairs={{0,1},{1,0},{2,3},{3,2},{4,5},{5,4},{6,7},{7,6},{8,9},{9,8},{10,11... | collective-permute-start | bytes 2359304 | tf_op jit(solution)/shard_map/ppermute | solution.py:347
  526.9 15.5 %collective-permute-start.48 = (bf16[2,2,2,32,768]{4,3,1,2,0:T(8,128)(2,1)S(1)}, bf16[2,2,2,32,768]{4,3,1,2,0:T(8,128)(2,1)S(1)}, u32[]{:S(2)}, u32[]{:S(2)}) collective-permute-start(bf16[2,2,2,32,768]{4,3,1,2,0:T(8,128)(2,1)S(1)} %get-tuple-element.308), channel_id=1, source_target_pairs={{0,8},{1,9},{2,10},{3,11},{4,12},{5,13},{6,14},{7,15},{8,0},{9,1},... | collective-permute-start | bytes 1179656 | tf_op jit(solution)/shard_map/ppermute | solution.py:347
  544.3 27.0 %collective-permute-start.55 = (f32[2,2,2,1,384]{4,1,0,3,2:T(2,128)S(1)}, f32[2,2,2,1,384]{4,1,0,3,2:T(2,128)S(1)}, u32[]{:S(2)}, u32[]{:S(2)}) collective-permute-start(f32[2,2,2,1,384]{4,1,0,3,2:T(2,128)S(1)} %copy.258), channel_id=1, source_target_pairs={{0,2},{1,3},{2,0},{3,1},{4,6},{5,7},{6,4},{7,5},{8,10},{9,11},{10,... | collective-permute-start | bytes 36872 | tf_op jit(solution)/shard_map/ppermute | solution.py:347
  553.1 18.2 %collective-permute-start.51 = (bf16[32,768]{1,0:T(8,128)(2,1)S(1)}, bf16[32,768]{1,0:T(8,128)(2,1)S(1)}, u32[]{:S(2)}, u32[]{:S(2)}) collective-permute-start(bf16[32,768]{1,0:T(8,128)(2,1)S(1)} %copy-done.32), channel_id=1, source_target_pairs={{0,16},{1,17},{2,18},{3,19},{4,20},{5,21},{6,22},{7,23},{8,24},{9,... | collective-permute-start | bytes 147464 | tf_op jit(solution)/shard_map/ppermute | solution.py:347
  554.8 16.6 %collective-permute-start.52 = (bf16[2,32,768]{2,1,0:T(8,128)(2,1)S(1)}, bf16[2,32,768]{2,1,0:T(8,128)(2,1)S(1)}, u32[]{:S(2)}, u32[]{:S(2)}) collective-permute-start(bf16[2,32,768]{2,1,0:T(8,128)(2,1)S(1)} %copy-done.31), channel_id=1, source_target_pairs={{0,16},{1,17},{2,18},{3,19},{4,20},{5,21},{6,22},{7,23},{8,24},{9,... | collective-permute-start | bytes 294920 | tf_op jit(solution)/shard_map/ppermute | solution.py:347
  556.0 15.4 %collective-permute-start.53 = (bf16[2,2,32,768]{3,2,0,1:T(8,128)(2,1)S(1)}, bf16[2,2,32,768]{3,2,0,1:T(8,128)(2,1)S(1)}, u32[]{:S(2)}, u32[]{:S(2)}) collective-permute-start(bf16[2,2,32,768]{3,2,0,1:T(8,128)(2,1)S(1)} %copy-done.28), channel_id=1, source_target_pairs={{0,16},{1,17},{2,18},{3,19},{4,20},{5,21},{6,22},{7,23},{8,24},{9,... | collective-permute-start | bytes 589832 | tf_op jit(solution)/shard_map/ppermute | solution.py:347
  (80 other events, 693.3 us)
Sparse Core Ops, SparseCore 0:
  55.0 125.8 all-gather.1

commit v4 on v3

--- a/solution.py
+++ b/solution.py
@@ -178,6 +178,17 @@
 WIDE = 512
 
 
+def natural(w_ref, out_ref, own):
+    width = out_ref.shape[1]
+    ratio = w_ref.shape[1] // width
+    for device in range(w_ref.shape[0] // own):
+        for block in range(ratio):
+            row = (device * ratio + block) * own
+            out_ref[row : row + own, :] = w_ref[
+                device * own : (device + 1) * own, block * width : (block + 1) * width
+            ]
+
+
 def up_kernel(x_ref, w_ref, b_ref, hidden_ref, slope_ref):
     weight = w_ref[...]
     bias = b_ref[...]
@@ -190,8 +201,9 @@
         slope_ref[at, :] = (area + pre * bell).astype(BF)
 
 
-def up_back_kernel(dz_ref, w_ref, slope_ref, du_ref, sum_ref):
-    weight = w_ref[...]
+def up_back_kernel(dz_ref, w_ref, slope_ref, du_ref, sum_ref, weight_ref, own):
+    natural(w_ref, weight_ref, own)
+    weight = weight_ref[...]
     total = jnp.zeros(sum_ref.shape, F32)
     for tile in range(dz_ref.shape[0] // TILE):
         at = slice(tile * TILE, (tile + 1) * TILE)
@@ -213,27 +225,28 @@
         out_shape=[jax.ShapeDtypeStruct((tokens, hidden), BF)] * 2, compiler_params=PARAMS)(x, packed, bias.reshape(1, hidden))
 
 
-def up_back_call(dz, weight, slope):
+def up_back_call(dz, weight, slope, own):
     tokens, width = dz.shape
     hidden = slope.shape[1]
-    halves = width // WIDE
+    sides = hidden // width
     tile = pl.BlockSpec((tokens, WIDE), lambda j: (0, j))
-    return pl.pallas_call(up_back_kernel, grid=(hidden // WIDE,), name="feed_back",
-        in_specs=[pl.BlockSpec((tokens, width), lambda j: (0, 0)), pl.BlockSpec((WIDE, width), lambda j: (j % halves, j // halves)), tile],
+    return pl.pallas_call(partial(up_back_kernel, own=own), scratch_shapes=[pltpu.VMEM((WIDE, width), BF)], grid=(hidden // WIDE,), name="feed_back",
+        in_specs=[pl.BlockSpec((tokens, width), lambda j: (0, 0)), pl.BlockSpec((WIDE // sides, hidden), lambda j: (j, 0)), tile],
         out_specs=[tile, pl.BlockSpec((1, WIDE), lambda j: (0, j))],
         out_shape=[jax.ShapeDtypeStruct((tokens, hidden), BF), jax.ShapeDtypeStruct((1, hidden), F32)], compiler_params=PARAMS)(dz, weight, slope)
 
 
 def settle_kernel(
     hidden_ref, w_ref, bias_ref, first_ref, gain_ref, shift_ref, cot_ref,
-    out_ref, grad_ref, low_ref, gain_sum, shift_sum, bias_sum,
+    out_ref, grad_ref, low_ref, gain_sum, shift_sum, bias_sum, weight_ref, own,
 ):
-    width = first_ref.shape[1]
     gain = gain_ref[...]
-    total = first_ref[...] + bias_ref[...]
-    for block in range(hidden_ref.shape[1] // width):
-        at = slice(block * width, (block + 1) * width)
-        total += matmul(hidden_ref[:, at], w_ref[:, at])
+
+    @pl.when(pl.program_id(0) == 0)
+    def _():
+        natural(w_ref, weight_ref, own)
+
+    total = first_ref[...] + bias_ref[...] + matmul(hidden_ref[...], weight_ref[...])
     output, normed, inverse = normalize(total, gain, shift_ref[...])
     out_ref[...] = output.astype(BF)
     incoming = cot_ref[...].astype(F32)
@@ -255,13 +268,14 @@
     bias_sum[...] += jnp.sum(low.astype(F32), axis=0, keepdims=True)
 
 
-def settle(hidden, packed, bias, first, gain, shift, cotangent):
+def settle(hidden, packed, bias, first, gain, shift, cotangent, own):
     tokens, width = first.shape
     units = hidden.shape[1]
     row = pl.BlockSpec((TILE, width), lambda i: (i, 0))
     vector = pl.BlockSpec((1, width), lambda i: (0, 0))
     return pl.pallas_call(
-        settle_kernel,
+        partial(settle_kernel, own=own),
+        scratch_shapes=[pltpu.VMEM((units, width), BF)],
         grid=(tokens // TILE,),
         name="settle",
         in_specs=[
@@ -464,21 +478,22 @@
     side = jnp.pad(side, ((0, 0), (0, PAIR - names - ratio)))
     head = jnp.concatenate([side, w_query, w_key, w_value], axis=1).astype(BF)
     down_side = w_down.reshape(ratio, own, width).transpose(1, 0, 2).reshape(own, ratio * width)
-    up_side = w_up.astype(BF).reshape(own, devices, ratio, own).transpose(0, 2, 1, 3)
-    later = jnp.concatenate(
-        [down_side.astype(BF), up_side.reshape(own, -1), w_out.astype(BF)], axis=1
-    )
-    head, later = gather_pairs(head, devices, later)
+    later = jnp.concatenate([down_side, w_up, w_out], axis=1).astype(BF)
+    head, (later, rows_t) = gather_pairs(head, devices, (later, rows_t))
     head = jnp.concatenate(head, axis=1)
     packed_full = head[:, PAIR:]
     query_bias, value_bias, out_bias, attn_gain, attn_shift, down_bias, ffn_gain, ffn_shift = [
         widen(head[:, i]) for i in range(names)
     ]
     up_bias = widen(head[:, names : names + ratio].reshape(-1))
-    up_bias = up_bias.reshape(devices, ratio, own).transpose(1, 0, 2).reshape(-1)
     rest = lax.all_gather(later, AXES, axis=0, tiled=True)
     units = ratio * width
     up_full, out_full = rest[:, units : 2 * units], rest[:, 2 * units :]
+    down_rows, own_rows = rest, own
+    if own % 32:
+        own_rows = 32
+        down_rows = rest[:, :units].reshape(devices, own, ratio, width).transpose(0, 2, 1, 3)
+        down_rows = down_rows.reshape(-1, ratio, own_rows, width).transpose(0, 2, 1, 3).reshape(width, units)
 
     packed_bias = jnp.concatenate([query_bias, jnp.zeros_like(query_bias), value_bias])
     packed = (matmul(rows, packed_full) + packed_bias).astype(BF)
@@ -489,19 +504,16 @@
     first_low = first.astype(BF)
     hidden, slope = up_call(first_low, rest, up_bias)
     output, grad_two, grad_branch, ffn_gain_grad, ffn_shift_grad, down_bias_grad = settle(
-        hidden, rest, down_bias, first, ffn_gain, ffn_shift, cotangent.reshape(blocks * length, width)
+        hidden, down_rows, down_bias, first, ffn_gain, ffn_shift,
+        cotangent.reshape(blocks * length, width), own_rows,
     )
     encoder_output = output.reshape(tokens.shape)
     ffn_gain_grad, ffn_shift_grad, down_bias_grad = ffn_gain_grad[0], ffn_shift_grad[0], down_bias_grad[0]
 
-    down_product = contract_rows(hidden, grad_branch).astype(BF).reshape(ratio, width, width)
-    orders = bit_orders(devices.bit_length() - 1)
-    down = [
-        Chain(down_product[p * ratio // 2 : (p + 1) * ratio // 2], orders[p], devices) for p in range(2)
-    ]
+    down = chains_of(contract_rows(hidden, grad_branch).astype(BF), devices, parts=2)
     running = list(down)
     grad_branch = tick(running, grad_branch)
-    grad_pre, up_bias_grad = up_back_call(grad_branch, rest, slope)
+    grad_pre, up_bias_grad = up_back_call(grad_branch, down_rows, slope, own_rows)
     up_bias_grad = up_bias_grad[0]
     grad_pre = tick(running, grad_pre)
     up_product = contract_rows(first_low, grad_pre).astype(BF)
@@ -541,7 +553,7 @@
         down_bias_grad, ffn_gain_grad, ffn_shift_grad,
     ]
     side_grad = jnp.concatenate(
-        [v.reshape(devices, own) for v in vector_grads] + [up_bias_grad.reshape(ratio, devices, own).transpose(1, 0, 2).reshape(devices, -1)],
+        [v.reshape(devices, own) for v in vector_grads] + [up_bias_grad.reshape(devices, own * ratio)],
         axis=1,
     )
     side = chains_of(side_grad, devices, parts=1, kind=F32)
@@ -553,9 +565,7 @@
     while not all(c.over for c in running):
         tick(running, ())
 
-    up_grad, out_grad = result(up), result(out)
-    up_grad = up_grad.reshape(own, ratio, devices, own).transpose(0, 2, 1, 3).reshape(own, -1)
-    down_grad = jnp.concatenate([c.keep for c in down], axis=0).reshape(ratio * own, width)
+    down_grad, up_grad, out_grad = result(down), result(up), result(out)
     shares = [result(share) for share in shares]
     step = width // CHUNKS
     query_grad, key_grad, value_grad = [

time: 611 us -> 595 us (0.974)
  local copies, waits for them, and re-layouts: 52.7 us -> 39.3 us
  waiting for transfers between devices: 112 us -> 121 us
    ppermute x65, waiting for transfers between devices: 89.5 us -> 98.4 us  [swap(): lax.ppermute(value, AXES, [(i, i ^ 1 << bit) for i in range(devices)])]
    reshape x5 -> x1, local copies, waits for them, and re-layouts: 7.27 us -> 0.21 us  [local(): w_down.reshape(ratio, own, width).transpose(1, 0, 2)]
    transpose x2 -> x0, local copies, waits for them, and re-layouts: 7.04 us -> none  [the longest x1 3.93 us: local(): rows_t = rows.T]
    dynamic_slice x3 -> x9, local copies, waits for them, and re-layouts: 1.3 us -> 8.28 us  [halve(): lax.dynamic_index_in_dim(t, 1 - own, axis, keepdims=False)]
  transfers between devices with their start and end apart: 66 -> 66, of which waited for: 19 -> 20; matrix products, arithmetic and copies ran while one was open for 20% -> 16% of each run, Pallas kernels for 30% -> 30%
where the time goes in v4:
time: 595 us; the launch traced here: 587 us
  Pallas kernels  218 us (37%)
  waiting for transfers between devices  121 us (20%)
  other arithmetic  72.8 us (12%)
  matrix products  61.2 us (10%)
  starting transfers between devices  58.6 us (10%)
  local copies, waits for them, and re-layouts  39.3 us (7%)
  between operations  15.9 us (3%)
    ppermute x65, waiting for transfers between devices, swap(): lax.ppermute(value, AXES, [(i, i ^ 1 << bit) for i in range(devices)])  98.4 us
    pallas_call x4, Pallas kernels, attend_back(): pl.pallas_call(backward_kernel, grid=(count,), name='attend_back', in_spe...  77 us
    ppermute x65, starting transfers between devices, swap(): lax.ppermute(value, AXES, [(i, i ^ 1 << bit) for i in range(devices)])  58.6 us
    pallas_call x1, Pallas kernels, attend(): pl.pallas_call(forward_kernel, grid=(pairs,), name='attend', in_specs=seg...  50.5 us
    convert_element_type x36, other arithmetic, halve(): self.send = send.astype(self.kind)  35.9 us
    dot_general x3, matrix products, contract_rows(): lax.dot_general(left, right, (((0,), (0,)), ((), ())), preferred_element_...  24.9 us
    dot_general x2, matrix products, contract_cols(): lax.dot_general(left, right, (((1,), (1,)), ((), ())), preferred_element_...  23.1 us
    all_gather x1, waiting for transfers between devices, local(): rest = lax.all_gather(later, AXES, axis=0, tiled=True)  23 us
  transfers between devices with their start and end apart: 66, of which 20 were waited for; matrix products, arithmetic and copies ran while one was open for 16% of the time, Pallas kernels for 30%

profile of v4, /device:TPU:0, one launch (start us, length us, event | category | flops | bytes accessed | tf_op | source)
XLA Modules:
  0.0 587.3 jit_solution(13768739564112115680)
XLA Ops:
  16.1 4.1 collective-permute-start
  40.0 8.0 %collective-permute-done.5 = bf16[2,2,32,1024]{3,2,1,0:T(8,128)(2,1)S(1)} collective-permute-done((bf16[2,2,32,1024]{3,2,1,0:T(8,128)(2,1)S(1)}, bf16[2,2,32,1024]{3,2,1,0:T(8,128)(2,1)S(1)}, u32[]{:S(2)}, u32[]{:S(2)}) %collective-permute-start.5) | collective-permute-done | bytes 262176 | tf_op jit(solution)/shard_map/ppermute | solution.py:361
  48.1 4.6 collective-permute-done.8
  54.7 14.8 %collective-permute-done.9 = bf16[2,2,2,32,1024]{4,3,0,1,2:T(8,128)(2,1)S(1)} collective-permute-done((bf16[2,2,2,32,1024]{4,3,0,1,2:T(8,128)(2,1)S(1)}, bf16[2,2,2,32,1024]{4,3,0,1,2:T(8,128)(2,1)S(1)}, u32[]{:S(2)}, u32[]{:S(2)}) %collective-permute-start.9) | collective-permute-done | bytes 524320 | tf_op jit(solution)/shard_map/ppermute | solution.py:361
  71.0 9.8 %collective-permute-done.13 = bf16[2,2,2,32,1152]{4,3,1,2,0:T(8,128)(2,1)S(1)} collective-permute-done((bf16[2,2,2,32,1152]{4,3,1,2,0:T(8,128)(2,1)S(1)}, bf16[2,2,2,32,1152]{4,3,1,2,0:T(8,128)(2,1)S(1)}, u32[]{:S(2)}, u32[]{:S(2)}) %collective-permute-start.13) | collective-permute-done | bytes 589856 | tf_op jit(solution)/shard_map/ppermute | solution.py:361
  96.7 8.6 %fusion.2.q_ref.k_ref.v_ref = bf16[1024,3072]{1,0:T(8,128)(2,1)} fusion(f32[3072]{0:T(1024)S(1)} %pad_maximum_fusion.11, bf16[1024,3200]{1,0:T(8,128)(2,1)S(1)} %pad_maximum_fusion.refs_1_, bf16[1,1024,1024]{2,1,0:T(8,128)(2,1)S(1)} %copy-done.11), kind=kOutput, calls=%fused_computation.6 | convolution fusion | flops 6448742400 | bytes 14692352 | tf_op jit(solution)/shard_map/dot_general | solution.py:25
  105.3 50.5 %attend.1 = (bf16[1024,1024]{1,0:T(8,128)(2,1)}, f32[8,2,1024]{2,1,0:T(2,128)}) custom-call(s32[1024,1]{1,0:T(8,128)} %copy.168.seg_col, s32[1,1024]{1,0:T(1,128)} %seg_row.9, bf16[1024,3072]{1,0:T(8,128)(2,1)} %fusion.2.q_ref.k_ref.v_ref, bf16[1024,3072]{1,0:T(8,128)(2,1)} %fusion.2.q_ref.k_ref.v_ref, bf16[1024,3072]{1,0:T(8,128)(2,1)} %fusion.2.q_ref.k_ref.v_ref), custom_call_target="tpu_custom_call" | custom-call | tf_op jit(solution)/shard_map/attend/pallas_call | solution.py:136
  155.8 23.0 %all-gather.2.cloned.1.call-done.w_ref = bf16[1024,9216]{1,0:T(8,128)(2,1)} async-done(((bf16[32,9216]{1,0:T(8,128)(2,1)}), bf16[1024,9216]{1,0:T(8,128)(2,1)}) %all-gather.2.cloned.1.call-update) | async-done | bytes 18874384 | tf_op jit(solution)/shard_map/all_gather | solution.py:489
  178.8 4.7 fusion.81
  189.1 20.0 %feed.1 = (bf16[1024,4096]{1,0:T(8,128)(2,1)}, bf16[1024,4096]{1,0:T(8,128)(2,1)}) custom-call(bf16[1024,1024]{1,0:T(8,128)(2,1)} %get-tuple-element.371.x_ref, bf16[1024,9216]{1,0:T(8,128)(2,1)} %all-gather.2.cloned.1.call-done.w_ref, f32[1,4096]{1,0:T(1,128)} %reshape.1345.b_ref), custom_call_target="tpu_custom_call" | custom-call | tf_op jit(solution)/shard_map/feed/pallas_call | solution.py:220
  209.1 20.0 %settle.1 = (bf16[1024,1024]{1,0:T(8,128)(2,1)}, f32[1024,1024]{1,0:T(8,128)}, bf16[1024,1024]{1,0:T(8,128)(2,1)}, f32[1,1024]{1,0:T(1,128)}, f32[1,1024]{1,0:T(1,128)}, /*index=5*/f32[1,1024]{1,0:T(1,128)}) custom-call(bf16[1024,4096]{1,0:T(8,128)(2,1)} %get-tuple-element.192.hidden_ref, bf16[1024,9216]{1,0:T(8,128)(2,1)} %all-gather.2.cloned.1.call-done.w_ref, ...), custom_call_target="tpu_custom_call" | custom-call | tf_op jit(solution)/shard_map/settle/pallas_call | solution.py:276
  229.1 12.9 %convolution_convert_fusion.1 = bf16[4096,1024]{1,0:T(8,128)(2,1)S(1)} fusion(bf16[1024,4096]{1,0:T(8,128)(2,1)} %get-tuple-element.192.hidden_ref, bf16[1024,1024]{1,0:T(8,128)(2,1)} %get-tuple-element.196.dz_ref), kind=kOutput, calls=%fused_computation.4 | convolution fusion | flops 8594128896 | bytes 18874368 | tf_op jit(solution)/shard_map/dot_general | solution.py:29
  249.0 16.7 %feed_back.1 = (bf16[1024,4096]{1,0:T(8,128)(2,1)}, f32[1,4096]{1,0:T(1,128)}) custom-call(bf16[1024,1024]{1,0:T(8,128)(2,1)} %get-tuple-element.196.dz_ref, bf16[1024,9216]{1,0:T(8,128)(2,1)} %all-gather.2.cloned.1.call-done.w_ref, bf16[1024,4096]{1,0:T(8,128)(2,1)} %get-tuple-element.197.slope_ref), custom_call_target="tpu_custom_call" | custom-call | tf_op jit(solution)/shard_map/feed_back/pallas_call | solution.py:233
  269.1 4.5 fusion.14
  275.7 9.6 %convolution_convert_fusion = bf16[1024,4096]{1,0:T(8,128)(2,1)S(1)} fusion(bf16[1024,1024]{1,0:T(8,128)(2,1)S(1)} %copy-done.4, bf16[1024,4096]{1,0:T(8,128)(2,1)S(1)} %copy-done.43), kind=kOutput, calls=%fused_computation.3 | convolution fusion | flops 8594128896 | bytes 18874368 | tf_op jit(solution)/shard_map/dot_general | solution.py:29
  292.8 6.5 %collective-permute-done.17 = bf16[2,2,2,128,512]{4,3,0,1,2:T(8,128)(2,1)} collective-permute-done((bf16[2,2,2,128,512]{4,3,0,1,2:T(8,128)(2,1)}, bf16[2,2,2,128,512]{4,3,0,1,2:T(8,128)(2,1)}, u32[]{:S(2)}, u32[]{:S(2)}) %collective-permute-start.17) | collective-permute-done | bytes 1048608 | tf_op jit(solution)/shard_map/ppermute | solution.py:361
  304.1 17.8 %multiply_reduce_fusion = (f32[1024]{0:T(1024)}, f32[1024]{0:T(1024)S(1)}, f32[1024]{0:T(1024)S(1)}, f32[1024]{0:T(1024)}, f32[1024,1024]{1,0:T(8,128)}) fusion(f32[1024,1024]{1,0:T(8,128)S(1)} %copy-done.1, f32[1024]{0:T(1024)S(1)} %add_rsqrt_fusion, f32[1024]{0:T(1024)S(1)} %broadcast_multiply_fusion.2, f32[1024]{0:T(1024)S(1)} %get-tuple-element.365, ...), kind=kOutput, calls=%fused_computation.9 | convolution fusion | flops 8600416256 | bytes 29388800 | tf_op jit(solution)/shard_map/dot_general | solution.py:33
  331.7 5.3 convolution_convert_fusion.3.do_ref
  347.3 3.9 copy.181.rows_t_ref
  351.3 19.5 %attend_back.4 = (bf16[3,1024,256]{2,1,0:T(8,128)(2,1)}, f32[1,256]{1,0:T(1,128)}, f32[1,256]{1,0:T(1,128)}) custom-call(s32[1024,1]{1,0:T(8,128)} %copy.168.seg_col, s32[1,1024]{1,0:T(1,128)} %seg_row.9, bf16[1024,3072]{1,0:T(8,128)(2,1)} %fusion.2.q_ref.k_ref.v_ref, bf16[1024,3072]{1,0:T(8,128)(2,1)} %fusion.2.q_ref.k_ref.v_ref, ...), custom_call_target="tpu_custom_call" | custom-call | tf_op jit(solution)/shard_map/attend_back/pallas_call | solution.py:158
  370.8 5.5 weight_halves.4
  392.6 19.1 %attend_back.5 = (bf16[3,1024,256]{2,1,0:T(8,128)(2,1)}, f32[1,256]{1,0:T(1,128)}, f32[1,256]{1,0:T(1,128)}) custom-call(s32[1024,1]{1,0:T(8,128)} %copy.168.seg_col, s32[1,1024]{1,0:T(1,128)} %seg_row.9, bf16[1024,3072]{1,0:T(8,128)(2,1)} %fusion.2.q_ref.k_ref.v_ref, bf16[1024,3072]{1,0:T(8,128)(2,1)} %fusion.2.q_ref.k_ref.v_ref, ...), custom_call_target="tpu_custom_call" | custom-call | tf_op jit(solution)/shard_map/attend_back/pallas_call | solution.py:158
  413.9 5.4 weight_halves.5
  419.5 16.8 %collective-permute-done.30 = bf16[2,2,32,2048]{3,2,0,1:T(8,128)(2,1)S(1)} collective-permute-done((bf16[2,2,32,2048]{3,2,0,1:T(8,128)(2,1)S(1)}, bf16[2,2,32,2048]{3,2,0,1:T(8,128)(2,1)S(1)}, u32[]{:S(2)}, u32[]{:S(2)}) %collective-permute-start.30) | collective-permute-done | bytes 524320 | tf_op jit(solution)/shard_map/ppermute | solution.py:361
  438.6 19.2 %attend_back.6 = (bf16[3,1024,256]{2,1,0:T(8,128)(2,1)}, f32[1,256]{1,0:T(1,128)}, f32[1,256]{1,0:T(1,128)}) custom-call(s32[1024,1]{1,0:T(8,128)} %copy.168.seg_col, s32[1,1024]{1,0:T(1,128)} %seg_row.9, bf16[1024,3072]{1,0:T(8,128)(2,1)} %fusion.2.q_ref.k_ref.v_ref, bf16[1024,3072]{1,0:T(8,128)(2,1)} %fusion.2.q_ref.k_ref.v_ref, ...), custom_call_target="tpu_custom_call" | custom-call | tf_op jit(solution)/shard_map/attend_back/pallas_call | solution.py:158
  460.6 5.4 weight_halves.6
  478.6 19.2 %attend_back.7 = (bf16[3,1024,256]{2,1,0:T(8,128)(2,1)}, f32[1,256]{1,0:T(1,128)}, f32[1,256]{1,0:T(1,128)}) custom-call(s32[1024,1]{1,0:T(8,128)} %copy.168.seg_col, s32[1,1024]{1,0:T(1,128)} %seg_row.9, bf16[1024,3072]{1,0:T(8,128)(2,1)} %fusion.2.q_ref.k_ref.v_ref, bf16[1024,3072]{1,0:T(8,128)(2,1)} %fusion.2.q_ref.k_ref.v_ref, ...), custom_call_target="tpu_custom_call" | custom-call | tf_op jit(solution)/shard_map/attend_back/pallas_call | solution.py:158
  502.6 5.4 weight_halves.7
  523.8 4.2 collective-permute-done.47
  528.0 7.7 %collective-permute-done.48 = bf16[2,2,2,32,768]{4,3,1,2,0:T(8,128)(2,1)S(1)} collective-permute-done((bf16[2,2,2,32,768]{4,3,1,2,0:T(8,128)(2,1)S(1)}, bf16[2,2,2,32,768]{4,3,1,2,0:T(8,128)(2,1)S(1)}, u32[]{:S(2)}, u32[]{:S(2)}) %collective-permute-start.48) | collective-permute-done | bytes 393248 | tf_op jit(solution)/shard_map/ppermute | solution.py:361
  543.6 12.2 %input_grad.1 = bf16[1024,1024]{1,0:T(8,128)(2,1)} custom-call(f32[1024,1024]{1,0:T(8,128)} %copy-done.3, bf16[1024,3200]{1,0:T(8,128)(2,1)} %copy-done.2, bf16[3,1024,256]{2,1,0:T(8,128)(2,1)} %get-tuple-element.315.part_ref.refs_2_, bf16[3,1024,256]{2,1,0:T(8,128)(2,1)} %get-tuple-element.316.part_ref.refs_3_, ...), custom_call_target="tpu_custom_call" | custom-call | tf_op jit(solution)/shard_map/input_grad/pallas_call | solution.py:348
  560.3 3.9 collective-permute-done.59
  (398 shorter events, 182.8 us)
Async XLA Ops:
  7.2 171.6 %all-gather.2.cloned.1.call-start = ((), (), s32[]{:S(2)}) async-start(), calls=%async_computation | async-start | bytes 19464192 | tf_op jit(solution)/shard_map/all_gather | solution.py:489
  37.3 15.4 %collective-permute-start.8 = (bf16[2,2,32,1152]{3,2,0,1:T(8,128)(2,1)S(1)}, bf16[2,2,32,1152]{3,2,0,1:T(8,128)(2,1)S(1)}, u32[]{:S(2)}, u32[]{:S(2)}) collective-permute-start(bf16[2,2,32,1152]{3,2,0,1:T(8,128)(2,1)S(1)} %maximum_select_fusion.12), channel_id=1, source_target_pairs={{0,16},{1,17},{2,18},{3,19},{4,20},{5,21},{6,22},{7,23},{8,24},{9,... | collective-permute-start | bytes 884744 | tf_op jit(solution)/shard_map/ppermute | solution.py:361
  52.8 16.8 %collective-permute-start.9 = (bf16[2,2,2,32,1024]{4,3,0,1,2:T(8,128)(2,1)S(1)}, bf16[2,2,2,32,1024]{4,3,0,1,2:T(8,128)(2,1)S(1)}, u32[]{:S(2)}, u32[]{:S(2)}) collective-permute-start(bf16[2,2,2,32,1024]{4,3,0,1,2:T(8,128)(2,1)S(1)} %maximum_select_fusion.9), channel_id=1, source_target_pairs={{0,2},{1,3},{2,0},{3,1},{4,6},{5,7},{6,4},{7,5},{8,10},{9,11},{10,... | collective-permute-start | bytes 1572872 | tf_op jit(solution)/shard_map/ppermute | solution.py:361
  53.4 16.4 %collective-permute-start.11 = (bf16[2,2,2,32,1024]{4,3,2,0,1:T(8,128)(2,1)S(1)}, bf16[2,2,2,32,1024]{4,3,2,0,1:T(8,128)(2,1)S(1)}, u32[]{:S(2)}, u32[]{:S(2)}) collective-permute-start(bf16[2,2,2,32,1024]{4,3,2,0,1:T(8,128)(2,1)S(1)} %maximum_select_fusion.10), channel_id=1, source_target_pairs={{0,4},{1,5},{2,6},{3,7},{4,0},{5,1},{6,2},{7,3},{8,12},{9,13},{10,... | collective-permute-start | bytes 1572872 | tf_op jit(solution)/shard_map/ppermute | solution.py:361
  54.7 26.0 %collective-permute-start.13 = (bf16[2,2,2,32,1152]{4,3,1,2,0:T(8,128)(2,1)S(1)}, bf16[2,2,2,32,1152]{4,3,1,2,0:T(8,128)(2,1)S(1)}, u32[]{:S(2)}, u32[]{:S(2)}) collective-permute-start(bf16[2,2,2,32,1152]{4,3,1,2,0:T(8,128)(2,1)S(1)} %maximum_select_fusion.8), channel_id=1, source_target_pairs={{0,8},{1,9},{2,10},{3,11},{4,12},{5,13},{6,14},{7,15},{8,0},{9,1},... | collective-permute-start | bytes 1769480 | tf_op jit(solution)/shard_map/ppermute | solution.py:361
  248.5 17.2 %collective-permute-start.15 = (bf16[2,2,2,2,128,512]{5,4,0,1,2,3:T(8,128)(2,1)S(1)}, bf16[2,2,2,2,128,512]{5,4,0,1,2,3:T(8,128)(2,1)}, u32[]{:S(2)}, u32[]{:S(2)}) collective-permute-start(bf16[2,2,2,2,128,512]{5,4,0,1,2,3:T(8,128)(2,1)S(1)} %bitcast.375), channel_id=1, source_target_pairs={{0,1},{1,0},{2,3},{3,2},{4,5},{5,4},{6,7},{7,6},{8,9},{9,8},{10,11... | collective-permute-start | bytes 6291464 | tf_op jit(solution)/shard_map/ppermute | solution.py:361
  248.8 20.3 %collective-permute-start.16 = (bf16[2,2,2,2,128,512]{5,4,3,0,1,2:T(8,128)(2,1)}, bf16[2,2,2,2,128,512]{5,4,3,0,1,2:T(8,128)(2,1)}, u32[]{:S(2)}, u32[]{:S(2)}) collective-permute-start(bf16[2,2,2,2,128,512]{5,4,3,0,1,2:T(8,128)(2,1)} %bitcast.338), channel_id=1, source_target_pairs={{0,1},{1,0},{2,3},{3,2},{4,5},{5,4},{6,7},{7,6},{8,9},{9,8},{10,11... | collective-permute-start | bytes 6291464 | tf_op jit(solution)/shard_map/ppermute | solution.py:361
  273.6 25.6 %collective-permute-start.17 = (bf16[2,2,2,128,512]{4,3,0,1,2:T(8,128)(2,1)}, bf16[2,2,2,128,512]{4,3,0,1,2:T(8,128)(2,1)}, u32[]{:S(2)}, u32[]{:S(2)}) collective-permute-start(bf16[2,2,2,128,512]{4,3,0,1,2:T(8,128)(2,1)} %get-tuple-element.205), channel_id=1, source_target_pairs={{0,2},{1,3},{2,0},{3,1},{4,6},{5,7},{6,4},{7,5},{8,10},{9,11},{10,... | collective-permute-start | bytes 3145736 | tf_op jit(solution)/shard_map/ppermute | solution.py:361
  275.1 26.6 %collective-permute-start.18 = (bf16[2,2,2,128,512]{4,3,2,0,1:T(8,128)(2,1)}, bf16[2,2,2,128,512]{4,3,2,0,1:T(8,128)(2,1)}, u32[]{:S(2)}, u32[]{:S(2)}) collective-permute-start(bf16[2,2,2,128,512]{4,3,2,0,1:T(8,128)(2,1)} %get-tuple-element.207), channel_id=1, source_target_pairs={{0,4},{1,5},{2,6},{3,7},{4,0},{5,1},{6,2},{7,3},{8,12},{9,13},{10,... | collective-permute-start | bytes 3145736 | tf_op jit(solution)/shard_map/ppermute | solution.py:361
  321.9 15.1 %collective-permute-start.19 = (bf16[2,2,128,512]{3,2,0,1:T(8,128)(2,1)}, bf16[2,2,128,512]{3,2,0,1:T(8,128)(2,1)S(1)}, u32[]{:S(2)}, u32[]{:S(2)}) collective-permute-start(bf16[2,2,128,512]{3,2,0,1:T(8,128)(2,1)} %get-tuple-element.210), channel_id=1, source_target_pairs={{0,4},{1,5},{2,6},{3,7},{4,0},{5,1},{6,2},{7,3},{8,12},{9,13},{10,... | collective-permute-start | bytes 1572872 | tf_op jit(solution)/shard_map/ppermute | solution.py:361
  323.8 15.2 %collective-permute-start.21 = (bf16[2,2,2,2,32,2048]{5,4,2,3,0,1:T(8,128)(2,1)S(1)}, bf16[2,2,2,2,32,2048]{5,4,2,3,0,1:T(8,128)(2,1)S(1)}, u32[]{:S(2)}, u32[]{:S(2)}) collective-permute-start(bf16[2,2,2,2,32,2048]{5,4,2,3,0,1:T(8,128)(2,1)S(1)} %bitcast.374), channel_id=1, source_target_pairs={{0,1},{1,0},{2,3},{3,2},{4,5},{5,4},{6,7},{7,6},{8,9},{9,8},{10,11... | collective-permute-start | bytes 6291464 | tf_op jit(solution)/shard_map/ppermute | solution.py:361
  323.8 16.8 %collective-permute-start.22 = (bf16[2,2,2,2,32,2048]{5,4,0,1,2,3:T(8,128)(2,1)S(1)}, bf16[2,2,2,2,32,2048]{5,4,0,1,2,3:T(8,128)(2,1)S(1)}, u32[]{:S(2)}, u32[]{:S(2)}) collective-permute-start(bf16[2,2,2,2,32,2048]{5,4,0,1,2,3:T(8,128)(2,1)S(1)} %bitcast.373), channel_id=1, source_target_pairs={{0,1},{1,0},{2,3},{3,2},{4,5},{5,4},{6,7},{7,6},{8,9},{9,8},{10,11... | collective-permute-start | bytes 6291464 | tf_op jit(solution)/shard_map/ppermute | solution.py:361
  343.0 39.4 %collective-permute-start.25 = (bf16[2,2,2,32,2048]{4,3,1,2,0:T(8,128)(2,1)}, bf16[2,2,2,32,2048]{4,3,1,2,0:T(8,128)(2,1)}, u32[]{:S(2)}, u32[]{:S(2)}) collective-permute-start(bf16[2,2,2,32,2048]{4,3,1,2,0:T(8,128)(2,1)} %get-tuple-element.229), channel_id=1, source_target_pairs={{0,8},{1,9},{2,10},{3,11},{4,12},{5,13},{6,14},{7,15},{8,0},{9,1},... | collective-permute-start | bytes 3145736 | tf_op jit(solution)/shard_map/ppermute | solution.py:361
  344.6 40.2 %collective-permute-start.26 = (bf16[2,2,2,32,2048]{4,3,0,1,2:T(8,128)(2,1)}, bf16[2,2,2,32,2048]{4,3,0,1,2:T(8,128)(2,1)}, u32[]{:S(2)}, u32[]{:S(2)}) collective-permute-start(bf16[2,2,2,32,2048]{4,3,0,1,2:T(8,128)(2,1)} %get-tuple-element.231), channel_id=1, source_target_pairs={{0,2},{1,3},{2,0},{3,1},{4,6},{5,7},{6,4},{7,5},{8,10},{9,11},{10,... | collective-permute-start | bytes 3145736 | tf_op jit(solution)/shard_map/ppermute | solution.py:361
  345.2 41.9 %collective-permute-start.27 = (bf16[2,2,2,2,32,1024]{5,4,2,3,0,1:T(8,128)(2,1)}, bf16[2,2,2,2,32,1024]{5,4,2,3,0,1:T(8,128)(2,1)}, u32[]{:S(2)}, u32[]{:S(2)}) collective-permute-start(bf16[2,2,2,2,32,1024]{5,4,2,3,0,1:T(8,128)(2,1)} %bitcast.342), channel_id=1, source_target_pairs={{0,1},{1,0},{2,3},{3,2},{4,5},{5,4},{6,7},{7,6},{8,9},{9,8},{10,11... | collective-permute-start | bytes 3145736 | tf_op jit(solution)/shard_map/ppermute | solution.py:361
  345.2 34.5 %collective-permute-start.23 = (bf16[2,128,512]{2,1,0:T(8,128)(2,1)S(1)}, bf16[2,128,512]{2,1,0:T(8,128)(2,1)}, u32[]{:S(2)}, u32[]{:S(2)}) collective-permute-start(bf16[2,128,512]{2,1,0:T(8,128)(2,1)S(1)} %get-tuple-element.225), channel_id=1, source_target_pairs={{0,8},{1,9},{2,10},{3,11},{4,12},{5,13},{6,14},{7,15},{8,0},{9,1},... | collective-permute-start | bytes 786440 | tf_op jit(solution)/shard_map/ppermute | solution.py:361
  345.6 35.8 %collective-permute-start.24 = (bf16[2,128,512]{2,1,0:T(8,128)(2,1)}, bf16[2,128,512]{2,1,0:T(8,128)(2,1)}, u32[]{:S(2)}, u32[]{:S(2)}) collective-permute-start(bf16[2,128,512]{2,1,0:T(8,128)(2,1)} %get-tuple-element.227), channel_id=1, source_target_pairs={{0,16},{1,17},{2,18},{3,19},{4,20},{5,21},{6,22},{7,23},{8,24},{9,... | collective-permute-start | bytes 786440 | tf_op jit(solution)/shard_map/ppermute | solution.py:361
  389.5 29.8 %collective-permute-start.28 = (bf16[128,512]{1,0:T(8,128)(2,1)}, bf16[128,512]{1,0:T(8,128)(2,1)S(1)}, u32[]{:S(2)}, u32[]{:S(2)}) collective-permute-start(bf16[128,512]{1,0:T(8,128)(2,1)} %get-tuple-element.244), channel_id=1, source_target_pairs={{0,16},{1,17},{2,18},{3,19},{4,20},{5,21},{6,22},{7,23},{8,24},{9,... | collective-permute-start | bytes 393224 | tf_op jit(solution)/shard_map/ppermute | solution.py:361
  390.3 29.0 %collective-permute-start.32 = (bf16[2,2,2,32,1024]{4,3,1,2,0:T(8,128)(2,1)}, bf16[2,2,2,32,1024]{4,3,1,2,0:T(8,128)(2,1)S(1)}, u32[]{:S(2)}, u32[]{:S(2)}) collective-permute-start(bf16[2,2,2,32,1024]{4,3,1,2,0:T(8,128)(2,1)} %get-tuple-element.252), channel_id=1, source_target_pairs={{0,8},{1,9},{2,10},{3,11},{4,12},{5,13},{6,14},{7,15},{8,0},{9,1},... | collective-permute-start | bytes 1572872 | tf_op jit(solution)/shard_map/ppermute | solution.py:361
  412.3 24.1 %collective-permute-start.30 = (bf16[2,2,32,2048]{3,2,0,1:T(8,128)(2,1)S(1)}, bf16[2,2,32,2048]{3,2,0,1:T(8,128)(2,1)S(1)}, u32[]{:S(2)}, u32[]{:S(2)}) collective-permute-start(bf16[2,2,32,2048]{3,2,0,1:T(8,128)(2,1)S(1)} %copy-done.25), channel_id=1, source_target_pairs={{0,16},{1,17},{2,18},{3,19},{4,20},{5,21},{6,22},{7,23},{8,24},{9,... | collective-permute-start | bytes 1572872 | tf_op jit(solution)/shard_map/ppermute | solution.py:361
  412.4 24.1 %collective-permute-start.31 = (bf16[2,2,32,2048]{3,2,0,1:T(8,128)(2,1)}, bf16[2,2,32,2048]{3,2,0,1:T(8,128)(2,1)S(1)}, u32[]{:S(2)}, u32[]{:S(2)}) collective-permute-start(bf16[2,2,32,2048]{3,2,0,1:T(8,128)(2,1)} %get-tuple-element.250), channel_id=1, source_target_pairs={{0,4},{1,5},{2,6},{3,7},{4,0},{5,1},{6,2},{7,3},{8,12},{9,13},{10,... | collective-permute-start | bytes 1572872 | tf_op jit(solution)/shard_map/ppermute | solution.py:361
  419.3 17.3 %collective-permute-start.33 = (bf16[2,2,2,2,32,768]{5,4,0,1,2,3:T(8,128)(2,1)S(1)}, bf16[2,2,2,2,32,768]{5,4,0,1,2,3:T(8,128)(2,1)S(1)}, u32[]{:S(2)}, u32[]{:S(2)}) collective-permute-start(bf16[2,2,2,2,32,768]{5,4,0,1,2,3:T(8,128)(2,1)S(1)} %copy.184), channel_id=1, source_target_pairs={{0,1},{1,0},{2,3},{3,2},{4,5},{5,4},{6,7},{7,6},{8,9},{9,8},{10,11... | collective-permute-start | bytes 2359304 | tf_op jit(solution)/shard_map/ppermute | solution.py:361
  436.8 29.2 %collective-permute-start.34 = (bf16[2,32,2048]{2,1,0:T(8,128)(2,1)S(1)}, bf16[2,32,2048]{2,1,0:T(8,128)(2,1)S(1)}, u32[]{:S(2)}, u32[]{:S(2)}) collective-permute-start(bf16[2,32,2048]{2,1,0:T(8,128)(2,1)S(1)} %get-tuple-element.264), channel_id=1, source_target_pairs={{0,2},{1,3},{2,0},{3,1},{4,6},{5,7},{6,4},{7,5},{8,10},{9,11},{10,... | collective-permute-start | bytes 786440 | tf_op jit(solution)/shard_map/ppermute | solution.py:361
  438.4 32.4 %collective-permute-start.38 = (bf16[2,2,2,2,32,768]{5,4,3,0,1,2:T(8,128)(2,1)S(1)}, bf16[2,2,2,2,32,768]{5,4,3,0,1,2:T(8,128)(2,1)S(1)}, u32[]{:S(2)}, u32[]{:S(2)}) collective-permute-start(bf16[2,2,2,2,32,768]{5,4,3,0,1,2:T(8,128)(2,1)S(1)} %copy.189), channel_id=1, source_target_pairs={{0,1},{1,0},{2,3},{3,2},{4,5},{5,4},{6,7},{7,6},{8,9},{9,8},{10,11... | collective-permute-start | bytes 2359304 | tf_op jit(solution)/shard_map/ppermute | solution.py:361
  438.5 28.2 %collective-permute-start.36 = (bf16[2,2,32,1024]{3,2,0,1:T(8,128)(2,1)S(1)}, bf16[2,2,32,1024]{3,2,0,1:T(8,128)(2,1)S(1)}, u32[]{:S(2)}, u32[]{:S(2)}) collective-permute-start(bf16[2,2,32,1024]{3,2,0,1:T(8,128)(2,1)S(1)} %get-tuple-element.268), channel_id=1, source_target_pairs={{0,16},{1,17},{2,18},{3,19},{4,20},{5,21},{6,22},{7,23},{8,24},{9,... | collective-permute-start | bytes 786440 | tf_op jit(solution)/shard_map/ppermute | solution.py:361
  471.8 38.8 %collective-permute-start.39 = (bf16[32,2048]{1,0:T(8,128)(2,1)}, bf16[32,2048]{1,0:T(8,128)(2,1)}, u32[]{:S(2)}, u32[]{:S(2)}) collective-permute-start(bf16[32,2048]{1,0:T(8,128)(2,1)} %get-tuple-element.278), channel_id=1, source_target_pairs={{0,4},{1,5},{2,6},{3,7},{4,0},{5,1},{6,2},{7,3},{8,12},{9,13},{10,... | collective-permute-start | bytes 393224 | tf_op jit(solution)/shard_map/ppermute | solution.py:361
  516.0 19.8 %collective-permute-start.49 = (bf16[2,2,2,2,32,768]{5,4,0,1,2,3:T(8,128)(2,1)S(1)}, bf16[2,2,2,2,32,768]{5,4,0,1,2,3:T(8,128)(2,1)S(1)}, u32[]{:S(2)}, u32[]{:S(2)}) collective-permute-start(bf16[2,2,2,2,32,768]{5,4,0,1,2,3:T(8,128)(2,1)S(1)} %copy.207), channel_id=1, source_target_pairs={{0,1},{1,0},{2,3},{3,2},{4,5},{5,4},{6,7},{7,6},{8,9},{9,8},{10,11... | collective-permute-start | bytes 2359304 | tf_op jit(solution)/shard_map/ppermute | solution.py:361
  520.3 15.5 %collective-permute-start.48 = (bf16[2,2,2,32,768]{4,3,1,2,0:T(8,128)(2,1)S(1)}, bf16[2,2,2,32,768]{4,3,1,2,0:T(8,128)(2,1)S(1)}, u32[]{:S(2)}, u32[]{:S(2)}) collective-permute-start(bf16[2,2,2,32,768]{4,3,1,2,0:T(8,128)(2,1)S(1)} %get-tuple-element.310), channel_id=1, source_target_pairs={{0,8},{1,9},{2,10},{3,11},{4,12},{5,13},{6,14},{7,15},{8,0},{9,1},... | collective-permute-start | bytes 1179656 | tf_op jit(solution)/shard_map/ppermute | solution.py:361
  536.0 19.8 %collective-permute-start.55 = (f32[2,2,2,1,384]{4,1,0,3,2:T(2,128)S(1)}, f32[2,2,2,1,384]{4,1,0,3,2:T(2,128)S(1)}, u32[]{:S(2)}, u32[]{:S(2)}) collective-permute-start(f32[2,2,2,1,384]{4,1,0,3,2:T(2,128)S(1)} %copy.210), channel_id=1, source_target_pairs={{0,2},{1,3},{2,0},{3,1},{4,6},{5,7},{6,4},{7,5},{8,10},{9,11},{10,... | collective-permute-start | bytes 36872 | tf_op jit(solution)/shard_map/ppermute | solution.py:361
  538.2 17.6 %collective-permute-start.51 = (bf16[32,768]{1,0:T(8,128)(2,1)S(1)}, bf16[32,768]{1,0:T(8,128)(2,1)S(1)}, u32[]{:S(2)}, u32[]{:S(2)}) collective-permute-start(bf16[32,768]{1,0:T(8,128)(2,1)S(1)} %get-tuple-element.320), channel_id=1, source_target_pairs={{0,16},{1,17},{2,18},{3,19},{4,20},{5,21},{6,22},{7,23},{8,24},{9,... | collective-permute-start | bytes 147464 | tf_op jit(solution)/shard_map/ppermute | solution.py:361
  539.9 15.9 %collective-permute-start.52 = (bf16[2,32,768]{2,1,0:T(8,128)(2,1)S(1)}, bf16[2,32,768]{2,1,0:T(8,128)(2,1)S(1)}, u32[]{:S(2)}, u32[]{:S(2)}) collective-permute-start(bf16[2,32,768]{2,1,0:T(8,128)(2,1)S(1)} %get-tuple-element.322), channel_id=1, source_target_pairs={{0,16},{1,17},{2,18},{3,19},{4,20},{5,21},{6,22},{7,23},{8,24},{9,... | collective-permute-start | bytes 294920 | tf_op jit(solution)/shard_map/ppermute | solution.py:361
  541.1 14.9 %collective-permute-start.53 = (bf16[2,2,32,768]{3,2,0,1:T(8,128)(2,1)S(1)}, bf16[2,2,32,768]{3,2,0,1:T(8,128)(2,1)S(1)}, u32[]{:S(2)}, u32[]{:S(2)}) collective-permute-start(bf16[2,2,32,768]{3,2,0,1:T(8,128)(2,1)S(1)} %get-tuple-element.324), channel_id=1, source_target_pairs={{0,16},{1,17},{2,18},{3,19},{4,20},{5,21},{6,22},{7,23},{8,24},{9,... | collective-permute-start | bytes 589832 | tf_op jit(solution)/shard_map/ppermute | solution.py:361
  (79 other events, 742.4 us)
Sparse Core Ops, SparseCore 0:
  52.9 125.8 all-gather.1

commit v5 on v4

--- a/solution.py
+++ b/solution.py
@@ -129,6 +129,65 @@
 PARAMS = pltpu.CompilerParams(dimension_semantics=("arbitrary",), vmem_limit_bytes=56 * 2**20)
 
 
+def turn_kernel(x_ref, out_ref):
+    out_ref[...] = x_ref[...].T
+
+
+def turned(rows):
+    tokens, width = rows.shape
+    return pl.pallas_call(
+        turn_kernel,
+        grid=(tokens // TILE,),
+        name="turned",
+        in_specs=[pl.BlockSpec((TILE, width), lambda i: (i, 0))],
+        out_specs=pl.BlockSpec((width, TILE), lambda i: (0, i)),
+        out_shape=jax.ShapeDtypeStruct((width, tokens), rows.dtype),
+        compiler_params=PARAMS,
+    )(rows)
+
+
+def project_kernel(own_ref, rows_ref, *refs):
+    halves, bias_ref, out_ref, weight_ref = refs[:6], refs[6], refs[7], refs[8]
+    groups, share, width = halves[0].shape
+
+    @pl.when(pl.program_id(0) == 0)
+    def _():
+        for part in range(3):
+            for side in range(2):
+                place = own_ref[0] if side == 0 else 1 - own_ref[0]
+                for group in range(groups):
+                    row = pl.multiple_of((group * 2 + place) * share, share)
+                    weight_ref[pl.ds(row, share), part * width : (part + 1) * width] = halves[
+                        part * 2 + side
+                    ][group]
+
+    out_ref[...] = (matmul(rows_ref[...], weight_ref[...]) + bias_ref[...]).astype(BF)
+
+
+def project(rows, halves, bias):
+    tokens, width = rows.shape
+    own = (lax.axis_index(AXES) & 1).astype(jnp.int32).reshape(1)
+    flat = [half for pair in halves for half in pair]
+    whole = pl.BlockSpec(flat[0].shape, lambda i: (0, 0, 0))
+    return pl.pallas_call(
+        project_kernel,
+        grid=(tokens // TILE,),
+        name="project",
+        in_specs=[pl.BlockSpec(memory_space=pltpu.SMEM), pl.BlockSpec((TILE, width), lambda i: (i, 0))]
+        + [whole] * 6
+        + [pl.BlockSpec((1, 3 * width), lambda i: (0, 0))],
+        out_specs=[
+            pl.BlockSpec((TILE, 3 * width), lambda i: (i, 0)),
+            pl.BlockSpec((width, 3 * width), lambda i: (0, 0)),
+        ],
+        out_shape=[
+            jax.ShapeDtypeStruct((tokens, 3 * width), BF),
+            jax.ShapeDtypeStruct((width, 3 * width), BF),
+        ],
+        compiler_params=PARAMS,
+    )(own, rows, *flat, bias.reshape(1, -1))
+
+
 def attend(segments, packed):
     tokens = packed.shape[0]
     width = packed.shape[1] // 3
@@ -336,7 +395,7 @@
     total = base_ref[...]
     for i, ref in enumerate(pieces):
         for part in range(3):
-            first = PAIR + part * width + i * step
+            first = part * width + i * step
             total += contract_cols(ref[part], weight_ref[:, first : first + step])
     out_ref[...] = total.astype(BF)
 
@@ -438,14 +497,21 @@
     return jnp.concatenate([c.keep for c in chains], axis=1)
 
 
-def gather_pairs(value, devices, later, parts=3):
+def join(halves, axis):
+    mine, got = halves
+    own = lax.axis_index(AXES) & 1
+    return jnp.where(own == 0, jnp.stack([mine, got], axis), jnp.stack([got, mine], axis))
+
+
+def gather_halves(values, devices, later):
     bits = devices.bit_length() - 1
     here = lax.axis_index(AXES)
     orders = [order[::-1] for order in bit_orders(bits)]
-    work = [value[:, a:b] for a, b in spans(value.shape[1], parts)]
-    held = [[] for _ in range(parts)]
-    for step in range(bits):
-        for p in range(parts):
+    orders = [orders[p % 3] for p in range(len(values))]
+    work = list(values)
+    held = [[] for _ in values]
+    for step in range(bits - 1):
+        for p in range(len(work)):
             bit = orders[p][step]
             name = bits - 1 - bit
             axis = sum(1 for h in held[p] if h < name)
@@ -453,9 +519,10 @@
             mine, got = work[p], swap(work[p], bit, devices)
             work[p] = jnp.where(own == 0, jnp.stack([mine, got], axis), jnp.stack([got, mine], axis))
             held[p] = sorted(held[p] + [name])
-        if step == bits - 3:
+        if step == bits - 4:
             work, later = lax.optimization_barrier((work, later))
-    return [w.reshape(devices * value.shape[0], w.shape[-1]) for w in work], later
+    work = [w.reshape(devices // 2, *v.shape) for w, v in zip(work, values)]
+    return [(w, swap(w, 0, devices)) for w in work], later
 
 
 def widen(vector):
@@ -468,7 +535,7 @@
 ):
     blocks, length, width = tokens.shape
     rows = tokens.reshape(blocks * length, width)
-    rows_t = rows.T
+    rows_t = turned(rows)
     own = w_query.shape[0]
     ratio = b_up.shape[0] // own
     vectors = [b_query, b_value, b_out, gain_attn, shift_attn, b_down, gain_ffn, shift_ffn]
@@ -476,12 +543,11 @@
     side = jnp.stack(vectors, axis=1)
     side = jnp.concatenate([side, b_up.reshape(own, ratio)], axis=1)
     side = jnp.pad(side, ((0, 0), (0, PAIR - names - ratio)))
-    head = jnp.concatenate([side, w_query, w_key, w_value], axis=1).astype(BF)
     down_side = w_down.reshape(ratio, own, width).transpose(1, 0, 2).reshape(own, ratio * width)
     later = jnp.concatenate([down_side, w_up, w_out], axis=1).astype(BF)
-    head, (later, rows_t) = gather_pairs(head, devices, (later, rows_t))
-    head = jnp.concatenate(head, axis=1)
-    packed_full = head[:, PAIR:]
+    values = [v.astype(BF) for v in (w_query, w_key, w_value, side)]
+    halves, (later, rows_t) = gather_halves(values, devices, (later, rows_t))
+    head = join(halves.pop(), 1).reshape(devices * own, PAIR)
     query_bias, value_bias, out_bias, attn_gain, attn_shift, down_bias, ffn_gain, ffn_shift = [
         widen(head[:, i]) for i in range(names)
     ]
@@ -496,7 +562,11 @@
         down_rows = down_rows.reshape(-1, ratio, own_rows, width).transpose(0, 2, 1, 3).reshape(width, units)
 
     packed_bias = jnp.concatenate([query_bias, jnp.zeros_like(query_bias), value_bias])
-    packed = (matmul(rows, packed_full) + packed_bias).astype(BF)
+    if own % 32 == 0:
+        packed, packed_full = project(rows, halves, packed_bias)
+    else:
+        packed_full = jnp.concatenate([join(pair, 1).reshape(width, -1) for pair in halves], axis=1)
+        packed = (matmul(rows, packed_full) + packed_bias).astype(BF)
     segments = segment_ids.reshape(-1)
     context, logsums = attend(segments, packed)
     attended = matmul(context, out_full) + out_bias
@@ -560,7 +630,7 @@
     running += side
     tick(running, ())
     pieces = tick(running, [piece[0] for piece in pieces])
-    total_input = input_call(grad_one, head, pieces)
+    total_input = input_call(grad_one, packed_full, pieces)
     layer_input_gradient = total_input.reshape(tokens.shape)
     while not all(c.over for c in running):
         tick(running, ())

time: 595 us -> 595 us (level)
  Pallas kernels: 218 us -> 234 us
  matrix products: 61.2 us -> 51.5 us
  starting transfers between devices: 58.6 us -> 66.5 us
  local copies, waits for them, and re-layouts: 39.3 us -> 32 us
    pallas_call x0 -> x2, Pallas kernels: none -> 16.9 us  [the longest x1 12.6 us: project(): pl.pallas_call(project_kernel, grid=(tokens // TILE,), name='project', in...]
    dot_general x2 -> x1, matrix products: 13.3 us -> 4.68 us  [matmul(): return jnp.dot(left, right, preferred_element_type=F32)]
    ppermute x65 -> x70, starting transfers between devices: 58.6 us -> 66.4 us  [swap(): lax.ppermute(value, AXES, [(i, i ^ 1 << bit) for i in range(devices)])]
    ppermute x65 -> x70, waiting for transfers between devices: 98.4 us -> 94.6 us  [swap(): lax.ppermute(value, AXES, [(i, i ^ 1 << bit) for i in range(devices)])]
  transfers between devices with their start and end apart: 66 -> 71, of which waited for: 20 -> 25; matrix products, arithmetic and copies ran while one was open for 16% -> 15% of each run, Pallas kernels for 30% -> 33%
where the time goes in v5:
time: 595 us; the launch traced here: 584 us
  Pallas kernels  234 us (39%)
  waiting for transfers between devices  116 us (19%)
  other arithmetic  68.5 us (12%)
  starting transfers between devices  66.5 us (11%)
  matrix products  51.5 us (9%)
  local copies, waits for them, and re-layouts  32 us (5%)
  between operations  15.9 us (3%)
    ppermute x70, waiting for transfers between devices, swap(): lax.ppermute(value, AXES, [(i, i ^ 1 << bit) for i in range(devices)])  94.6 us
    pallas_call x4, Pallas kernels, attend_back(): pl.pallas_call(backward_kernel, grid=(count,), name='attend_back', in_spe...  76.9 us
    ppermute x70, starting transfers between devices, swap(): lax.ppermute(value, AXES, [(i, i ^ 1 << bit) for i in range(devices)])  66.4 us
    pallas_call x1, Pallas kernels, attend(): pl.pallas_call(forward_kernel, grid=(pairs,), name='attend', in_specs=seg...  50.6 us
    convert_element_type x36, other arithmetic, halve(): self.send = send.astype(self.kind)  33.7 us
    dot_general x3, matrix products, contract_rows(): lax.dot_general(left, right, (((0,), (0,)), ((), ())), preferred_element_...  25.3 us
    dot_general x2, matrix products, contract_cols(): lax.dot_general(left, right, (((1,), (1,)), ((), ())), preferred_element_...  21.5 us
    pallas_call x4, Pallas kernels, weight_halves(): pl.pallas_call(weight_kernel, grid=(3,), name='weight_halves', in_specs=[...  21.5 us
  transfers between devices with their start and end apart: 71, of which 25 were waited for; matrix products, arithmetic and copies ran while one was open for 15% of the time, Pallas kernels for 33%

profile of v5, /device:TPU:0, one launch (start us, length us, event | category | flops | bytes accessed | tf_op | source)
XLA Modules:
  0.0 584.3 jit_solution(14005365757190244235)
XLA Ops:
  8.2 4.1 collective-permute-start
  31.6 4.2 turned.1.rows_t_ref
  56.2 9.5 %collective-permute-done.11 = bf16[2,2,32,1024]{3,2,1,0:T(8,128)(2,1)S(1)} collective-permute-done((bf16[2,2,32,1024]{3,2,1,0:T(8,128)(2,1)S(1)}, bf16[2,2,32,1024]{3,2,1,0:T(8,128)(2,1)S(1)}, u32[]{:S(2)}, u32[]{:S(2)}) %collective-permute-start.11) | collective-permute-done | bytes 262176 | tf_op jit(solution)/shard_map/ppermute | solution.py:420
  68.8 6.2 %collective-permute-done.12 = bf16[2,2,2,32,1024]{4,3,2,0,1:T(8,128)(2,1)S(1)} collective-permute-done((bf16[2,2,2,32,1024]{4,3,2,0,1:T(8,128)(2,1)S(1)}, bf16[2,2,2,32,1024]{4,3,2,0,1:T(8,128)(2,1)S(1)}, u32[]{:S(2)}, u32[]{:S(2)}) %collective-permute-start.12) | collective-permute-done | bytes 524320 | tf_op jit(solution)/shard_map/ppermute | solution.py:420
  75.4 8.0 %collective-permute-done.15 = bf16[2,2,2,32,1024]{4,3,1,2,0:T(8,128)(2,1)S(1)} collective-permute-done((bf16[2,2,2,32,1024]{4,3,1,2,0:T(8,128)(2,1)S(1)}, bf16[2,2,2,32,1024]{4,3,1,2,0:T(8,128)(2,1)S(1)}, u32[]{:S(2)}, u32[]{:S(2)}) %collective-permute-start.15) | collective-permute-done | bytes 524320 | tf_op jit(solution)/shard_map/ppermute | solution.py:420
  84.4 4.0 collective-permute-done.18
  95.3 12.6 %project.1 = (bf16[1024,3072]{1,0:T(8,128)(2,1)}, bf16[1024,3072]{1,0:T(8,128)(2,1)}) custom-call(s32[1]{0:T(128)} %bitcast.2.own_ref, bf16[1024,1024]{1,0:T(8,128)(2,1)} %bitcast.337, bf16[16,32,1024]{2,1,0:T(8,128)(2,1)} %bitcast.343, bf16[16,32,1024]{2,1,0:T(8,128)(2,1)} %collective-permute-done.10.refs_1_, bf16[16,32,1024]{2,1,0:T(8,128)(2,1)} %bitcast.345, ...), custom_call_target="tpu_custom_call" | custom-call | tf_op jit(solution)/shard_map/project/pallas_call | solution.py:172
  107.9 50.6 %attend.1 = (bf16[1024,1024]{1,0:T(8,128)(2,1)}, f32[8,2,1024]{2,1,0:T(2,128)}) custom-call(s32[1024,1]{1,0:T(8,128)} %copy.145.seg_col, s32[1,1024]{1,0:T(1,128)} %seg_row.9, bf16[1024,3072]{1,0:T(8,128)(2,1)} %get-tuple-element.194.q_ref.k_ref.v_ref, bf16[1024,3072]{1,0:T(8,128)(2,1)} %get-tuple-element.194.q_ref.k_ref.v_ref, ...), custom_call_target="tpu_custom_call" | custom-call | tf_op jit(solution)/shard_map/attend/pallas_call | solution.py:195
  158.5 21.4 %all-gather.2.cloned.1.call-done.w_ref = bf16[1024,9216]{1,0:T(8,128)(2,1)} async-done(((bf16[32,9216]{1,0:T(8,128)(2,1)}), bf16[1024,9216]{1,0:T(8,128)(2,1)}) %all-gather.2.cloned.1.call-update) | async-done | bytes 18874384 | tf_op jit(solution)/shard_map/all_gather | solution.py:555
  179.9 4.7 fusion.71
  190.0 19.6 %feed.1 = (bf16[1024,4096]{1,0:T(8,128)(2,1)}, bf16[1024,4096]{1,0:T(8,128)(2,1)}) custom-call(bf16[1024,1024]{1,0:T(8,128)(2,1)} %get-tuple-element.377.x_ref, bf16[1024,9216]{1,0:T(8,128)(2,1)} %all-gather.2.cloned.1.call-done.w_ref, f32[1,4096]{1,0:T(1,128)} %reshape.1145.b_ref), custom_call_target="tpu_custom_call" | custom-call | tf_op jit(solution)/shard_map/feed/pallas_call | solution.py:279
  209.6 20.0 %settle.1 = (bf16[1024,1024]{1,0:T(8,128)(2,1)}, f32[1024,1024]{1,0:T(8,128)}, bf16[1024,1024]{1,0:T(8,128)(2,1)}, f32[1,1024]{1,0:T(1,128)}, f32[1,1024]{1,0:T(1,128)}, /*index=5*/f32[1,1024]{1,0:T(1,128)}) custom-call(bf16[1024,4096]{1,0:T(8,128)(2,1)} %get-tuple-element.197.hidden_ref, bf16[1024,9216]{1,0:T(8,128)(2,1)} %all-gather.2.cloned.1.call-done.w_ref, ...), custom_call_target="tpu_custom_call" | custom-call | tf_op jit(solution)/shard_map/settle/pallas_call | solution.py:335
  229.6 13.3 %convolution_convert_fusion.1 = bf16[4096,1024]{1,0:T(8,128)(2,1)S(1)} fusion(bf16[1024,4096]{1,0:T(8,128)(2,1)} %get-tuple-element.197.hidden_ref, bf16[1024,1024]{1,0:T(8,128)(2,1)} %get-tuple-element.201.dz_ref), kind=kOutput, calls=%fused_computation.3 | convolution fusion | flops 8594128896 | bytes 18874368 | tf_op jit(solution)/shard_map/dot_general | solution.py:29
  249.9 16.5 %feed_back.1 = (bf16[1024,4096]{1,0:T(8,128)(2,1)}, f32[1,4096]{1,0:T(1,128)}) custom-call(bf16[1024,1024]{1,0:T(8,128)(2,1)} %get-tuple-element.201.dz_ref, bf16[1024,9216]{1,0:T(8,128)(2,1)} %all-gather.2.cloned.1.call-done.w_ref, bf16[1024,4096]{1,0:T(8,128)(2,1)} %get-tuple-element.202.slope_ref), custom_call_target="tpu_custom_call" | custom-call | tf_op jit(solution)/shard_map/feed_back/pallas_call | solution.py:292
  269.9 4.6 fusion.8
  276.5 9.6 %convolution_convert_fusion = bf16[1024,4096]{1,0:T(8,128)(2,1)S(1)} fusion(bf16[1024,1024]{1,0:T(8,128)(2,1)S(1)} %copy-done.3, bf16[1024,4096]{1,0:T(8,128)(2,1)S(1)} %copy-done.42), kind=kOutput, calls=%fused_computation.2 | convolution fusion | flops 8594128896 | bytes 18874368 | tf_op jit(solution)/shard_map/dot_general | solution.py:29
  295.0 5.1 collective-permute-done.22
  304.1 16.2 %multiply_reduce_fusion = (f32[1024]{0:T(1024)}, f32[1024]{0:T(1024)S(1)}, f32[1024]{0:T(1024)S(1)}, f32[1024]{0:T(1024)}, f32[1024,1024]{1,0:T(8,128)S(1)}) fusion(f32[1024,1024]{1,0:T(8,128)S(1)} %copy-done.1, f32[1024]{0:T(1024)S(1)} %add_rsqrt_fusion, f32[1024]{0:T(1024)S(1)} %broadcast_multiply_fusion.2, f32[1024]{0:T(1024)S(1)} %get-tuple-element.371, ...), kind=kOutput, calls=%fused_computation.4 | convolution fusion | flops 8600416256 | bytes 29388800 | tf_op jit(solution)/shard_map/dot_general | solution.py:33
  328.5 5.3 convolution_convert_fusion.3.do_ref
  343.1 19.2 %attend_back.4 = (bf16[3,1024,256]{2,1,0:T(8,128)(2,1)}, f32[1,256]{1,0:T(1,128)}, f32[1,256]{1,0:T(1,128)}) custom-call(s32[1024,1]{1,0:T(8,128)} %copy.145.seg_col, s32[1,1024]{1,0:T(1,128)} %seg_row.9, bf16[1024,3072]{1,0:T(8,128)(2,1)} %get-tuple-element.194.q_ref.k_ref.v_ref, bf16[1024,3072]{1,0:T(8,128)(2,1)} %get-tuple-element.194.q_ref.k_ref.v_ref, ...), custom_call_target="tpu_custom_call" | custom-call | tf_op jit(solution)/shard_map/attend_back/pallas_call | solution.py:217
  362.3 5.4 weight_halves.4
  367.7 7.7 %collective-permute-done.28 = bf16[2,128,512]{2,1,0:T(8,128)(2,1)} collective-permute-done((bf16[2,128,512]{2,1,0:T(8,128)(2,1)S(1)}, bf16[2,128,512]{2,1,0:T(8,128)(2,1)}, u32[]{:S(2)}, u32[]{:S(2)}) %collective-permute-start.28) | collective-permute-done | bytes 262176 | tf_op jit(solution)/shard_map/ppermute | solution.py:420
  386.1 19.4 %attend_back.5 = (bf16[3,1024,256]{2,1,0:T(8,128)(2,1)}, f32[1,256]{1,0:T(1,128)}, f32[1,256]{1,0:T(1,128)}) custom-call(s32[1024,1]{1,0:T(8,128)} %copy.145.seg_col, s32[1,1024]{1,0:T(1,128)} %seg_row.9, bf16[1024,3072]{1,0:T(8,128)(2,1)} %get-tuple-element.194.q_ref.k_ref.v_ref, bf16[1024,3072]{1,0:T(8,128)(2,1)} %get-tuple-element.194.q_ref.k_ref.v_ref, ...), custom_call_target="tpu_custom_call" | custom-call | tf_op jit(solution)/shard_map/attend_back/pallas_call | solution.py:217
  407.7 5.4 weight_halves.5
  414.3 15.9 %collective-permute-done.35 = bf16[2,2,32,2048]{3,2,0,1:T(8,128)(2,1)} collective-permute-done((bf16[2,2,32,2048]{3,2,0,1:T(8,128)(2,1)S(1)}, bf16[2,2,32,2048]{3,2,0,1:T(8,128)(2,1)}, u32[]{:S(2)}, u32[]{:S(2)}) %collective-permute-start.35) | collective-permute-done | bytes 524320 | tf_op jit(solution)/shard_map/ppermute | solution.py:420
  435.2 19.1 %attend_back.6 = (bf16[3,1024,256]{2,1,0:T(8,128)(2,1)}, f32[1,256]{1,0:T(1,128)}, f32[1,256]{1,0:T(1,128)}) custom-call(s32[1024,1]{1,0:T(8,128)} %copy.145.seg_col, s32[1,1024]{1,0:T(1,128)} %seg_row.9, bf16[1024,3072]{1,0:T(8,128)(2,1)} %get-tuple-element.194.q_ref.k_ref.v_ref, bf16[1024,3072]{1,0:T(8,128)(2,1)} %get-tuple-element.194.q_ref.k_ref.v_ref, ...), custom_call_target="tpu_custom_call" | custom-call | tf_op jit(solution)/shard_map/attend_back/pallas_call | solution.py:217
  457.0 5.4 weight_halves.6
  475.8 19.1 %attend_back.7 = (bf16[3,1024,256]{2,1,0:T(8,128)(2,1)}, f32[1,256]{1,0:T(1,128)}, f32[1,256]{1,0:T(1,128)}) custom-call(s32[1024,1]{1,0:T(8,128)} %copy.145.seg_col, s32[1,1024]{1,0:T(1,128)} %seg_row.9, bf16[1024,3072]{1,0:T(8,128)(2,1)} %get-tuple-element.194.q_ref.k_ref.v_ref, bf16[1024,3072]{1,0:T(8,128)(2,1)} %get-tuple-element.194.q_ref.k_ref.v_ref, ...), custom_call_target="tpu_custom_call" | custom-call | tf_op jit(solution)/shard_map/attend_back/pallas_call | solution.py:217
  499.7 5.4 weight_halves.7
  520.7 4.2 collective-permute-done.52
  525.0 7.7 %collective-permute-done.53 = bf16[2,2,2,32,768]{4,3,1,2,0:T(8,128)(2,1)S(1)} collective-permute-done((bf16[2,2,2,32,768]{4,3,1,2,0:T(8,128)(2,1)S(1)}, bf16[2,2,2,32,768]{4,3,1,2,0:T(8,128)(2,1)S(1)}, u32[]{:S(2)}, u32[]{:S(2)}) %collective-permute-start.53) | collective-permute-done | bytes 393248 | tf_op jit(solution)/shard_map/ppermute | solution.py:420
  540.5 12.1 %input_grad.1 = bf16[1024,1024]{1,0:T(8,128)(2,1)} custom-call(f32[1024,1024]{1,0:T(8,128)} %copy-done.2, bf16[1024,3072]{1,0:T(8,128)(2,1)} %get-tuple-element.214.refs_1_, bf16[3,1024,256]{2,1,0:T(8,128)(2,1)} %get-tuple-element.321.part_ref.refs_2_, bf16[3,1024,256]{2,1,0:T(8,128)(2,1)} %get-tuple-element.322.part_ref.refs_3_, ...), custom_call_target="tpu_custom_call" | custom-call | tf_op jit(solution)/shard_map/input_grad/pallas_call | solution.py:407
  (409 shorter events, 186.8 us)
Async XLA Ops:
  7.2 172.7 %all-gather.2.cloned.1.call-start = ((), (), s32[]{:S(2)}) async-start(), calls=%async_computation | async-start | bytes 19464192 | tf_op jit(solution)/shard_map/all_gather | solution.py:555
  8.2 31.4 %collective-permute-start = (bf16[32,1024]{1,0:T(8,128)(2,1)S(1)}, bf16[32,1024]{1,0:T(8,128)(2,1)S(1)}, u32[]{:S(2)}, u32[]{:S(2)}) collective-permute-start(bf16[32,1024]{1,0:T(8,128)(2,1)S(1)} %convert_element_type.735), channel_id=1, source_target_pairs={{0,16},{1,17},{2,18},{3,19},{4,20},{5,21},{6,22},{7,23},{8,24},{9,... | collective-permute-start | bytes 196616 | tf_op jit(solution)/shard_map/ppermute | solution.py:420
  13.3 28.0 %collective-permute-start.2 = (bf16[32,1024]{1,0:T(8,128)(2,1)S(1)}, bf16[32,1024]{1,0:T(8,128)(2,1)S(1)}, u32[]{:S(2)}, u32[]{:S(2)}) collective-permute-start(bf16[32,1024]{1,0:T(8,128)(2,1)S(1)} %convert_element_type.736), channel_id=1, source_target_pairs={{0,2},{1,3},{2,0},{3,1},{4,6},{5,7},{6,4},{7,5},{8,10},{9,11},{10,... | collective-permute-start | bytes 196616 | tf_op jit(solution)/shard_map/ppermute | solution.py:420
  15.8 28.2 %collective-permute-start.4 = (bf16[32,1024]{1,0:T(8,128)(2,1)S(1)}, bf16[32,1024]{1,0:T(8,128)(2,1)S(1)}, u32[]{:S(2)}, u32[]{:S(2)}) collective-permute-start(bf16[32,1024]{1,0:T(8,128)(2,1)S(1)} %convert_element_type.737), channel_id=1, source_target_pairs={{0,4},{1,5},{2,6},{3,7},{4,0},{5,1},{6,2},{7,3},{8,12},{9,13},{10,... | collective-permute-start | bytes 196616 | tf_op jit(solution)/shard_map/ppermute | solution.py:420
  49.7 16.1 %collective-permute-start.11 = (bf16[2,2,32,1024]{3,2,1,0:T(8,128)(2,1)S(1)}, bf16[2,2,32,1024]{3,2,1,0:T(8,128)(2,1)S(1)}, u32[]{:S(2)}, u32[]{:S(2)}) collective-permute-start(bf16[2,2,32,1024]{3,2,1,0:T(8,128)(2,1)S(1)} %maximum_select_fusion.10), channel_id=1, source_target_pairs={{0,8},{1,9},{2,10},{3,11},{4,12},{5,13},{6,14},{7,15},{8,0},{9,1},... | collective-permute-start | bytes 786440 | tf_op jit(solution)/shard_map/ppermute | solution.py:420
  50.1 15.8 %collective-permute-start.14 = (bf16[2,2,32,1024]{3,2,0,1:T(8,128)(2,1)S(1)}, bf16[2,2,32,1024]{3,2,0,1:T(8,128)(2,1)S(1)}, u32[]{:S(2)}, u32[]{:S(2)}) collective-permute-start(bf16[2,2,32,1024]{3,2,0,1:T(8,128)(2,1)S(1)} %maximum_select_fusion.11), channel_id=1, source_target_pairs={{0,16},{1,17},{2,18},{3,19},{4,20},{5,21},{6,22},{7,23},{8,24},{9,... | collective-permute-start | bytes 786440 | tf_op jit(solution)/shard_map/ppermute | solution.py:420
  52.4 31.4 %collective-permute-start.17 = (bf16[2,2,32,128]{3,2,0,1:T(8,128)(2,1)S(1)}, bf16[2,2,32,128]{3,2,0,1:T(8,128)(2,1)S(1)}, u32[]{:S(2)}, u32[]{:S(2)}) collective-permute-start(bf16[2,2,32,128]{3,2,0,1:T(8,128)(2,1)S(1)} %maximum_select_fusion.22), channel_id=1, source_target_pairs={{0,4},{1,5},{2,6},{3,7},{4,0},{5,1},{6,2},{7,3},{8,12},{9,13},{10,... | collective-permute-start | bytes 98312 | tf_op jit(solution)/shard_map/ppermute | solution.py:420
  66.0 17.4 %collective-permute-start.15 = (bf16[2,2,2,32,1024]{4,3,1,2,0:T(8,128)(2,1)S(1)}, bf16[2,2,2,32,1024]{4,3,1,2,0:T(8,128)(2,1)S(1)}, u32[]{:S(2)}, u32[]{:S(2)}) collective-permute-start(bf16[2,2,2,32,1024]{4,3,1,2,0:T(8,128)(2,1)S(1)} %maximum_select_fusion.8), channel_id=1, source_target_pairs={{0,8},{1,9},{2,10},{3,11},{4,12},{5,13},{6,14},{7,15},{8,0},{9,1},... | collective-permute-start | bytes 1572872 | tf_op jit(solution)/shard_map/ppermute | solution.py:420
  68.7 26.5 %collective-permute-start.10 = (bf16[16,32,1024]{2,1,0:T(8,128)(2,1)S(1)}, bf16[16,32,1024]{2,1,0:T(8,128)(2,1)}, u32[]{:S(2)}, u32[]{:S(2)}) collective-permute-start(bf16[16,32,1024]{2,1,0:T(8,128)(2,1)S(1)} %bitcast.342), channel_id=1, source_target_pairs={{0,1},{1,0},{2,3},{3,2},{4,5},{5,4},{6,7},{7,6},{8,9},{9,8},{10,11... | collective-permute-start | bytes 3145736 | tf_op jit(solution)/shard_map/ppermute | solution.py:420
  75.4 19.9 %collective-permute-start.13 = (bf16[16,32,1024]{2,1,0:T(8,128)(2,1)S(1)}, bf16[16,32,1024]{2,1,0:T(8,128)(2,1)}, u32[]{:S(2)}, u32[]{:S(2)}) collective-permute-start(bf16[16,32,1024]{2,1,0:T(8,128)(2,1)S(1)} %bitcast.344), channel_id=1, source_target_pairs={{0,1},{1,0},{2,3},{3,2},{4,5},{5,4},{6,7},{7,6},{8,9},{9,8},{10,11... | collective-permute-start | bytes 3145736 | tf_op jit(solution)/shard_map/ppermute | solution.py:420
  249.4 17.1 %collective-permute-start.20 = (bf16[2,2,2,2,128,512]{5,4,0,1,2,3:T(8,128)(2,1)S(1)}, bf16[2,2,2,2,128,512]{5,4,0,1,2,3:T(8,128)(2,1)}, u32[]{:S(2)}, u32[]{:S(2)}) collective-permute-start(bf16[2,2,2,2,128,512]{5,4,0,1,2,3:T(8,128)(2,1)S(1)} %bitcast.360), channel_id=1, source_target_pairs={{0,1},{1,0},{2,3},{3,2},{4,5},{5,4},{6,7},{7,6},{8,9},{9,8},{10,11... | collective-permute-start | bytes 6291464 | tf_op jit(solution)/shard_map/ppermute | solution.py:420
  249.7 20.2 %collective-permute-start.21 = (bf16[2,2,2,2,128,512]{5,4,3,0,1,2:T(8,128)(2,1)}, bf16[2,2,2,2,128,512]{5,4,3,0,1,2:T(8,128)(2,1)}, u32[]{:S(2)}, u32[]{:S(2)}) collective-permute-start(bf16[2,2,2,2,128,512]{5,4,3,0,1,2:T(8,128)(2,1)} %bitcast.323), channel_id=1, source_target_pairs={{0,1},{1,0},{2,3},{3,2},{4,5},{5,4},{6,7},{7,6},{8,9},{9,8},{10,11... | collective-permute-start | bytes 6291464 | tf_op jit(solution)/shard_map/ppermute | solution.py:420
  274.4 25.6 %collective-permute-start.22 = (bf16[2,2,2,128,512]{4,3,0,1,2:T(8,128)(2,1)}, bf16[2,2,2,128,512]{4,3,0,1,2:T(8,128)(2,1)}, u32[]{:S(2)}, u32[]{:S(2)}) collective-permute-start(bf16[2,2,2,128,512]{4,3,0,1,2:T(8,128)(2,1)} %get-tuple-element.210), channel_id=1, source_target_pairs={{0,2},{1,3},{2,0},{3,1},{4,6},{5,7},{6,4},{7,5},{8,10},{9,11},{10,... | collective-permute-start | bytes 3145736 | tf_op jit(solution)/shard_map/ppermute | solution.py:420
  275.9 25.7 %collective-permute-start.23 = (bf16[2,2,2,128,512]{4,3,2,0,1:T(8,128)(2,1)}, bf16[2,2,2,128,512]{4,3,2,0,1:T(8,128)(2,1)}, u32[]{:S(2)}, u32[]{:S(2)}) collective-permute-start(bf16[2,2,2,128,512]{4,3,2,0,1:T(8,128)(2,1)} %get-tuple-element.212), channel_id=1, source_target_pairs={{0,4},{1,5},{2,6},{3,7},{4,0},{5,1},{6,2},{7,3},{8,12},{9,13},{10,... | collective-permute-start | bytes 3145736 | tf_op jit(solution)/shard_map/ppermute | solution.py:420
  338.8 38.4 %collective-permute-start.30 = (bf16[2,2,2,32,2048]{4,3,1,2,0:T(8,128)(2,1)}, bf16[2,2,2,32,2048]{4,3,1,2,0:T(8,128)(2,1)}, u32[]{:S(2)}, u32[]{:S(2)}) collective-permute-start(bf16[2,2,2,32,2048]{4,3,1,2,0:T(8,128)(2,1)} %get-tuple-element.235), channel_id=1, source_target_pairs={{0,8},{1,9},{2,10},{3,11},{4,12},{5,13},{6,14},{7,15},{8,0},{9,1},... | collective-permute-start | bytes 3145736 | tf_op jit(solution)/shard_map/ppermute | solution.py:420
  340.4 39.1 %collective-permute-start.31 = (bf16[2,2,2,32,2048]{4,3,0,1,2:T(8,128)(2,1)}, bf16[2,2,2,32,2048]{4,3,0,1,2:T(8,128)(2,1)S(1)}, u32[]{:S(2)}, u32[]{:S(2)}) collective-permute-start(bf16[2,2,2,32,2048]{4,3,0,1,2:T(8,128)(2,1)} %get-tuple-element.237), channel_id=1, source_target_pairs={{0,2},{1,3},{2,0},{3,1},{4,6},{5,7},{6,4},{7,5},{8,10},{9,11},{10,... | collective-permute-start | bytes 3145736 | tf_op jit(solution)/shard_map/ppermute | solution.py:420
  340.9 39.6 %collective-permute-start.32 = (bf16[2,2,2,2,32,1024]{5,4,2,3,0,1:T(8,128)(2,1)}, bf16[2,2,2,2,32,1024]{5,4,2,3,0,1:T(8,128)(2,1)}, u32[]{:S(2)}, u32[]{:S(2)}) collective-permute-start(bf16[2,2,2,2,32,1024]{5,4,2,3,0,1:T(8,128)(2,1)} %bitcast.327), channel_id=1, source_target_pairs={{0,1},{1,0},{2,3},{3,2},{4,5},{5,4},{6,7},{7,6},{8,9},{9,8},{10,11... | collective-permute-start | bytes 3145736 | tf_op jit(solution)/shard_map/ppermute | solution.py:420
  340.9 34.5 %collective-permute-start.28 = (bf16[2,128,512]{2,1,0:T(8,128)(2,1)S(1)}, bf16[2,128,512]{2,1,0:T(8,128)(2,1)}, u32[]{:S(2)}, u32[]{:S(2)}) collective-permute-start(bf16[2,128,512]{2,1,0:T(8,128)(2,1)S(1)} %get-tuple-element.231), channel_id=1, source_target_pairs={{0,8},{1,9},{2,10},{3,11},{4,12},{5,13},{6,14},{7,15},{8,0},{9,1},... | collective-permute-start | bytes 786440 | tf_op jit(solution)/shard_map/ppermute | solution.py:420
  341.4 35.7 %collective-permute-start.29 = (bf16[2,128,512]{2,1,0:T(8,128)(2,1)S(1)}, bf16[2,128,512]{2,1,0:T(8,128)(2,1)S(1)}, u32[]{:S(2)}, u32[]{:S(2)}) collective-permute-start(bf16[2,128,512]{2,1,0:T(8,128)(2,1)S(1)} %get-tuple-element.233), channel_id=1, source_target_pairs={{0,16},{1,17},{2,18},{3,19},{4,20},{5,21},{6,22},{7,23},{8,24},{9,... | collective-permute-start | bytes 786440 | tf_op jit(solution)/shard_map/ppermute | solution.py:420
  383.0 30.1 %collective-permute-start.33 = (bf16[128,512]{1,0:T(8,128)(2,1)}, bf16[128,512]{1,0:T(8,128)(2,1)S(1)}, u32[]{:S(2)}, u32[]{:S(2)}) collective-permute-start(bf16[128,512]{1,0:T(8,128)(2,1)} %get-tuple-element.250), channel_id=1, source_target_pairs={{0,16},{1,17},{2,18},{3,19},{4,20},{5,21},{6,22},{7,23},{8,24},{9,... | collective-permute-start | bytes 393224 | tf_op jit(solution)/shard_map/ppermute | solution.py:420
  383.7 29.4 %collective-permute-start.37 = (bf16[2,2,2,32,1024]{4,3,1,2,0:T(8,128)(2,1)}, bf16[2,2,2,32,1024]{4,3,1,2,0:T(8,128)(2,1)}, u32[]{:S(2)}, u32[]{:S(2)}) collective-permute-start(bf16[2,2,2,32,1024]{4,3,1,2,0:T(8,128)(2,1)} %get-tuple-element.258), channel_id=1, source_target_pairs={{0,8},{1,9},{2,10},{3,11},{4,12},{5,13},{6,14},{7,15},{8,0},{9,1},... | collective-permute-start | bytes 1572872 | tf_op jit(solution)/shard_map/ppermute | solution.py:420
  406.1 24.1 %collective-permute-start.35 = (bf16[2,2,32,2048]{3,2,0,1:T(8,128)(2,1)S(1)}, bf16[2,2,32,2048]{3,2,0,1:T(8,128)(2,1)}, u32[]{:S(2)}, u32[]{:S(2)}) collective-permute-start(bf16[2,2,32,2048]{3,2,0,1:T(8,128)(2,1)S(1)} %copy-done.23), channel_id=1, source_target_pairs={{0,16},{1,17},{2,18},{3,19},{4,20},{5,21},{6,22},{7,23},{8,24},{9,... | collective-permute-start | bytes 1572872 | tf_op jit(solution)/shard_map/ppermute | solution.py:420
  406.2 25.9 %collective-permute-start.36 = (bf16[2,2,32,2048]{3,2,0,1:T(8,128)(2,1)S(1)}, bf16[2,2,32,2048]{3,2,0,1:T(8,128)(2,1)}, u32[]{:S(2)}, u32[]{:S(2)}) collective-permute-start(bf16[2,2,32,2048]{3,2,0,1:T(8,128)(2,1)S(1)} %copy-done.24), channel_id=1, source_target_pairs={{0,4},{1,5},{2,6},{3,7},{4,0},{5,1},{6,2},{7,3},{8,12},{9,13},{10,... | collective-permute-start | bytes 1572872 | tf_op jit(solution)/shard_map/ppermute | solution.py:420
  413.0 20.2 %collective-permute-start.38 = (bf16[2,2,2,2,32,768]{5,4,0,1,2,3:T(8,128)(2,1)S(1)}, bf16[2,2,2,2,32,768]{5,4,0,1,2,3:T(8,128)(2,1)S(1)}, u32[]{:S(2)}, u32[]{:S(2)}) collective-permute-start(bf16[2,2,2,2,32,768]{5,4,0,1,2,3:T(8,128)(2,1)S(1)} %copy.160), channel_id=1, source_target_pairs={{0,1},{1,0},{2,3},{3,2},{4,5},{5,4},{6,7},{7,6},{8,9},{9,8},{10,11... | collective-permute-start | bytes 2359304 | tf_op jit(solution)/shard_map/ppermute | solution.py:420
  433.5 28.9 %collective-permute-start.39 = (bf16[2,32,2048]{2,1,0:T(8,128)(2,1)}, bf16[2,32,2048]{2,1,0:T(8,128)(2,1)S(1)}, u32[]{:S(2)}, u32[]{:S(2)}) collective-permute-start(bf16[2,32,2048]{2,1,0:T(8,128)(2,1)} %get-tuple-element.270), channel_id=1, source_target_pairs={{0,2},{1,3},{2,0},{3,1},{4,6},{5,7},{6,4},{7,5},{8,10},{9,11},{10,... | collective-permute-start | bytes 786440 | tf_op jit(solution)/shard_map/ppermute | solution.py:420
  435.1 32.3 %collective-permute-start.43 = (bf16[2,2,2,2,32,768]{5,4,3,0,1,2:T(8,128)(2,1)S(1)}, bf16[2,2,2,2,32,768]{5,4,3,0,1,2:T(8,128)(2,1)S(1)}, u32[]{:S(2)}, u32[]{:S(2)}) collective-permute-start(bf16[2,2,2,2,32,768]{5,4,3,0,1,2:T(8,128)(2,1)S(1)} %copy.164), channel_id=1, source_target_pairs={{0,1},{1,0},{2,3},{3,2},{4,5},{5,4},{6,7},{7,6},{8,9},{9,8},{10,11... | collective-permute-start | bytes 2359304 | tf_op jit(solution)/shard_map/ppermute | solution.py:420
  435.2 27.9 %collective-permute-start.41 = (bf16[2,2,32,1024]{3,2,0,1:T(8,128)(2,1)S(1)}, bf16[2,2,32,1024]{3,2,0,1:T(8,128)(2,1)S(1)}, u32[]{:S(2)}, u32[]{:S(2)}) collective-permute-start(bf16[2,2,32,1024]{3,2,0,1:T(8,128)(2,1)S(1)} %get-tuple-element.274), channel_id=1, source_target_pairs={{0,16},{1,17},{2,18},{3,19},{4,20},{5,21},{6,22},{7,23},{8,24},{9,... | collective-permute-start | bytes 786440 | tf_op jit(solution)/shard_map/ppermute | solution.py:420
  468.4 39.3 %collective-permute-start.44 = (bf16[32,2048]{1,0:T(8,128)(2,1)}, bf16[32,2048]{1,0:T(8,128)(2,1)}, u32[]{:S(2)}, u32[]{:S(2)}) collective-permute-start(bf16[32,2048]{1,0:T(8,128)(2,1)} %get-tuple-element.284), channel_id=1, source_target_pairs={{0,4},{1,5},{2,6},{3,7},{4,0},{5,1},{6,2},{7,3},{8,12},{9,13},{10,... | collective-permute-start | bytes 393224 | tf_op jit(solution)/shard_map/ppermute | solution.py:420
  513.1 19.6 %collective-permute-start.54 = (bf16[2,2,2,2,32,768]{5,4,0,1,2,3:T(8,128)(2,1)S(1)}, bf16[2,2,2,2,32,768]{5,4,0,1,2,3:T(8,128)(2,1)S(1)}, u32[]{:S(2)}, u32[]{:S(2)}) collective-permute-start(bf16[2,2,2,2,32,768]{5,4,0,1,2,3:T(8,128)(2,1)S(1)} %copy.180), channel_id=1, source_target_pairs={{0,1},{1,0},{2,3},{3,2},{4,5},{5,4},{6,7},{7,6},{8,9},{9,8},{10,11... | collective-permute-start | bytes 2359304 | tf_op jit(solution)/shard_map/ppermute | solution.py:420
  532.9 19.6 %collective-permute-start.60 = (f32[2,2,2,1,384]{4,1,0,3,2:T(2,128)S(1)}, f32[2,2,2,1,384]{4,1,0,3,2:T(2,128)S(1)}, u32[]{:S(2)}, u32[]{:S(2)}) collective-permute-start(f32[2,2,2,1,384]{4,1,0,3,2:T(2,128)S(1)} %copy.183), channel_id=1, source_target_pairs={{0,2},{1,3},{2,0},{3,1},{4,6},{5,7},{6,4},{7,5},{8,10},{9,11},{10,... | collective-permute-start | bytes 36872 | tf_op jit(solution)/shard_map/ppermute | solution.py:420
  535.3 17.3 %collective-permute-start.56 = (bf16[32,768]{1,0:T(8,128)(2,1)S(1)}, bf16[32,768]{1,0:T(8,128)(2,1)S(1)}, u32[]{:S(2)}, u32[]{:S(2)}) collective-permute-start(bf16[32,768]{1,0:T(8,128)(2,1)S(1)} %get-tuple-element.326), channel_id=1, source_target_pairs={{0,16},{1,17},{2,18},{3,19},{4,20},{5,21},{6,22},{7,23},{8,24},{9,... | collective-permute-start | bytes 147464 | tf_op jit(solution)/shard_map/ppermute | solution.py:420
  537.0 15.6 %collective-permute-start.57 = (bf16[2,32,768]{2,1,0:T(8,128)(2,1)S(1)}, bf16[2,32,768]{2,1,0:T(8,128)(2,1)S(1)}, u32[]{:S(2)}, u32[]{:S(2)}) collective-permute-start(bf16[2,32,768]{2,1,0:T(8,128)(2,1)S(1)} %get-tuple-element.328), channel_id=1, source_target_pairs={{0,16},{1,17},{2,18},{3,19},{4,20},{5,21},{6,22},{7,23},{8,24},{9,... | collective-permute-start | bytes 294920 | tf_op jit(solution)/shard_map/ppermute | solution.py:420
  (83 other events, 805.5 us)
Sparse Core Ops, SparseCore 0:
  49.2 130.6 all-gather.1
